TPU v7x, 32 devices: a whole 2x2x4 slice. The times are simulated.
32 devices in a mesh: dp: 8 (over z, y), fsdp: 4 (over x, core).
Axes of the slice: x: 2, y: 2, z: 4, core: 2. Of those that a mesh axis runs over, the one named last changes fastest.
Arguments:
- tokens: bfloat16 [8192, 768], P(('dp', 'fsdp')), may hold values from -6 to 6
- starts: int32 [32], P(('dp', 'fsdp')), may hold values from 0 to 1, as said below
- valid: int32 [8192], P(('dp', 'fsdp')), may hold values from 0 to 1, as said below
- norm_gain: bfloat16 [2, 768], P(None, ('dp', 'fsdp')), may hold values from 0.5 to 1.5
- w_gate: bfloat16 [2, 768, 1536], P(None, ('dp', 'fsdp')), may hold values from -0.21875 to 0.21875
- w_xbc: bfloat16 [2, 768, 1792], P(None, ('dp', 'fsdp')), may hold values from -0.21875 to 0.21875
- w_dt: bfloat16 [2, 768, 24], P(None, ('dp', 'fsdp')), may hold values from -0.21875 to 0.21875
- conv_weight: bfloat16 [2, 4, 1792], P(None, None, ('dp', 'fsdp')), may hold values from -3 to 3
- conv_bias: bfloat16 [2, 1792], P(None, ('dp', 'fsdp')), may hold values from -0.5 to 0.5
- dt_bias: float32 [2, 24], replicated, may hold values from -9 to -2
- a_log: float32 [2, 24], replicated, may hold values from -2 to 2
- skip_weight: float32 [2, 24], replicated, may hold values from 0.5 to 1.5
- gate_gain: bfloat16 [2, 1536], P(None, ('dp', 'fsdp')), may hold values from 0.5 to 1.5
- w_out: bfloat16 [2, 1536, 768], P(None, ('dp', 'fsdp')), may hold values from -0.15625 to 0.15625
- cotangent: bfloat16 [8192, 768], P(('dp', 'fsdp')), may hold values from -6 to 6
Outputs:
- activations: float32 [8192, 768], P(('dp', 'fsdp'))
- input_grad: float32 [8192, 768], P(('dp', 'fsdp'))
- grad_norm_gain: float32 [2, 768], P(None, ('dp', 'fsdp'))
- grad_w_gate: float32 [2, 768, 1536], P(None, ('dp', 'fsdp'))
- grad_w_xbc: float32 [2, 768, 1792], P(None, ('dp', 'fsdp'))
- grad_w_dt: float32 [2, 768, 24], P(None, ('dp', 'fsdp'))
- grad_conv_weight: float32 [2, 4, 1792], P(None, None, ('dp', 'fsdp'))
- grad_conv_bias: float32 [2, 1792], P(None, ('dp', 'fsdp'))
- grad_dt_bias: float32 [2, 24], replicated
- grad_a_log: float32 [2, 24], replicated
- grad_skip_weight: float32 [2, 24], replicated
- grad_gate_gain: float32 [2, 1536], P(None, ('dp', 'fsdp'))
- grad_w_out: float32 [2, 1536, 768], P(None, ('dp', 'fsdp'))
Inputs may be any that keep to these rules, and one draw needn't show every extreme that they name: starts is 1 where a span of 256 tokens begins a packed sequence; within every 1024 tokens of one dp index the first span is 1 and the second is 0. valid is 0 only on fewer than 128 padding tokens at the end of a sequence's last span.
All inputs are finite; a program needn't handle non-finite values.
Results may differ from a plain program's by a relative error of at most 0.02.
Values may be sent and summed in bfloat16 or wider, within the bound.
No kernel may reach another device: no remote copies, remote signals or barrier semaphores. Data moves between devices by JAX's collectives and lax.ppermute only.
A program may use at most 256 MiB of HBM per device.

v0:
```python
from functools import partial

import jax
import jax.numpy as jnp
from jax import lax
from jax.sharding import PartitionSpec as P

INNER = 1536
HEADS = 24
HEAD_DIM = 64
STATE = 128
KCONV = 4
SPAN = 256


epsilon = 1e-05


def shifted(block, axis, distance):
    devices = range(lax.axis_size(axis))
    route = [(i - distance, i) for i in devices if i - distance in devices]
    return lax.ppermute(block, axis, route)


def prefix_2(shard, axis, join, neutral):
    place = lax.axis_index(axis)
    gathered = jax.tree.map(
        lambda a, kind: lax.all_gather(a.astype(kind), axis), shard, (jnp.bfloat16, jnp.bfloat16)
    )
    state = jax.tree.map(lambda a, e: jnp.zeros_like(a) + jnp.asarray(e, a.dtype), shard, neutral)

    def prefix_one(step, state):
        return join(
            state,
            jax.tree.map(
                lambda a, own: lax.dynamic_index_in_dim(a, step, 0, False).astype(own.dtype),
                gathered,
                shard,
            ),
        )

    return lax.fori_loop(0, place, prefix_one, state)


def entering_2(shard, axis, join, neutral):
    count = lax.axis_size(axis)
    place = lax.axis_index(axis)
    ahead = count - 1 - place
    gathered = jax.tree.map(
        lambda a, kind: lax.all_gather(a.astype(kind), axis),
        shard,
        jax.tree.map(lambda a: jnp.bfloat16 if a.dtype == jnp.float32 else a.dtype, shard),
    )
    state = jax.tree.map(lambda a, e: jnp.zeros_like(a) + jnp.asarray(e, a.dtype), shard, neutral)

    def entering_one(step, state):
        source = count - 1 - step
        return join(
            state,
            jax.tree.map(
                lambda a, own: lax.dynamic_index_in_dim(a, source, 0, False).astype(own.dtype),
                gathered,
                shard,
            ),
        )

    return lax.fori_loop(0, ahead, entering_one, state)


def rms_scale(hidden, gain):
    return hidden * lax.rsqrt(jnp.mean(hidden * hidden, axis=-1, keepdims=True) + epsilon) * gain


def gated_norm(mixed, gate, gain):
    return rms_scale(mixed * jax.nn.silu(gate), gain)


def tap_masks(starts, count):
    offset = jnp.arange(count) % SPAN
    begins = jnp.repeat(starts, SPAN) > 0
    rows = []
    for shift in range(1, KCONV):
        rows.append(jnp.where(jnp.logical_and(begins, offset < shift), 0.0, 1.0))
    return jnp.stack(rows).astype(jnp.float32)


def conv_act(extended, weight, bias, masks):
    count = masks.shape[1]
    total = bias[None, :] + weight[KCONV - 1][None, :] * extended[KCONV - 1 :]
    for shift in range(1, KCONV):
        window = lax.slice_in_dim(extended, KCONV - 1 - shift, KCONV - 1 - shift + count, axis=0)
        total = total + weight[KCONV - 1 - shift][None, :] * window * masks[shift - 1][:, None]
    return jax.nn.silu(total)


def combine(earlier, later):
    return (earlier[0] * later[0], later[0][:, None, None] * earlier[1] + later[1])


def forward_chain(arriving, growth, keep, fresh):
    carry = arriving
    entering = keep[0] * carry
    states = [entering]
    carry = growth[0][:, None, None] * entering + fresh[0]
    return (jnp.stack(states), carry)


def back_chain(arriving, entering, growth, keep, local_grad):
    spans = entering.shape[0]
    pending = arriving
    fresh_grads = [None] * spans
    grow_grads = [None] * spans
    for index in reversed(range(spans)):
        fresh_grads[index] = pending
        grow_grads[index] = jnp.sum(pending * entering[index], axis=(1, 2))
        pending = keep[index] * (local_grad[index] + growth[index][:, None, None] * pending)
    return (pending, jnp.stack(fresh_grads), jnp.stack(grow_grads))


def layer_forward(hidden, weights, heads, starts, valid):
    norm_gain, w_gate, w_xbc, w_dt, conv_weight, conv_bias, gate_gain, w_out = weights
    dt_bias, a_log, skip_weight = heads
    count = hidden.shape[0]
    spans = count // SPAN
    norm_scale = norm_gain.astype(jnp.float32)
    normed = rms_scale(hidden, norm_scale).astype(jnp.bfloat16)
    gate = jnp.dot(normed, w_gate, preferred_element_type=jnp.float32)
    conv_in = jnp.dot(normed, w_xbc, preferred_element_type=jnp.float32).astype(jnp.bfloat16)
    dt_raw = jnp.dot(normed, w_dt, preferred_element_type=jnp.float32)
    rim = shifted(conv_in[count - (KCONV - 1) :], "fsdp", 1)
    extended = jnp.concatenate([rim, conv_in], axis=0).astype(jnp.float32)
    masks = tap_masks(starts, count)
    conv_kernel = conv_weight.astype(jnp.float32)
    conv_offset = conv_bias.astype(jnp.float32)
    activated = conv_act(extended, conv_kernel, conv_offset, masks)
    input_heads = activated[:, :INNER].reshape(spans, SPAN, HEADS, HEAD_DIM)
    rounded_in = input_heads.astype(jnp.bfloat16)
    keys = activated[:, INNER : INNER + STATE].astype(jnp.bfloat16).reshape(spans, SPAN, STATE)
    queries = activated[:, INNER + STATE :].astype(jnp.bfloat16).reshape(spans, SPAN, STATE)
    valid_rows = valid.astype(jnp.float32)
    step_size = jax.nn.softplus(dt_raw + dt_bias) * valid_rows[:, None]
    decay = -jnp.exp(a_log) * step_size
    step_spans = step_size.reshape(spans, SPAN, HEADS)
    cumulative = jnp.cumsum(decay.reshape(spans, SPAN, HEADS), axis=1)
    scores = jnp.einsum("cin,cjn->cij", queries, keys, preferred_element_type=jnp.float32)
    lower = jnp.arange(SPAN)[:, None] >= jnp.arange(SPAN)[None, :]
    along = jnp.transpose(cumulative, (0, 2, 1))
    spread = along[:, :, :, None] - along[:, :, None, :]
    factor = jnp.exp(jnp.where(lower, spread, 0.0)) * lower
    step_cols = jnp.transpose(step_spans, (0, 2, 1))
    kernel = scores[:, None] * factor
    mixing = (kernel * step_cols[:, :, None, :]).astype(jnp.bfloat16)
    diag_out = jnp.einsum("chij,cjhp->cihp", mixing, rounded_in, preferred_element_type=jnp.float32)
    fade = jnp.exp(cumulative[:, -1:, :] - cumulative)
    tail = fade * step_spans
    weighted = (rounded_in * tail[..., None]).astype(jnp.bfloat16)
    span_state = jnp.einsum("cjhp,cjn->chpn", weighted, keys, preferred_element_type=jnp.float32)
    growth = jnp.exp(cumulative[:, -1, :])
    keep = 1.0 - starts.astype(jnp.float32)
    passing = jnp.prod(keep[:, None] * growth, axis=0)
    _, leaving = forward_chain(jnp.zeros_like(span_state[0]), growth, keep, span_state)
    prefix = prefix_2(
        (passing, leaving), "fsdp", combine, (jnp.ones_like(passing), jnp.zeros_like(leaving))
    )
    entering, _ = forward_chain(prefix[1], growth, keep, span_state)
    carried = entering.astype(jnp.bfloat16)
    from_state = jnp.einsum("cin,chpn->cihp", queries, carried, preferred_element_type=jnp.float32)
    rise = jnp.exp(cumulative)
    state_out = rise[..., None] * from_state
    mixed = (diag_out + state_out + skip_weight[None, None, :, None] * input_heads).reshape(
        count, INNER
    )
    gate_scale = gate_gain.astype(jnp.float32)
    normed_out = gated_norm(mixed, gate, gate_scale).astype(jnp.bfloat16)
    result = hidden + jnp.dot(normed_out, w_out, preferred_element_type=jnp.float32)
    saved = dict(
        hidden=hidden,
        norm_scale=norm_scale,
        normed=normed,
        gate=gate,
        extended=extended,
        masks=masks,
        conv_kernel=conv_kernel,
        conv_offset=conv_offset,
        input_heads=input_heads,
        rounded_in=rounded_in,
        keys=keys,
        queries=queries,
        valid_rows=valid_rows,
        dt_raw=dt_raw,
        decay=decay,
        step_cols=step_cols,
        factor=factor,
        kernel=kernel,
        mixing=mixing,
        fade=fade,
        tail=tail,
        weighted=weighted,
        growth=growth,
        keep=keep,
        passing=passing,
        entering=entering,
        carried=carried,
        rise=rise,
        state_out=state_out,
        mixed=mixed,
        gate_scale=gate_scale,
        normed_out=normed_out,
    )
    return (result, saved)


def layer_backward(grad_in, saved, weights, heads):
    norm_gain, w_gate, w_xbc, w_dt, conv_weight, conv_bias, gate_gain, w_out = weights
    dt_bias, a_log, skip_weight = heads
    hidden = saved["hidden"]
    count = hidden.shape[0]
    spans = count // SPAN
    rounded_in = saved["rounded_in"]
    keys = saved["keys"]
    queries = saved["queries"]
    out_low = grad_in.astype(jnp.bfloat16)
    grad_w_out = jnp.dot(saved["normed_out"].T, out_low, preferred_element_type=jnp.float32)
    grad_normed_out = jnp.dot(out_low, w_out.T, preferred_element_type=jnp.float32)
    _, pull_norm = jax.vjp(gated_norm, saved["mixed"], saved["gate"], saved["gate_scale"])
    grad_mixed, grad_gate, grad_gate_gain = pull_norm(grad_normed_out)
    gate_low = grad_gate.astype(jnp.bfloat16)
    grad_heads = grad_mixed.reshape(spans, SPAN, HEADS, HEAD_DIM)
    grad_skip = jnp.sum(grad_heads * saved["input_heads"], axis=(0, 1, 3))
    grad_inputs = skip_weight[None, None, :, None] * grad_heads
    diag_low = grad_heads.astype(jnp.bfloat16)
    state_low = (saved["rise"][..., None] * grad_heads).astype(jnp.bfloat16)
    grad_cum = jnp.sum(grad_heads * saved["state_out"], axis=-1)
    grad_mixing = jnp.einsum(
        "cihp,cjhp->chij", diag_low, rounded_in, preferred_element_type=jnp.float32
    )
    grad_x = jnp.einsum(
        "chij,cihp->cjhp", saved["mixing"], diag_low, preferred_element_type=jnp.float32
    )
    grad_queries = jnp.einsum(
        "cihp,chpn->cin", state_low, saved["carried"], preferred_element_type=jnp.float32
    )
    grad_entering = jnp.einsum(
        "cihp,cin->chpn", state_low, queries, preferred_element_type=jnp.float32
    )
    scaled = grad_mixing * saved["step_cols"][:, :, None, :]
    grad_scores = jnp.sum(scaled * saved["factor"], axis=1)
    grad_spread = scaled * saved["kernel"]
    grad_step_cols = jnp.sum(grad_mixing * saved["kernel"], axis=2)
    grad_cum = grad_cum + jnp.transpose(
        jnp.sum(grad_spread, axis=3) - jnp.sum(grad_spread, axis=2), (0, 2, 1)
    )
    scores_low = grad_scores.astype(jnp.bfloat16)
    grad_queries = grad_queries + jnp.einsum(
        "cij,cjn->cin", scores_low, keys, preferred_element_type=jnp.float32
    )
    grad_keys = jnp.einsum("cij,cin->cjn", scores_low, queries, preferred_element_type=jnp.float32)
    entering = saved["entering"]
    growth = saved["growth"]
    keep = saved["keep"]
    passing = saved["passing"]
    local_back, _, _ = back_chain(
        jnp.zeros_like(entering[0]), entering, growth, keep, grad_entering
    )
    suffix = entering_2(
        (passing, local_back), "fsdp", combine, (jnp.ones_like(passing), jnp.zeros_like(local_back))
    )
    _, grad_span, grad_growth = back_chain(suffix[1], entering, growth, keep, grad_entering)
    span_low = grad_span.astype(jnp.bfloat16)
    grad_weighted = jnp.einsum("chpn,cjn->cjhp", span_low, keys, preferred_element_type=jnp.float32)
    grad_keys = grad_keys + jnp.einsum(
        "cjhp,chpn->cjn", saved["weighted"], span_low, preferred_element_type=jnp.float32
    )
    tail = saved["tail"]
    grad_x = grad_x + grad_weighted * tail[..., None]
    grad_tail = jnp.sum(grad_weighted * rounded_in, axis=-1)
    grad_steps = grad_tail * saved["fade"] + jnp.transpose(grad_step_cols, (0, 2, 1))
    through_tail = grad_tail * tail
    grad_cum = grad_cum - through_tail
    grad_last = jnp.sum(through_tail, axis=1) + grad_growth * growth
    grad_cum = grad_cum.at[:, SPAN - 1, :].add(grad_last)
    grad_decay = jnp.cumsum(grad_cum[:, ::-1], axis=1)[:, ::-1].reshape(count, HEADS)
    grad_steps = grad_steps.reshape(count, HEADS) - jnp.exp(a_log) * grad_decay
    grad_a_log = jnp.sum(grad_decay * saved["decay"], axis=0)
    grad_pre = grad_steps * saved["valid_rows"][:, None] * jax.nn.sigmoid(saved["dt_raw"] + dt_bias)
    grad_dt_bias = jnp.sum(grad_pre, axis=0)
    dt_low = grad_pre.astype(jnp.bfloat16)
    grad_act = jnp.concatenate(
        [
            (grad_inputs + grad_x).reshape(count, INNER),
            grad_keys.reshape(count, STATE),
            grad_queries.reshape(count, STATE),
        ],
        axis=1,
    )
    _, pull_conv = jax.vjp(
        partial(conv_act, masks=saved["masks"]),
        saved["extended"],
        saved["conv_kernel"],
        saved["conv_offset"],
    )
    grad_ext, grad_conv_weight, grad_conv_bias = pull_conv(grad_act)
    returned = shifted(grad_ext[: KCONV - 1], "fsdp", -1)
    grad_conv_in = grad_ext[KCONV - 1 :].at[count - (KCONV - 1) :].add(returned)
    conv_low = grad_conv_in.astype(jnp.bfloat16)
    normed = saved["normed"]
    grad_normed = jnp.dot(gate_low, w_gate.T, preferred_element_type=jnp.float32)
    grad_normed = grad_normed + jnp.dot(conv_low, w_xbc.T, preferred_element_type=jnp.float32)
    grad_normed = grad_normed + jnp.dot(dt_low, w_dt.T, preferred_element_type=jnp.float32)
    grad_w_gate = jnp.dot(normed.T, gate_low, preferred_element_type=jnp.float32)
    grad_w_xbc = jnp.dot(normed.T, conv_low, preferred_element_type=jnp.float32)
    grad_w_dt = jnp.dot(normed.T, dt_low, preferred_element_type=jnp.float32)
    _, pull_rms = jax.vjp(rms_scale, hidden, saved["norm_scale"])
    grad_hidden, grad_norm_gain = pull_rms(grad_normed)
    weight_grads = (
        grad_norm_gain,
        grad_w_gate,
        grad_w_xbc,
        grad_w_dt,
        grad_conv_weight,
        grad_conv_bias,
        grad_gate_gain,
        grad_w_out,
    )
    return (grad_in + grad_hidden, weight_grads, (grad_dt_bias, grad_a_log, grad_skip))


def shards(
    tokens,
    starts,
    valid,
    norm_gain,
    w_gate,
    w_xbc,
    w_dt,
    conv_weight,
    conv_bias,
    dt_bias,
    a_log,
    skip_weight,
    gate_gain,
    w_out,
    cotangent,
):
    layers = norm_gain.shape[0]
    hidden = tokens.astype(jnp.float32)
    kept = []
    saves = []
    for layer_index in range(layers):
        whole = (
            lax.all_gather(norm_gain[layer_index], ("dp", "fsdp"), axis=0, tiled=True),
            lax.all_gather(w_gate[layer_index], ("dp", "fsdp"), axis=0, tiled=True),
            lax.all_gather(w_xbc[layer_index], ("dp", "fsdp"), axis=0, tiled=True),
            lax.all_gather(w_dt[layer_index], ("dp", "fsdp"), axis=0, tiled=True),
            lax.all_gather(conv_weight[layer_index], ("dp", "fsdp"), axis=1, tiled=True),
            lax.all_gather(conv_bias[layer_index], ("dp", "fsdp"), axis=0, tiled=True),
            lax.all_gather(gate_gain[layer_index], ("dp", "fsdp"), axis=0, tiled=True),
            lax.all_gather(w_out[layer_index], ("dp", "fsdp"), axis=0, tiled=True),
        )
        heads = (dt_bias[layer_index], a_log[layer_index], skip_weight[layer_index])
        hidden, saved = layer_forward(hidden, whole, heads, starts, valid)
        kept.append(None)
        saves.append(saved)
    grad = cotangent.astype(jnp.float32)
    owned_list = [None] * layers
    summed_list = [None] * layers
    for layer_index in reversed(range(layers)):
        whole = (
            lax.all_gather(norm_gain[layer_index], ("dp", "fsdp"), axis=0, tiled=True),
            lax.all_gather(w_gate[layer_index], ("dp", "fsdp"), axis=0, tiled=True),
            lax.all_gather(w_xbc[layer_index], ("dp", "fsdp"), axis=0, tiled=True),
            lax.all_gather(w_dt[layer_index], ("dp", "fsdp"), axis=0, tiled=True),
            lax.all_gather(conv_weight[layer_index], ("dp", "fsdp"), axis=1, tiled=True),
            lax.all_gather(conv_bias[layer_index], ("dp", "fsdp"), axis=0, tiled=True),
            lax.all_gather(gate_gain[layer_index], ("dp", "fsdp"), axis=0, tiled=True),
            lax.all_gather(w_out[layer_index], ("dp", "fsdp"), axis=0, tiled=True),
        )
        heads = (dt_bias[layer_index], a_log[layer_index], skip_weight[layer_index])
        grad, weight_grads, head_grads = layer_backward(grad, saves[layer_index], whole, heads)
        (
            grad_norm_gain,
            grad_w_gate,
            grad_w_xbc,
            grad_w_dt,
            grad_conv_weight,
            grad_conv_bias,
            grad_gate_gain,
            grad_w_out,
        ) = weight_grads
        grad_dt_bias, grad_a_log, grad_skip = head_grads
        owned_list[layer_index] = (
            lax.psum_scatter(grad_norm_gain, ("dp", "fsdp"), scatter_dimension=0, tiled=True),
            lax.psum_scatter(grad_w_gate, ("dp", "fsdp"), scatter_dimension=0, tiled=True),
            lax.psum_scatter(grad_w_xbc, ("dp", "fsdp"), scatter_dimension=0, tiled=True),
            lax.psum_scatter(grad_w_dt, ("dp", "fsdp"), scatter_dimension=0, tiled=True),
            lax.psum_scatter(grad_conv_weight, ("dp", "fsdp"), scatter_dimension=1, tiled=True),
            lax.psum_scatter(grad_conv_bias, ("dp", "fsdp"), scatter_dimension=0, tiled=True),
            lax.psum_scatter(grad_gate_gain, ("dp", "fsdp"), scatter_dimension=0, tiled=True),
            lax.psum_scatter(grad_w_out, ("dp", "fsdp"), scatter_dimension=0, tiled=True),
        )
        summed_list[layer_index] = lax.psum((grad_dt_bias, grad_a_log, grad_skip), ("dp", "fsdp"))

    def stacked(position, source):
        return jnp.stack([member[position] for member in source])

    return (
        hidden,
        grad,
        stacked(0, owned_list),
        stacked(1, owned_list),
        stacked(2, owned_list),
        stacked(3, owned_list),
        stacked(4, owned_list),
        stacked(5, owned_list),
        stacked(0, summed_list),
        stacked(1, summed_list),
        stacked(2, summed_list),
        stacked(6, owned_list),
        stacked(7, owned_list),
    )


def solution(mesh):
    return jax.shard_map(
        shards,
        mesh=mesh,
        in_specs=(
            P(("dp", "fsdp"), None),
            P(("dp", "fsdp")),
            P(("dp", "fsdp")),
            P(None, ("dp", "fsdp")),
            P(None, ("dp", "fsdp"), None),
            P(None, ("dp", "fsdp"), None),
            P(None, ("dp", "fsdp"), None),
            P(None, None, ("dp", "fsdp")),
            P(None, ("dp", "fsdp")),
            P(),
            P(),
            P(),
            P(None, ("dp", "fsdp")),
            P(None, ("dp", "fsdp"), None),
            P(("dp", "fsdp"), None),
        ),
        out_specs=(
            P(("dp", "fsdp"), None),
            P(("dp", "fsdp"), None),
            P(None, ("dp", "fsdp")),
            P(None, ("dp", "fsdp"), None),
            P(None, ("dp", "fsdp"), None),
            P(None, ("dp", "fsdp"), None),
            P(None, None, ("dp", "fsdp")),
            P(None, ("dp", "fsdp")),
            P(),
            P(),
            P(),
            P(None, ("dp", "fsdp")),
            P(None, ("dp", "fsdp"), None),
        ),
        check_vma=False,
    )
```

profile of v0, /device:TPU:0, one launch (start us, length us, event | category | flops | bytes accessed | tf_op | source)
XLA Modules:
  0.0 1766.0 jit_solution(8948943956029316214)
XLA Ops:
  13.1 42.6 %all-reduce.33 = (bf16[768]{0:T(1024)(128)(2,1)S(1)}, bf16[1792]{0:T(1024)(128)(2,1)S(1)}, bf16[1536]{0:T(1024)(128)(2,1)}, bf16[768]{0:T(1024)(128)(2,1)}, bf16...) all-reduce(bf16[768]{0:T(1024)(128)(2,1)S(1)} %dynamic-update-slice.13, ...), channel_id=4, replica_groups=mesh['dp'=8,'fsdp'=4] {'dp','fsdp'}, use_global_device_ids=true, to_apply=%add.17 | all-reduce | flops 8192 | bytes 32768
  57.0 41.1 %all-gather.4 = bf16[1,768,24]{2,1,0:T(8,128)(2,1)S(1)} all-gather(bf16[1,24,24]{2,1,0:T(8,128)(2,1)S(1)} %get-tuple-element.485), channel_id=6, replica_groups=mesh['dp'=8,'fsdp'=4] {'dp','fsdp'}, dimensions={1}, use_global_device_ids=true | all-gather | bytes 38016 | tf_op jit(solution)/shard_map/all_gather | solution.py:354
  105.5 39.5 %all-gather.1 = bf16[1,4,1792]{1,0,2:T(2,128)(2,1)S(1)} all-gather(bf16[1,4,56]{1,0,2:T(2,128)(2,1)S(1)} %copy.422), channel_id=3, replica_groups=mesh['dp'=8,'fsdp'=4] {'dp','fsdp'}, dimensions={2}, use_global_device_ids=true | all-gather | bytes 14784 | tf_op jit(solution)/shard_map/all_gather | solution.py:355
  147.1 37.5 %slice_reduce_fusion.7 = (f32[1792]{0:T(1024)S(1)}, f32[1792]{0:T(1024)S(1)}, f32[1792]{0:T(1024)S(1)}, f32[1792]{0:T(1024)S(1)}) fusion(f32[1,4,1792]{1,0,2:T(1,128)S(1)} %convert_element_type.479), kind=kLoop, calls=%fused_computation.169 | loop fusion | bytes 57344 | tf_op jit(solution)/shard_map/slice | solution.py:89
  184.7 2.7 fusion.16
  187.5 13.7 collective-permute-start
  204.5 3.0 fusion.201
  218.2 5.5 all-gather.5
  225.6 38.4 %all-gather.14 = bf16[1,768,24]{2,1,0:T(8,128)(2,1)S(1)} all-gather(bf16[1,24,24]{2,1,0:T(8,128)(2,1)} %get-tuple-element.484), channel_id=16, replica_groups=mesh['dp'=8,'fsdp'=4] {'dp','fsdp'}, dimensions={1}, use_global_device_ids=true | all-gather | bytes 38016 | tf_op jit(solution)/shard_map/all_gather | solution.py:354
  264.9 40.5 %all-gather.11 = bf16[1,4,1792]{1,0,2:T(2,128)(2,1)S(1)} all-gather(bf16[1,4,56]{1,0,2:T(2,128)(2,1)S(1)} %copy.423), channel_id=13, replica_groups=mesh['dp'=8,'fsdp'=4] {'dp','fsdp'}, dimensions={2}, use_global_device_ids=true | all-gather | bytes 14784 | tf_op jit(solution)/shard_map/all_gather | solution.py:355
  306.3 38.1 %slice_reduce_fusion.3 = (f32[1792]{0:T(1024)}, f32[1792]{0:T(1024)}, f32[1792]{0:T(1024)}, f32[1792]{0:T(1024)}) fusion(f32[1,4,1792]{1,0,2:T(1,128)S(1)} %convert_element_type.483), kind=kLoop, calls=%fused_computation.165 | loop fusion | bytes 57344 | tf_op jit(solution)/shard_map/slice | solution.py:89
  345.1 3.0 copy.350
  353.3 4.6 fusion.57
  357.8 3.0 copy.351
  360.8 4.8 multiply_reduce_fusion.23
  366.2 3.1 multiply_reduce_fusion.28
  373.6 38.4 %all-gather.41.cloned.1.call-done = bf16[1,768,1792]{2,1,0:T(8,128)(2,1)} async-done(((bf16[1,24,1792]{2,1,0:T(8,128)(2,1)}), bf16[1,768,1792]{2,1,0:T(8,128)(2,1)}) %all-gather.41.cloned.1.call-update) | async-done | bytes 2752528 | tf_op jit(solution)/shard_map/all_gather | solution.py:353
  412.0 2.7 fusion.19
  419.5 3.0 copy.362
  424.2 3.0 fusion.198
  436.0 5.0 all-gather.15
  446.2 3.0 copy.369
  450.7 3.0 copy.364
  458.6 4.6 fusion.56
  463.3 3.0 copy.365
  466.3 45.3 %all-gather.45.cloned.1.call-done = bf16[1,768,1536]{2,1,0:T(8,128)(2,1)} async-done(((bf16[1,24,1536]{2,1,0:T(8,128)(2,1)}), bf16[1,768,1536]{2,1,0:T(8,128)(2,1)}) %all-gather.45.cloned.1.call-update) | async-done | bytes 2359312 | tf_op jit(solution)/shard_map/all_gather | solution.py:352
  511.6 4.8 multiply_reduce_fusion.22
  516.3 54.3 %all-gather.47.cloned.1.call-done = bf16[1,1536,768]{2,1,0:T(8,128)(2,1)} async-done(((bf16[1,48,768]{2,1,0:T(8,128)(2,1)}), bf16[1,1536,768]{2,1,0:T(8,128)(2,1)}) %all-gather.47.cloned.1.call-update) | async-done | bytes 2359312 | tf_op jit(solution)/shard_map/all_gather | solution.py:358
  570.6 4.0 multiply_reduce_fusion.12
  574.7 4.3 multiply_reduce_fusion.14
  587.1 3.0 copy.386
  590.1 3.2 copy.367
  593.3 6.2 fusion.6
  609.6 3.4 fusion.26
  614.0 7.1 while.58
  626.2 3.1 fusion.55
  629.4 3.1 copy.375
  632.5 2.9 multiply_multiply_fusion.5
  652.5 3.1 fusion.70
  672.9 3.0 copy.384
  676.0 6.5 fusion.4
  685.4 2.8 multiply_reduce_fusion.16
  697.2 3.4 fusion.34
  700.7 5.7 while.59
  712.0 3.1 fusion.54
  715.1 3.0 copy.392
  718.2 8.1 multiply_reduce_fusion.7
  741.1 3.0 fusion.67
  748.5 3.0 fusion.181
  752.6 4.5 fusion.108
  758.2 3.0 fusion.208
  762.4 3.1 fusion.184
  765.5 4.5 fusion.209
  771.3 3.4 fusion.87
  775.8 3.5 fusion.64
  780.5 97.9 %all-reduce.36.cloned.1.call-done = (f32[768]{0:T(1024)}, f32[768]{0:T(1024)}, f32[4,1792]{1,0:T(4,128)}, f32[4,1792]{1,0:T(4,128)}, f32[1792]{0:T(1024)}, /*ind...) async-done(((f32[768]{0:T(1024)}, f32[768]{0:T(1024)}, ...) | async-done | bytes 90704
  890.4 88.7 %reduce-scatter.29.cloned.1.call-done = f32[24,24]{1,0:T(8,128)} async-done(((f32[768,24]{1,0:T(8,128)}), f32[24,24]{1,0:T(8,128)}) %reduce-scatter.29.cloned.1.call-update) | async-done | bytes 2320
  979.1 99.7 %reduce-scatter.27.cloned.1.call-done = f32[24,24]{1,0:T(8,128)} async-done(((f32[768,24]{1,0:T(8,128)}), f32[24,24]{1,0:T(8,128)}) %reduce-scatter.27.cloned.1.call-update) | async-done | bytes 2320
  1080.2 110.1 %reduce-scatter.25.cloned.1.call-done = f32[48,768]{1,0:T(8,128)} async-done(((f32[1536,768]{1,0:T(8,128)}), f32[48,768]{1,0:T(8,128)}) %reduce-scatter.25.cloned.1.call-update) | async-done | bytes 147472 | tf_op jit(solution)/shard_map/reduce_scatter | solution.py:399
  1190.3 112.3 %reduce-scatter.23.cloned.1.call-done = f32[48,768]{1,0:T(8,128)} async-done(((f32[1536,768]{1,0:T(8,128)}), f32[48,768]{1,0:T(8,128)}) %reduce-scatter.23.cloned.1.call-update) | async-done | bytes 147472 | tf_op jit(solution)/shard_map/reduce_scatter | solution.py:399
  1304.3 109.7 %reduce-scatter.17.cloned.1.call-done = f32[24,1536]{1,0:T(8,128)} async-done(((f32[768,1536]{1,0:T(8,128)}), f32[24,1536]{1,0:T(8,128)}) %reduce-scatter.17.cloned.1.call-update) | async-done | bytes 147472 | tf_op jit(solution)/shard_map/reduce_scatter | solution.py:393
  1414.0 112.4 %reduce-scatter.15.cloned.1.call-done = f32[24,1536]{1,0:T(8,128)} async-done(((f32[768,1536]{1,0:T(8,128)}), f32[24,1536]{1,0:T(8,128)}) %reduce-scatter.15.cloned.1.call-update) | async-done | bytes 147472 | tf_op jit(solution)/shard_map/reduce_scatter | solution.py:393
  1528.1 113.3 %reduce-scatter.21.cloned.1.call-done = f32[24,1792]{1,0:T(8,128)} async-done(((f32[768,1792]{1,0:T(8,128)}), f32[24,1792]{1,0:T(8,128)}) %reduce-scatter.21.cloned.1.call-update) | async-done | bytes 172048 | tf_op jit(solution)/shard_map/reduce_scatter | solution.py:394
  1641.4 116.1 %reduce-scatter.19.cloned.1.call-done = f32[24,1792]{1,0:T(8,128)} async-done(((f32[768,1792]{1,0:T(8,128)}), f32[24,1792]{1,0:T(8,128)}) %reduce-scatter.19.cloned.1.call-update) | async-done | bytes 172048 | tf_op jit(solution)/shard_map/reduce_scatter | solution.py:394
  (660 shorter events, 202.7 us)
Async XLA Ops:
  7.2 97.7 %copy-start.175 = (bf16[2,4,56]{2,1,0:T(4,128)(2,1)S(1)}, bf16[2,4,56]{2,1,0:T(4,128)(2,1)}, u32[]{:S(2)}) copy-start(bf16[2,4,56]{2,1,0:T(4,128)(2,1)} %param.38) | copy-start | bytes 2692
  7.2 177.5 %all-gather.33.cloned.1.call-start = ((), (), s32[]{:S(2)}) async-start(), calls=%async_computation.14 | async-start | bytes 2838528 | tf_op jit(solution)/shard_map/all_gather | solution.py:353
  8.9 342.2 %all-gather.35.cloned.1.call-start = ((), (), s32[]{:S(2)}) async-start(), calls=%async_computation.15 | async-start | bytes 1966080 | tf_op jit(solution)/shard_map/all_gather | solution.py:28
  9.6 137.3 %copy-start.124 = (f32[256]{0:T(256)}, f32[256]{0:T(256)S(1)}, u32[]{:S(2)}) copy-start(f32[256]{0:T(256)S(1)} %convert_element_type.413) | copy-start | bytes 3076
  99.4 46.7 %copy-start.160 = (f32[256]{0:T(256)}, f32[256]{0:T(256)S(1)}, u32[]{:S(2)}) copy-start(f32[256]{0:T(256)S(1)} %fusion.83) | copy-start | bytes 3076
  100.6 260.2 %copy-start.112 = (f32[256]{0:T(256)}, f32[256]{0:T(256)S(1)}, u32[]{:S(2)}) copy-start(f32[256]{0:T(256)S(1)} %fusion.167) | copy-start | bytes 3076
  103.3 43.6 %copy-start.71 = (f32[256,24]{1,0:T(8,128)}, f32[256,24]{1,0:T(8,128)S(1)}, u32[]{:S(2)}) copy-start(f32[256,24]{1,0:T(8,128)S(1)} %convolution_add_fusion.7) | copy-start | bytes 73732
  146.3 38.3 %copy-start.67 = (f32[1,24,256]{1,2,0:T(8,128)}, f32[1,24,256]{1,2,0:T(8,128)S(1)}, u32[]{:S(2)}) copy-start(f32[1,24,256]{1,2,0:T(8,128)S(1)} %get-tuple-element.448) | copy-start | bytes 73732
  146.3 58.1 %copy-start.127 = (f32[256]{0:T(256)}, f32[256]{0:T(256)S(1)}, u32[]{:S(2)}) copy-start(f32[256]{0:T(256)S(1)} %get-tuple-element.514) | copy-start | bytes 3076
  146.3 58.1 %copy-start.131 = (f32[256]{0:T(256)}, f32[256]{0:T(256)S(1)}, u32[]{:S(2)}) copy-start(f32[256]{0:T(256)S(1)} %get-tuple-element.515) | copy-start | bytes 3076
  146.4 38.3 %copy-start.164 = (f32[24]{0:T(128)}, f32[24]{0:T(128)S(1)}, u32[]{:S(2)}) copy-start(f32[24]{0:T(128)S(1)} %get-tuple-element.482) | copy-start | bytes 292
  147.1 54.1 %copy-start.75 = (f32[1,256,24]{2,1,0:T(8,128)}, f32[1,256,24]{2,1,0:T(8,128)S(1)}, u32[]{:S(2)}) copy-start(f32[1,256,24]{2,1,0:T(8,128)S(1)} %bitcast_multiply_fusion.9) | copy-start | bytes 73732
  147.1 37.6 %copy-start.14 = (bf16[256,768]{1,0:T(8,128)(2,1)S(1)}, bf16[256,768]{1,0:T(8,128)(2,1)}, u32[]{:S(2)}) copy-start(bf16[256,768]{1,0:T(8,128)(2,1)} %param.31) | copy-start | bytes 1179652
  184.7 19.8 %copy-start.104 = (f32[1792]{0:T(1024)}, f32[1792]{0:T(1024)S(1)}, u32[]{:S(2)}) copy-start(f32[1792]{0:T(1024)S(1)} %get-tuple-element.351) | copy-start | bytes 21508
  184.7 19.8 %copy-start.106 = (f32[1792]{0:T(1024)}, f32[1792]{0:T(1024)S(1)}, u32[]{:S(2)}) copy-start(f32[1792]{0:T(1024)S(1)} %get-tuple-element.352) | copy-start | bytes 21508
  184.7 19.8 %copy-start.108 = (f32[1792]{0:T(1024)}, f32[1792]{0:T(1024)S(1)}, u32[]{:S(2)}) copy-start(f32[1792]{0:T(1024)S(1)} %get-tuple-element.353) | copy-start | bytes 21508
  184.7 19.8 %copy-start.110 = (f32[1792]{0:T(1024)}, f32[1792]{0:T(1024)S(1)}, u32[]{:S(2)}) copy-start(f32[1792]{0:T(1024)S(1)} %get-tuple-element.354) | copy-start | bytes 21508
  187.5 13.8 copy-start.79
  187.5 15.6 collective-permute-start
  211.2 52.9 %copy-start.35 = (bf16[256,1536]{0,1:T(8,128)(2,1)}, bf16[256,1536]{0,1:T(8,128)(2,1)S(1)}, u32[]{:S(2)}) copy-start(bf16[256,1536]{0,1:T(8,128)(2,1)S(1)} %copy.349) | copy-start | bytes 2359300
  211.2 13.8 copy-start.181
  211.2 14.4 copy-start.169
  211.2 14.4 copy-start.174
  213.4 147.4 %all-gather.37.cloned.1.call-start = ((), (), s32[]{:S(2)}) async-start(), calls=%async_computation.16 | async-start | bytes 2433024 | tf_op jit(solution)/shard_map/all_gather | solution.py:352
  215.1 150.6 %all-gather.39.cloned.1.call-start = ((), (), s32[]{:S(2)}) async-start(), calls=%async_computation.17 | async-start | bytes 2433024 | tf_op jit(solution)/shard_map/all_gather | solution.py:358
  216.7 195.3 %all-gather.41.cloned.1.call-start = ((), (), s32[]{:S(2)}) async-start(), calls=%async_computation.18 | async-start | bytes 2838528 | tf_op jit(solution)/shard_map/all_gather | solution.py:353
  217.3 239.3 %all-gather.43.cloned.1.call-start = ((), (), s32[]{:S(2)}) async-start(), calls=%async_computation.19 | async-start | bytes 1966080 | tf_op jit(solution)/shard_map/all_gather | solution.py:28
  225.6 127.4 %copy-start.182 = (f32[24]{0:T(128)}, f32[24]{0:T(128)S(1)}, u32[]{:S(2)}) copy-start(f32[24]{0:T(128)S(1)} %get-tuple-element.493) | copy-start | bytes 292
  225.6 143.7 %copy-start.117 = (f32[768]{0:T(1024)}, f32[768]{0:T(1024)S(1)}, u32[]{:S(2)}) copy-start(f32[768]{0:T(1024)S(1)} %convert_element_type.490) | copy-start | bytes 9220
  264.1 106.2 %copy-start.62 = (bf16[1,768,24]{2,1,0:T(8,128)(2,1)}, bf16[1,768,24]{2,1,0:T(8,128)(2,1)S(1)}, u32[]{:S(2)}) copy-start(bf16[1,768,24]{2,1,0:T(8,128)(2,1)S(1)} %all-gather.14) | copy-start | bytes 110596
  306.3 38.2 %copy-start.168 = (bf16[1792]{0:T(1024)(128)(2,1)S(1)}, bf16[1792]{0:T(1024)(128)(2,1)}, u32[]{:S(2)}) copy-start(bf16[1792]{0:T(1024)(128)(2,1)} %get-tuple-element.418) | copy-start | bytes 10756
  345.1 7.9 copy-start.153
  370.3 44.4 %copy-start.27 = (bf16[256,768]{1,0:T(8,128)(2,1)}, bf16[256,768]{1,0:T(8,128)(2,1)S(1)}, u32[]{:S(2)}) copy-start(bf16[256,768]{1,0:T(8,128)(2,1)S(1)} %multiply_convert_fusion.20) | copy-start | bytes 1179652
  370.6 44.1 %copy-start.60 = (f32[256,24]{1,0:T(8,128)}, f32[256,24]{1,0:T(8,128)S(1)}, u32[]{:S(2)}) copy-start(f32[256,24]{1,0:T(8,128)S(1)} %convolution_add_fusion.6) | copy-start | bytes 73732
  372.3 42.4 %copy-start.158 = (f32[24,2]{0,1:T(2,128)}, f32[24,2]{0,1:T(2,128)S(1)}, u32[]{:S(2)}) copy-start(f32[24,2]{0,1:T(2,128)S(1)} %slice_bitcast_fusion.2) | copy-start | bytes 580
  373.0 44.6 %copy-start.69 = (f32[1,24,256]{1,2,0:T(8,128)}, f32[1,24,256]{1,2,0:T(8,128)S(1)}, u32[]{:S(2)}) copy-start(f32[1,24,256]{1,2,0:T(8,128)S(1)} %get-tuple-element.439) | copy-start | bytes 73732
  373.5 41.2 %copy-start.166 = (f32[24]{0:T(128)}, f32[24]{0:T(128)S(1)}, u32[]{:S(2)}) copy-start(f32[24]{0:T(128)S(1)} %get-tuple-element.480) | copy-start | bytes 292
  373.6 44.5 %copy-start.78 = (f32[1,256,24]{2,1,0:T(8,128)}, f32[1,256,24]{2,1,0:T(8,128)S(1)}, u32[]{:S(2)}) copy-start(f32[1,256,24]{2,1,0:T(8,128)S(1)} %bitcast_multiply_fusion.8) | copy-start | bytes 73732
  415.4 7.3 collective-permute-start.1
  429.4 13.3 copy-start.159
  430.8 15.4 copy-start.36
  432.9 78.7 %all-gather.45.cloned.1.call-start = ((), (), s32[]{:S(2)}) async-start(), calls=%async_computation.20 | async-start | bytes 2433024 | tf_op jit(solution)/shard_map/all_gather | solution.py:352
  433.6 137.0 %all-gather.47.cloned.1.call-start = ((), (), s32[]{:S(2)}) async-start(), calls=%async_computation.21 | async-start | bytes 2433024 | tf_op jit(solution)/shard_map/all_gather | solution.py:358
  434.4 178.6 %all-gather.49.cloned.1.call-start = ((), (), s32[]{:S(2)}) async-start(), calls=%async_computation.22 | async-start | bytes 1966080 | tf_op jit(solution)/shard_map/all_gather | solution.py:50
  585.7 114.9 %all-gather.51.cloned.1.call-start = ((), (), s32[]{:S(2)}) async-start(), calls=%async_computation.23 | async-start | bytes 1966080 | tf_op jit(solution)/shard_map/all_gather | solution.py:50
  643.9 5.6 collective-permute-start.2
  662.8 34.4 %copy-start.51 = (bf16[256,1536]{1,0:T(8,128)(2,1)}, bf16[256,1536]{1,0:T(8,128)(2,1)S(1)}, u32[]{:S(2)}) copy-start(bf16[256,1536]{1,0:T(8,128)(2,1)S(1)} %get-tuple-element.449) | copy-start | bytes 2359300
  669.7 208.7 %all-reduce.36.cloned.1.call-start = ((), (), s32[]{:S(2)}) async-start(), calls=%async_computation.26 | async-start | bytes 202752
  718.1 8.2 copy-start.105
  718.1 8.2 copy-start.107
  718.1 8.2 copy-start.109
  718.1 8.2 copy-start.111
  718.1 8.2 copy-start.130
  718.1 8.2 copy-start.134
  718.1 8.2 copy-start.147
  733.8 5.2 collective-permute-start.3
  746.0 233.1 %reduce-scatter.29.cloned.1.call-start = ((), (), s32[]{:S(2)}) async-start(), calls=%async_computation.25 | async-start | bytes 405504
  747.1 331.7 %reduce-scatter.27.cloned.1.call-start = ((), (), s32[]{:S(2)}) async-start(), calls=%async_computation.24 | async-start | bytes 405504
  748.4 441.9 %reduce-scatter.25.cloned.1.call-start = ((), (), s32[]{:S(2)}) async-start(), calls=%async_computation.13 | async-start | bytes 4866048 | tf_op jit(solution)/shard_map/reduce_scatter | solution.py:399
  751.5 551.1 %reduce-scatter.23.cloned.1.call-start = ((), (), s32[]{:S(2)}) async-start(), calls=%async_computation.12 | async-start | bytes 4866048 | tf_op jit(solution)/shard_map/reduce_scatter | solution.py:399
  757.1 656.9 %reduce-scatter.17.cloned.1.call-start = ((), (), s32[]{:S(2)}) async-start(), calls=%async_computation.9 | async-start | bytes 4866048 | tf_op jit(solution)/shard_map/reduce_scatter | solution.py:393
  761.3 765.2 %reduce-scatter.15.cloned.1.call-start = ((), (), s32[]{:S(2)}) async-start(), calls=%async_computation.8 | async-start | bytes 4866048 | tf_op jit(solution)/shard_map/reduce_scatter | solution.py:393
  765.5 875.9 %reduce-scatter.21.cloned.1.call-start = ((), (), s32[]{:S(2)}) async-start(), calls=%async_computation.11 | async-start | bytes 5677056 | tf_op jit(solution)/shard_map/reduce_scatter | solution.py:394
  770.1 987.4 %reduce-scatter.19.cloned.1.call-start = ((), (), s32[]{:S(2)}) async-start(), calls=%async_computation.10 | async-start | bytes 5677056 | tf_op jit(solution)/shard_map/reduce_scatter | solution.py:394
  (146 other events, 429.0 us)
Sparse Core Ops, SparseCore 0:
  11.5 60.7 all-gather.32
  213.5 17.0 all-gather.34
  233.6 59.0 all-gather.36
  296.0 56.1 all-gather.38
  354.9 57.0 all-gather.40
  433.0 18.3 all-gather.42
  454.3 57.2 all-gather.44
  514.5 56.1 all-gather.46
  585.9 18.5 all-gather.48
  669.8 19.4 all-gather.50
  746.1 132.2 all-reduce.35
  883.2 95.8 reduce-scatter.28
  984.8 93.9 reduce-scatter.26
  1084.2 106.0 reduce-scatter.24
  1196.5 106.0 reduce-scatter.22
  1307.9 106.0 reduce-scatter.16
  1420.3 106.1 reduce-scatter.14
  1531.8 109.5 reduce-scatter.20
  1647.9 109.5 reduce-scatter.18
where the time goes:
time: 1770 us
  waiting for transfers between devices  1100 us (62%)
  blocking collectives  213 us (12%)
  local copies, waits for them, and re-layouts  189 us (11%)
  matrix products  128 us (7%)
  other arithmetic  97.5 us (6%)
  starting transfers between devices  19.8 us (1%)
    unnamed x22, waiting for transfers between devices  289 us
    reduce_scatter x2, waiting for transfers between devices, shards(): lax.psum_scatter(grad_w_xbc, ('dp', 'fsdp'), scatter_dimension=0, tiled=T...  229 us
    reduce_scatter x2, waiting for transfers between devices, shards(): lax.psum_scatter(grad_w_out, ('dp', 'fsdp'), scatter_dimension=0, tiled=T...  222 us
    reduce_scatter x2, waiting for transfers between devices, shards(): lax.psum_scatter(grad_w_gate, ('dp', 'fsdp'), scatter_dimension=0, tiled=...  222 us
    all_gather x2, blocking collectives, shards(): lax.all_gather(conv_weight[layer_index], ('dp', 'fsdp'), axis=1, tiled=True)  80 us
    all_gather x2, blocking collectives, shards(): lax.all_gather(w_dt[layer_index], ('dp', 'fsdp'), axis=0, tiled=True)  79.6 us
    slice x2, local copies, waits for them, and re-layouts, conv_act(): total = bias[None, :] + weight[KCONV - 1][None, :] * extended[KCONV - 1:]  75.7 us
    all_gather x2, waiting for transfers between devices, shards(): lax.all_gather(w_out[layer_index], ('dp', 'fsdp'), axis=0, tiled=True)  54.3 us
  transfers between devices with their start and end apart: 23, of which 12 were waited for; matrix products, arithmetic and copies ran while one was open for 15% of the time, Pallas kernels for 0%

commit v1 on v0

--- a/solution.py
+++ b/solution.py
@@ -22,49 +22,192 @@
     return lax.ppermute(block, axis, route)
 
 
-def prefix_2(shard, axis, join, neutral):
-    place = lax.axis_index(axis)
-    gathered = jax.tree.map(
-        lambda a, kind: lax.all_gather(a.astype(kind), axis), shard, (jnp.bfloat16, jnp.bfloat16)
-    )
-    state = jax.tree.map(lambda a, e: jnp.zeros_like(a) + jnp.asarray(e, a.dtype), shard, neutral)
-
-    def prefix_one(step, state):
-        return join(
-            state,
-            jax.tree.map(
-                lambda a, own: lax.dynamic_index_in_dim(a, step, 0, False).astype(own.dtype),
-                gathered,
-                shard,
-            ),
+AXES = ("dp", "fsdp")
+
+
+def radices(count):
+    factors = []
+    for radix in (2, 2, 2, 4):
+        if count % radix == 0 and count > 1:
+            factors.append(radix)
+            count //= radix
+    radix = 2
+    while count > 1:
+        while count % radix:
+            radix += 1
+        factors.append(radix)
+        count //= radix
+    return factors
+
+
+class Grid:
+    def __init__(self):
+        self.count = lax.axis_size("dp") * lax.axis_size("fsdp")
+        self.factors = radices(self.count)
+        self.place = lax.axis_index("dp") * lax.axis_size("fsdp") + lax.axis_index("fsdp")
+        self.strides = []
+        stride = 1
+        for radix in self.factors:
+            self.strides.append(stride)
+            stride *= radix
+        self.depth = len(self.factors)
+
+    def digit(self, k):
+        return (self.place // self.strides[k]) % self.factors[k]
+
+    def dims(self):
+        return tuple(reversed(self.factors))
+
+    def axis(self, k):
+        return self.depth - 1 - k
+
+    def swap(self, block, k):
+        stride = self.strides[k]
+        route = []
+        for i in range(self.count):
+            up = (i // stride) % 2 == 0
+            route.append((i, i + stride if up else i - stride))
+        return lax.ppermute(block, AXES, route)
+
+    def hop(self, block, k, way, keep):
+        stride, radix = self.strides[k], self.factors[k]
+        route = []
+        for i in range(self.count):
+            digit = (i // stride) % radix
+            if 0 <= digit + way < radix and keep(digit):
+                route.append((i, i + way * stride))
+        return lax.ppermute(block, AXES, route)
+
+    def gather_step(self, block, k):
+        axis, radix = self.axis(k), self.factors[k]
+        digit = self.digit(k)
+        if radix == 2:
+            other = self.swap(block, k)
+            first = jnp.where(digit == 0, block, other)
+            second = jnp.where(digit == 0, other, block)
+            return jnp.concatenate([first, second], axis=axis)
+        before, after = [], []
+        left = right = block
+        for d in range(1, radix):
+            left = self.hop(left, k, 1, lambda digit: digit >= d - 1)
+            right = self.hop(right, k, -1, lambda digit: digit + d - 1 < radix)
+            before.insert(0, left)
+            after.append(right)
+        line = jnp.concatenate(before + [block] + after, axis=axis)
+        return lax.dynamic_slice_in_dim(line, radix - 1 - digit, radix, axis)
+
+    def scatter_step(self, block, k, kind):
+        axis, radix = self.axis(k), self.factors[k]
+        digit = self.digit(k)
+
+        def pick(index):
+            index = jnp.clip(index, 0, radix - 1)
+            return lax.dynamic_slice_in_dim(block, index, 1, axis)
+
+        wide = jnp.float32
+        if radix == 2:
+            got = self.swap(pick(1 - digit), k)
+            return (pick(digit).astype(wide) + got.astype(wide)).astype(kind)
+        total = pick(digit).astype(wide)
+        for way in (1, -1):
+            run = None
+            for d in range(radix - 1, 0, -1):
+                part = pick(digit + way * d)
+                if run is not None:
+                    part = (part.astype(wide) + run.astype(wide)).astype(block.dtype)
+                run = self.hop(part, k, way, lambda digit: 0 <= digit + way * d < radix)
+            total = total + run.astype(wide)
+        return total.astype(kind)
+
+    def orders(self):
+        far = list(range(self.depth - 1, 2, -1))
+        if self.depth < 3:
+            one = list(range(self.depth - 1, -1, -1))
+            return far, one[:-1], one[:-1]
+        return far, [1, 2], [2, 1]
+
+    def sum_all(self, value):
+        for k in range(self.depth):
+            if self.factors[k] == 2:
+                value = value + self.swap(value, k)
+            else:
+                value = lax.psum(value, AXES) if False else self.sum_line(value, k)
+        return value
+
+    def sum_line(self, value, k):
+        stride, radix = self.strides[k], self.factors[k]
+        if radix & (radix - 1):
+            raise ValueError(radix)
+        step = 1
+        while step < radix:
+            route = []
+            for i in range(self.count):
+                digit = (i // stride) % radix
+                route.append((i, i + ((digit ^ step) - digit) * stride))
+            value = value + lax.ppermute(value, AXES, route)
+            step *= 2
+        return value
+
+
+def tied(value, *others):
+    others = [o for o in others if o is not None]
+    if not others:
+        return value
+    return lax.optimization_barrier((value, *others))[0]
+
+
+def gather_weights(grid, shards_list):
+    far, first, second = grid.orders()
+    gathered = []
+    last_far = last_near = None
+    for shard in shards_list:
+        rows, cols = shard.shape
+        block = shard.reshape((1,) * grid.depth + shard.shape)
+        block = tied(block, last_far)
+        for k in far:
+            block = grid.gather_step(block, k)
+        last_far = block
+        block = tied(block, last_near)
+        cut = cols // 256 * 128
+        parts = []
+        for order, part in ((first, block[..., :cut]), (second, block[..., cut:])):
+            for k in order:
+                part = grid.gather_step(part, k)
+            parts.append(part)
+        last_near = parts[0]
+        gathered.append(
+            [grid.gather_step(p, 0).reshape(grid.count * rows, p.shape[-1]) for p in parts]
         )
-
-    return lax.fori_loop(0, place, prefix_one, state)
-
-
-def entering_2(shard, axis, join, neutral):
-    count = lax.axis_size(axis)
-    place = lax.axis_index(axis)
-    ahead = count - 1 - place
-    gathered = jax.tree.map(
-        lambda a, kind: lax.all_gather(a.astype(kind), axis),
-        shard,
-        jax.tree.map(lambda a: jnp.bfloat16 if a.dtype == jnp.float32 else a.dtype, shard),
-    )
-    state = jax.tree.map(lambda a, e: jnp.zeros_like(a) + jnp.asarray(e, a.dtype), shard, neutral)
-
-    def entering_one(step, state):
-        source = count - 1 - step
-        return join(
-            state,
-            jax.tree.map(
-                lambda a, own: lax.dynamic_index_in_dim(a, source, 0, False).astype(own.dtype),
-                gathered,
-                shard,
-            ),
-        )
-
-    return lax.fori_loop(0, ahead, entering_one, state)
+    return gathered
+
+
+def scatter_grads(grid, whole):
+    far, first, second = grid.orders()
+    rows = whole.shape[0] // grid.count
+    cols = whole.shape[1]
+    block = whole.reshape(grid.dims() + (rows, cols))
+    cut = cols // 256 * 128
+    parts = []
+    for order, part in ((first, block[..., :cut]), (second, block[..., cut:])):
+        part = grid.scatter_step(part, 0, jnp.bfloat16)
+        for k in order:
+            part = grid.scatter_step(part, k, jnp.bfloat16)
+        parts.append(part)
+    block = jnp.concatenate(parts, axis=-1)
+    for k in reversed(far):
+        block = grid.scatter_step(block, k, jnp.bfloat16 if k != far[0] else jnp.float32)
+    return block.reshape(rows, cols).astype(jnp.float32)
+
+
+def state_chain(growth, keep, fresh, axis, way):
+    devices = lax.axis_size(axis)
+    carry = jnp.zeros_like(fresh)
+    for s in range(1, devices):
+        leaving = (growth * carry + fresh) * keep
+        at = s - 1 if way == 1 else devices - s
+        got = lax.ppermute(leaving.astype(jnp.bfloat16), axis, [(at, at + way)])
+        carry = carry + got.astype(jnp.float32)
+    return carry
 
 
 def rms_scale(hidden, gain):
@@ -91,30 +234,6 @@
         window = lax.slice_in_dim(extended, KCONV - 1 - shift, KCONV - 1 - shift + count, axis=0)
         total = total + weight[KCONV - 1 - shift][None, :] * window * masks[shift - 1][:, None]
     return jax.nn.silu(total)
-
-
-def combine(earlier, later):
-    return (earlier[0] * later[0], later[0][:, None, None] * earlier[1] + later[1])
-
-
-def forward_chain(arriving, growth, keep, fresh):
-    carry = arriving
-    entering = keep[0] * carry
-    states = [entering]
-    carry = growth[0][:, None, None] * entering + fresh[0]
-    return (jnp.stack(states), carry)
-
-
-def back_chain(arriving, entering, growth, keep, local_grad):
-    spans = entering.shape[0]
-    pending = arriving
-    fresh_grads = [None] * spans
-    grow_grads = [None] * spans
-    for index in reversed(range(spans)):
-        fresh_grads[index] = pending
-        grow_grads[index] = jnp.sum(pending * entering[index], axis=(1, 2))
-        pending = keep[index] * (local_grad[index] + growth[index][:, None, None] * pending)
-    return (pending, jnp.stack(fresh_grads), jnp.stack(grow_grads))
 
 
 def layer_forward(hidden, weights, heads, starts, valid):
@@ -157,12 +276,8 @@
     span_state = jnp.einsum("cjhp,cjn->chpn", weighted, keys, preferred_element_type=jnp.float32)
     growth = jnp.exp(cumulative[:, -1, :])
     keep = 1.0 - starts.astype(jnp.float32)
-    passing = jnp.prod(keep[:, None] * growth, axis=0)
-    _, leaving = forward_chain(jnp.zeros_like(span_state[0]), growth, keep, span_state)
-    prefix = prefix_2(
-        (passing, leaving), "fsdp", combine, (jnp.ones_like(passing), jnp.zeros_like(leaving))
-    )
-    entering, _ = forward_chain(prefix[1], growth, keep, span_state)
+    carry = state_chain((keep * growth[0])[:, None, None], 1.0, span_state[0], "fsdp", 1)
+    entering = (keep * carry)[None]
     carried = entering.astype(jnp.bfloat16)
     from_state = jnp.einsum("cin,chpn->cihp", queries, carried, preferred_element_type=jnp.float32)
     rise = jnp.exp(cumulative)
@@ -198,7 +313,6 @@
         weighted=weighted,
         growth=growth,
         keep=keep,
-        passing=passing,
         entering=entering,
         carried=carried,
         rise=rise,
@@ -258,14 +372,9 @@
     entering = saved["entering"]
     growth = saved["growth"]
     keep = saved["keep"]
-    passing = saved["passing"]
-    local_back, _, _ = back_chain(
-        jnp.zeros_like(entering[0]), entering, growth, keep, grad_entering
-    )
-    suffix = entering_2(
-        (passing, local_back), "fsdp", combine, (jnp.ones_like(passing), jnp.zeros_like(local_back))
-    )
-    _, grad_span, grad_growth = back_chain(suffix[1], entering, growth, keep, grad_entering)
+    pending = state_chain(growth[0][:, None, None], keep, grad_entering[0], "fsdp", -1)
+    grad_span = pending[None]
+    grad_growth = jnp.sum(pending * entering[0], axis=(1, 2))[None]
     span_low = grad_span.astype(jnp.bfloat16)
     grad_weighted = jnp.einsum("chpn,cjn->cjhp", span_low, keys, preferred_element_type=jnp.float32)
     grad_keys = grad_keys + jnp.einsum(
@@ -343,40 +452,53 @@
     cotangent,
 ):
     layers = norm_gain.shape[0]
+    grid = Grid()
+    count = grid.count
+    rows = w_gate.shape[1]
+    outer = w_out.shape[1]
+    taps, chans = conv_weight.shape[1:]
+    width = w_xbc.shape[2]
+    small = rows + (taps + 1) * chans + outer
+    small_cols = -(-small // rows)
+    pad = -(HEADS + small_cols) % 128
+    packs = []
+    for l in range(layers):
+        extra = jnp.concatenate(
+            [norm_gain[l], conv_weight[l].reshape(-1), conv_bias[l], gate_gain[l]]
+        )
+        extra = jnp.pad(extra, (0, rows * small_cols - small)).reshape(rows, small_cols)
+        first = jnp.concatenate([w_xbc[l], w_dt[l], extra, jnp.zeros((rows, pad), extra.dtype)], 1)
+        packs.extend([first, w_gate[l], w_out[l]])
+    gathered = gather_weights(grid, packs)
+    wholes = []
+    for l in range(layers):
+        first, gate_w, out_w = (jnp.concatenate(p, axis=1) for p in gathered[3 * l : 3 * l + 3])
+        extra = first[:, width + HEADS : width + HEADS + small_cols].reshape(count, -1)
+        at = rows + taps * chans
+        wholes.append(
+            (
+                extra[:, :rows].reshape(-1),
+                gate_w,
+                first[:, :width],
+                first[:, width : width + HEADS],
+                jnp.moveaxis(extra[:, rows:at].reshape(count, taps, chans), 1, 0).reshape(taps, -1),
+                extra[:, at : at + chans].reshape(-1),
+                extra[:, at + chans : at + chans + outer].reshape(-1),
+                out_w,
+            )
+        )
     hidden = tokens.astype(jnp.float32)
-    kept = []
     saves = []
-    for layer_index in range(layers):
-        whole = (
-            lax.all_gather(norm_gain[layer_index], ("dp", "fsdp"), axis=0, tiled=True),
-            lax.all_gather(w_gate[layer_index], ("dp", "fsdp"), axis=0, tiled=True),
-            lax.all_gather(w_xbc[layer_index], ("dp", "fsdp"), axis=0, tiled=True),
-            lax.all_gather(w_dt[layer_index], ("dp", "fsdp"), axis=0, tiled=True),
-            lax.all_gather(conv_weight[layer_index], ("dp", "fsdp"), axis=1, tiled=True),
-            lax.all_gather(conv_bias[layer_index], ("dp", "fsdp"), axis=0, tiled=True),
-            lax.all_gather(gate_gain[layer_index], ("dp", "fsdp"), axis=0, tiled=True),
-            lax.all_gather(w_out[layer_index], ("dp", "fsdp"), axis=0, tiled=True),
-        )
-        heads = (dt_bias[layer_index], a_log[layer_index], skip_weight[layer_index])
-        hidden, saved = layer_forward(hidden, whole, heads, starts, valid)
-        kept.append(None)
+    for l in range(layers):
+        heads = (dt_bias[l], a_log[l], skip_weight[l])
+        hidden, saved = layer_forward(hidden, wholes[l], heads, starts, valid)
         saves.append(saved)
     grad = cotangent.astype(jnp.float32)
     owned_list = [None] * layers
     summed_list = [None] * layers
-    for layer_index in reversed(range(layers)):
-        whole = (
-            lax.all_gather(norm_gain[layer_index], ("dp", "fsdp"), axis=0, tiled=True),
-            lax.all_gather(w_gate[layer_index], ("dp", "fsdp"), axis=0, tiled=True),
-            lax.all_gather(w_xbc[layer_index], ("dp", "fsdp"), axis=0, tiled=True),
-            lax.all_gather(w_dt[layer_index], ("dp", "fsdp"), axis=0, tiled=True),
-            lax.all_gather(conv_weight[layer_index], ("dp", "fsdp"), axis=1, tiled=True),
-            lax.all_gather(conv_bias[layer_index], ("dp", "fsdp"), axis=0, tiled=True),
-            lax.all_gather(gate_gain[layer_index], ("dp", "fsdp"), axis=0, tiled=True),
-            lax.all_gather(w_out[layer_index], ("dp", "fsdp"), axis=0, tiled=True),
-        )
-        heads = (dt_bias[layer_index], a_log[layer_index], skip_weight[layer_index])
-        grad, weight_grads, head_grads = layer_backward(grad, saves[layer_index], whole, heads)
+    for l in reversed(range(layers)):
+        heads = (dt_bias[l], a_log[l], skip_weight[l])
+        grad, weight_grads, head_grads = layer_backward(grad, saves[l], wholes[l], heads)
         (
             grad_norm_gain,
             grad_w_gate,
@@ -387,18 +509,37 @@
             grad_gate_gain,
             grad_w_out,
         ) = weight_grads
-        grad_dt_bias, grad_a_log, grad_skip = head_grads
-        owned_list[layer_index] = (
-            lax.psum_scatter(grad_norm_gain, ("dp", "fsdp"), scatter_dimension=0, tiled=True),
-            lax.psum_scatter(grad_w_gate, ("dp", "fsdp"), scatter_dimension=0, tiled=True),
-            lax.psum_scatter(grad_w_xbc, ("dp", "fsdp"), scatter_dimension=0, tiled=True),
-            lax.psum_scatter(grad_w_dt, ("dp", "fsdp"), scatter_dimension=0, tiled=True),
-            lax.psum_scatter(grad_conv_weight, ("dp", "fsdp"), scatter_dimension=1, tiled=True),
-            lax.psum_scatter(grad_conv_bias, ("dp", "fsdp"), scatter_dimension=0, tiled=True),
-            lax.psum_scatter(grad_gate_gain, ("dp", "fsdp"), scatter_dimension=0, tiled=True),
-            lax.psum_scatter(grad_w_out, ("dp", "fsdp"), scatter_dimension=0, tiled=True),
+        extra = jnp.concatenate(
+            [
+                grad_norm_gain.reshape(count, rows),
+                jnp.moveaxis(grad_conv_weight.reshape(taps, count, chans), 0, 1).reshape(count, -1),
+                grad_conv_bias.reshape(count, chans),
+                grad_gate_gain.reshape(count, outer),
+                jnp.zeros((count, rows * small_cols - small), jnp.float32),
+            ],
+            axis=1,
+        ).reshape(count * rows, small_cols)
+        first = jnp.concatenate(
+            [grad_w_xbc, grad_w_dt, extra, jnp.zeros((count * rows, pad), jnp.float32)], axis=1
+        ).astype(jnp.bfloat16)
+        out_part = scatter_grads(grid, grad_w_out.astype(jnp.bfloat16))
+        gate_part = scatter_grads(grid, grad_w_gate.astype(jnp.bfloat16))
+        first_part = scatter_grads(grid, first)
+        extra = first_part[:, width + HEADS : width + HEADS + small_cols].reshape(-1)
+        at = rows + taps * chans
+        owned_list[l] = (
+            extra[:rows],
+            gate_part,
+            first_part[:, :width],
+            first_part[:, width : width + HEADS],
+            extra[rows:at].reshape(taps, chans),
+            extra[at : at + chans],
+            extra[at + chans : at + chans + outer],
+            out_part,
         )
-        summed_list[layer_index] = lax.psum((grad_dt_bias, grad_a_log, grad_skip), ("dp", "fsdp"))
+        summed_list[l] = head_grads
+    sums = grid.sum_all(jnp.stack([jnp.stack(s) for s in summed_list]))
+    summed_list = [tuple(sums[l, i] for i in range(3)) for l in range(layers)]
 
     def stacked(position, source):
         return jnp.stack([member[position] for member in source])

time: 1770 us -> 778 us (0.44)
  waiting for transfers between devices: 1100 us -> 133 us
  starting transfers between devices: 19.8 us -> 249 us
  blocking collectives: 213 us -> 0 us
  local copies, waits for them, and re-layouts: 189 us -> 141 us
  other arithmetic: 97.5 us -> 133 us
  matrix products: 128 us -> 101 us
    reduce_scatter x6 -> x0, waiting for transfers between devices: 674 us -> none  [the longest x2 229 us: shards(): lax.psum_scatter(grad_w_xbc, ('dp', 'fsdp'), scatter_dimension=0, tiled=T...]
    unnamed x22 -> x0, waiting for transfers between devices: 289 us -> none
    ppermute x0 -> x161, starting transfers between devices: none -> 241 us  [the longest x72 135 us: hop(): return lax.ppermute(block, AXES, route)]
    all_gather x6 -> x0, blocking collectives: 170 us -> none  [the longest x2 80 us: shards(): lax.all_gather(conv_weight[layer_index], ('dp', 'fsdp'), axis=1, tiled=True)]
    all_gather x10 -> x0, waiting for transfers between devices: 138 us -> none  [the longest x2 54.3 us: shards(): lax.all_gather(w_out[layer_index], ('dp', 'fsdp'), axis=0, tiled=True)]
    ppermute x0 -> x161, waiting for transfers between devices: none -> 133 us  [the longest x72 65 us: hop(): return lax.ppermute(block, AXES, route)]
    slice x2, local copies, waits for them, and re-layouts: 75.7 us -> 0.37 us  [conv_act(): total = bias[None, :] + weight[KCONV - 1][None, :] * extended[KCONV - 1:]]
    unnamed x1 -> x0, blocking collectives: 42.6 us -> none
  transfers between devices with their start and end apart: 23 -> 165, of which waited for: 12 -> 43; matrix products, arithmetic and copies ran while one was open for 15% -> 41% of each run, Pallas kernels for 0% -> 0%
where the time goes in v1:
time: 778 us; the launch traced here: 765 us
  starting transfers between devices  249 us (32%)
  local copies, waits for them, and re-layouts  141 us (18%)
  other arithmetic  133 us (17%)
  waiting for transfers between devices  133 us (17%)
  matrix products  101 us (13%)
  between operations  8.21 us (1%)
    ppermute x72, starting transfers between devices, hop(): return lax.ppermute(block, AXES, route)  135 us
    ppermute x75, starting transfers between devices, swap(): return lax.ppermute(block, AXES, route)  78.5 us
    ppermute x72, waiting for transfers between devices, hop(): return lax.ppermute(block, AXES, route)  65 us
    ppermute x75, waiting for transfers between devices, swap(): return lax.ppermute(block, AXES, route)  63.1 us
    unnamed x648, local copies, waits for them, and re-layouts  21.4 us
    concatenate x36, other arithmetic, gather_step(): return jnp.concatenate([first, second], axis=axis)  20.7 us
    ppermute x12, starting transfers between devices, state_chain(): got = lax.ppermute(leaving.astype(jnp.bfloat16), axis, [(at, at + way)])  15.9 us
  transfers between devices with their start and end apart: 165, of which 43 were waited for; matrix products, arithmetic and copies ran while one was open for 41% of the time, Pallas kernels for 0%

profile of v1, /device:TPU:0, one launch (start us, length us, event | category | flops | bytes accessed | tf_op | source)
XLA Modules:
  0.0 764.9 jit_solution(11165153207783206055)
XLA Ops:
  1.6 4.9 collective-permute-start.16
  12.9 4.5 collective-permute-start
  27.1 7.3 collective-permute-start.17
  44.0 3.9 collective-permute-done.4
  50.2 3.6 collective-permute-start.28
  67.7 4.8 collective-permute-done.33
  77.9 3.7 collective-permute-done.43
  84.3 3.9 collective-permute-done.44
  89.6 5.7 collective-permute-done.45
  100.3 3.5 collective-permute-done.59
  107.2 4.1 collective-permute-done.60
  112.7 5.2 collective-permute-done.61
  128.4 4.2 collective-permute-done.72
  134.1 4.9 collective-permute-done.73
  188.9 3.0 fusion.252
  197.1 3.2 collective-permute-start.13
  217.7 6.5 collective-permute-done.50
  237.9 5.3 collective-permute-done.63
  255.3 3.3 fusion.29
  260.6 4.3 multiply_reduce_fusion.23
  287.7 3.0 fusion.249
  296.2 3.6 collective-permute-start.53
  299.8 3.1 copy.321
  320.9 3.3 fusion.28
  324.2 3.2 copy.322
  327.4 3.0 multiply_reduce_fusion.22
  340.1 5.6 fusion.6
  367.8 4.0 collective-permute-start.156
  385.0 5.2 collective-permute-start.154
  393.8 4.5 collective-permute-start.158
  401.1 3.5 collective-permute-start.129
  414.7 3.2 collective-permute-start.160
  422.7 5.8 collective-permute-start.161
  430.5 5.2 collective-permute-start.132
  447.3 5.3 fusion.27
  452.7 3.1 copy.333
  474.5 3.0 fusion.19
  490.9 6.4 fusion.4
  502.4 5.7 collective-permute-start.144
  541.3 3.5 collective-permute-start.142
  546.6 2.9 collective-permute-start.101
  551.1 5.1 collective-permute-done.142
  559.0 3.5 collective-permute-done.113
  562.7 9.5 %collective-permute-done.146 = bf16[4,1,1,1,48,384]{5,4,3,2,1,0:T(8,128)(2,1)S(1)} collective-permute-done((bf16[4,1,1,1,48,384]{5,4,3,2,1,0:T(8,128)(2,1)S(1)}, bf16[4,1,1,1,48,384]{5,4,3,2,1,0:T(8,128)(2,1)S(1)}, u32[]{:S(2)}, u32[]{:S(2)}) %collective-permute-start.146) | collective-permute-done | bytes 147488 | tf_op jit(solution)/shard_map/ppermute | solution.py:70
  573.8 3.4 collective-permute-start.147
  587.5 4.0 collective-permute-start.119
  593.0 3.2 fusion.26
  596.1 3.0 copy.350
  601.2 5.5 multiply_reduce_fusion.7
  623.5 5.3 concatenate.293
  636.9 7.6 collective-permute-start.139
  650.8 4.2 collective-permute-start.140
  662.4 5.4 collective-permute-start.120
  680.7 4.4 concatenate.287
  689.4 3.9 collective-permute-done.123
  704.3 3.1 collective-permute-done.89
  709.1 4.7 collective-permute-done.104
  715.5 6.7 collective-permute-done.92
  725.6 3.4 collective-permute-start.106
  732.7 3.1 collective-permute-start.107
  736.5 4.7 collective-permute-start.95
  742.0 5.2 collective-permute-start.108
  748.5 5.2 collective-permute-start.96
  755.8 4.3 collective-permute-done.99
  (1426 shorter events, 472.1 us)
Async XLA Ops:
  1.6 25.5 %collective-permute-start.16 = (bf16[1,1,1,1,24,1536]{5,4,3,2,1,0:T(8,128)(2,1)S(1)}, bf16[1,1,1,1,24,1536]{5,4,3,2,1,0:T(8,128)(2,1)S(1)}, u32[]{:S(2)}, u32[]{:S(2)}) collective-permute-start(bf16[1,1,1,1,24,1536]{5,4,3,2,1,0:T(8,128)(2,1)S(1)} %get-tuple-element.71), channel_id=1, source_target_pairs={{0,8},{1,9},{2,10},{3,11},{4,12},{5,13},{6,14},{7,15},{8,16},{9,17... | collective-permute-start | bytes 221192 | tf_op jit(solution)/shard_map/ppermute | solution.py:79
  6.5 28.5 %collective-permute-start.19 = (bf16[1,1,1,1,24,1536]{5,4,3,2,1,0:T(8,128)(2,1)S(1)}, bf16[1,1,1,1,24,1536]{5,4,3,2,1,0:T(8,128)(2,1)S(1)}, u32[]{:S(2)}, u32[]{:S(2)}) collective-permute-start(bf16[1,1,1,1,24,1536]{5,4,3,2,1,0:T(8,128)(2,1)S(1)} %get-tuple-element.71), channel_id=1, source_target_pairs={{8,0},{9,1},{10,2},{11,3},{12,4},{13,5},{14,6},{15,7},{16,8},{17,9... | collective-permute-start | bytes 221192 | tf_op jit(solution)/shard_map/ppermute | solution.py:79
  12.9 23.5 %collective-permute-start = (bf16[1,1,1,1,24,1920]{5,4,3,2,1,0:T(8,128)(2,1)S(1)}, bf16[1,1,1,1,24,1920]{5,4,3,2,1,0:T(8,128)(2,1)S(1)}, u32[]{:S(2)}, u32[]{:S(2)}) collective-permute-start(bf16[1,1,1,1,24,1920]{5,4,3,2,1,0:T(8,128)(2,1)S(1)} %bitcast.573), channel_id=1, source_target_pairs={{0,8},{1,9},{2,10},{3,11},{4,12},{5,13},{6,14},{7,15},{8,16},{9,17... | collective-permute-start | bytes 276488 | tf_op jit(solution)/shard_map/ppermute | solution.py:79
  17.4 19.6 %collective-permute-start.3 = (bf16[1,1,1,1,24,1920]{5,4,3,2,1,0:T(8,128)(2,1)S(1)}, bf16[1,1,1,1,24,1920]{5,4,3,2,1,0:T(8,128)(2,1)S(1)}, u32[]{:S(2)}, u32[]{:S(2)}) collective-permute-start(bf16[1,1,1,1,24,1920]{5,4,3,2,1,0:T(8,128)(2,1)S(1)} %bitcast.574), channel_id=1, source_target_pairs={{8,0},{9,1},{10,2},{11,3},{12,4},{13,5},{14,6},{15,7},{16,8},{17,9... | collective-permute-start | bytes 276488 | tf_op jit(solution)/shard_map/ppermute | solution.py:79
  56.5 19.0 %collective-permute-start.9 = (bf16[4,1,1,1,24,896]{5,4,3,2,1,0:T(8,128)(2,1)S(1)}, bf16[4,1,1,1,24,896]{5,4,3,2,1,0:T(8,128)(2,1)S(1)}, u32[]{:S(2)}, u32[]{:S(2)}) collective-permute-start(bf16[4,1,1,1,24,896]{5,4,3,2,1,0:T(8,128)(2,1)S(1)} %constant_dynamic-slice_fusion), channel_id=1, source_target_pairs={{0,2},{1,3},{2,0},{3,1},{4,6},{5,7},{6,4},{7,5},{8,10},{9,11},{10,... | collective-permute-start | bytes 516104 | tf_op jit(solution)/shard_map/ppermute | solution.py:70
  62.1 15.7 %collective-permute-start.6 = (bf16[4,1,1,1,24,1024]{5,4,3,2,1,0:T(8,128)(2,1)S(1)}, bf16[4,1,1,1,24,1024]{5,4,3,2,1,0:T(8,128)(2,1)S(1)}, u32[]{:S(2)}, u32[]{:S(2)}) collective-permute-start(bf16[4,1,1,1,24,1024]{5,4,3,2,1,0:T(8,128)(2,1)S(1)} %constant_dynamic-slice_fusion.1), channel_id=1, source_target_pairs={{0,4},{1,5},{2,6},{3,7},{4,0},{5,1},{6,2},{7,3},{8,12},{9,13},{10,... | collective-permute-start | bytes 589832 | tf_op jit(solution)/shard_map/ppermute | solution.py:70
  75.6 23.2 %collective-permute-start.10 = (bf16[4,1,2,1,24,896]{5,4,3,2,1,0:T(8,128)(2,1)S(1)}, bf16[4,1,2,1,24,896]{5,4,3,2,1,0:T(8,128)(2,1)S(1)}, u32[]{:S(2)}, u32[]{:S(2)}) collective-permute-start(bf16[4,1,2,1,24,896]{5,4,3,2,1,0:T(8,128)(2,1)S(1)} %pad_maximum_fusion.54), channel_id=1, source_target_pairs={{0,4},{1,5},{2,6},{3,7},{4,0},{5,1},{6,2},{7,3},{8,12},{9,13},{10,... | collective-permute-start | bytes 1032200 | tf_op jit(solution)/shard_map/ppermute | solution.py:70
  83.6 22.8 %collective-permute-start.7 = (bf16[4,2,1,1,24,1024]{5,4,3,2,1,0:T(8,128)(2,1)S(1)}, bf16[4,2,1,1,24,1024]{5,4,3,2,1,0:T(8,128)(2,1)S(1)}, u32[]{:S(2)}, u32[]{:S(2)}) collective-permute-start(bf16[4,2,1,1,24,1024]{5,4,3,2,1,0:T(8,128)(2,1)S(1)} %pad_maximum_fusion.52), channel_id=1, source_target_pairs={{0,2},{1,3},{2,0},{3,1},{4,6},{5,7},{6,4},{7,5},{8,10},{9,11},{10,... | collective-permute-start | bytes 1179656 | tf_op jit(solution)/shard_map/ppermute | solution.py:70
  99.0 52.1 %collective-permute-start.11 = (bf16[4,2,2,1,24,896]{5,4,3,2,1,0:T(8,128)(2,1)S(1)}, bf16[4,2,2,1,24,896]{5,4,3,2,1,0:T(8,128)(2,1)S(1)}, u32[]{:S(2)}, u32[]{:S(2)}) collective-permute-start(bf16[4,2,2,1,24,896]{5,4,3,2,1,0:T(8,128)(2,1)S(1)} %pad_maximum_fusion.42), channel_id=1, source_target_pairs={{0,1},{1,0},{2,3},{3,2},{4,5},{5,4},{6,7},{7,6},{8,9},{9,8},{10,11... | collective-permute-start | bytes 2064392 | tf_op jit(solution)/shard_map/ppermute | solution.py:70
  100.2 19.9 %collective-permute-start.22 = (bf16[4,1,1,1,24,768]{5,4,3,2,1,0:T(8,128)(2,1)S(1)}, bf16[4,1,1,1,24,768]{5,4,3,2,1,0:T(8,128)(2,1)S(1)}, u32[]{:S(2)}, u32[]{:S(2)}) collective-permute-start(bf16[4,1,1,1,24,768]{5,4,3,2,1,0:T(8,128)(2,1)S(1)} %get-tuple-element.291), channel_id=1, source_target_pairs={{0,2},{1,3},{2,0},{3,1},{4,6},{5,7},{6,4},{7,5},{8,10},{9,11},{10,... | collective-permute-start | bytes 442376 | tf_op jit(solution)/shard_map/ppermute | solution.py:70
  103.8 17.7 %collective-permute-start.25 = (bf16[4,1,1,1,24,768]{5,4,3,2,1,0:T(8,128)(2,1)S(1)}, bf16[4,1,1,1,24,768]{5,4,3,2,1,0:T(8,128)(2,1)S(1)}, u32[]{:S(2)}, u32[]{:S(2)}) collective-permute-start(bf16[4,1,1,1,24,768]{5,4,3,2,1,0:T(8,128)(2,1)S(1)} %get-tuple-element.290), channel_id=1, source_target_pairs={{0,4},{1,5},{2,6},{3,7},{4,0},{5,1},{6,2},{7,3},{8,12},{9,13},{10,... | collective-permute-start | bytes 442376 | tf_op jit(solution)/shard_map/ppermute | solution.py:70
  111.3 40.5 %collective-permute-start.8 = (bf16[4,2,2,1,24,1024]{5,4,3,2,1,0:T(8,128)(2,1)S(1)}, bf16[4,2,2,1,24,1024]{5,4,3,2,1,0:T(8,128)(2,1)S(1)}, u32[]{:S(2)}, u32[]{:S(2)}) collective-permute-start(bf16[4,2,2,1,24,1024]{5,4,3,2,1,0:T(8,128)(2,1)S(1)} %pad_maximum_fusion.40), channel_id=1, source_target_pairs={{0,1},{1,0},{2,3},{3,2},{4,5},{5,4},{6,7},{7,6},{8,9},{9,8},{10,11... | collective-permute-start | bytes 2359304 | tf_op jit(solution)/shard_map/ppermute | solution.py:70
  122.8 16.9 %collective-permute-start.23 = (bf16[4,1,2,1,24,768]{5,4,3,2,1,0:T(8,128)(2,1)S(1)}, bf16[4,1,2,1,24,768]{5,4,3,2,1,0:T(8,128)(2,1)S(1)}, u32[]{:S(2)}, u32[]{:S(2)}) collective-permute-start(bf16[4,1,2,1,24,768]{5,4,3,2,1,0:T(8,128)(2,1)S(1)} %pad_maximum_fusion.57), channel_id=1, source_target_pairs={{0,4},{1,5},{2,6},{3,7},{4,0},{5,1},{6,2},{7,3},{8,12},{9,13},{10,... | collective-permute-start | bytes 884744 | tf_op jit(solution)/shard_map/ppermute | solution.py:70
  140.7 66.8 %collective-permute-start.24 = (bf16[4,2,2,1,24,768]{5,4,3,2,1,0:T(8,128)(2,1)}, bf16[4,2,2,1,24,768]{5,4,3,2,1,0:T(8,128)(2,1)}, u32[]{:S(2)}, u32[]{:S(2)}) collective-permute-start(bf16[4,2,2,1,24,768]{5,4,3,2,1,0:T(8,128)(2,1)} %pad_maximum_fusion.44), channel_id=1, source_target_pairs={{0,1},{1,0},{2,3},{3,2},{4,5},{5,4},{6,7},{7,6},{8,9},{9,8},{10,11... | collective-permute-start | bytes 1769480 | tf_op jit(solution)/shard_map/ppermute | solution.py:70
  147.3 62.8 %collective-permute-start.27 = (bf16[4,2,2,1,24,768]{5,4,3,2,1,0:T(8,128)(2,1)}, bf16[4,2,2,1,24,768]{5,4,3,2,1,0:T(8,128)(2,1)}, u32[]{:S(2)}, u32[]{:S(2)}) collective-permute-start(bf16[4,2,2,1,24,768]{5,4,3,2,1,0:T(8,128)(2,1)} %pad_maximum_fusion.45), channel_id=1, source_target_pairs={{0,1},{1,0},{2,3},{3,2},{4,5},{5,4},{6,7},{7,6},{8,9},{9,8},{10,11... | collective-permute-start | bytes 1769480 | tf_op jit(solution)/shard_map/ppermute | solution.py:70
  149.7 55.2 %collective-permute-start.35 = (bf16[4,1,2,1,48,384]{5,4,3,2,1,0:T(8,128)(2,1)}, bf16[4,1,2,1,48,384]{5,4,3,2,1,0:T(8,128)(2,1)}, u32[]{:S(2)}, u32[]{:S(2)}) collective-permute-start(bf16[4,1,2,1,48,384]{5,4,3,2,1,0:T(8,128)(2,1)} %pad_maximum_fusion.59), channel_id=1, source_target_pairs={{0,4},{1,5},{2,6},{3,7},{4,0},{5,1},{6,2},{7,3},{8,12},{9,13},{10,... | collective-permute-start | bytes 884744 | tf_op jit(solution)/shard_map/ppermute | solution.py:70
  151.1 55.1 %collective-permute-start.38 = (bf16[4,2,1,1,48,384]{5,4,3,2,1,0:T(8,128)(2,1)}, bf16[4,2,1,1,48,384]{5,4,3,2,1,0:T(8,128)(2,1)}, u32[]{:S(2)}, u32[]{:S(2)}) collective-permute-start(bf16[4,2,1,1,48,384]{5,4,3,2,1,0:T(8,128)(2,1)} %pad_maximum_fusion.60), channel_id=1, source_target_pairs={{0,2},{1,3},{2,0},{3,1},{4,6},{5,7},{6,4},{7,5},{8,10},{9,11},{10,... | collective-permute-start | bytes 884744 | tf_op jit(solution)/shard_map/ppermute | solution.py:70
  167.4 19.9 %collective-permute-start.12 = (bf16[3,1792]{1,0:T(4,128)(2,1)}, bf16[3,1792]{1,0:T(4,128)(2,1)}, u32[]{:S(2)}, u32[]{:S(2)}) collective-permute-start(bf16[3,1792]{1,0:T(4,128)(2,1)} %slice.603), channel_id=1, source_target_pairs={{0,1},{1,2},{2,3},{4,5},{5,6},{6,7},{8,9},{9,10},{10,11},{12,13},{... | collective-permute-start | bytes 32264 | tf_op jit(solution)/shard_map/ppermute | solution.py:22
  197.1 19.6 %collective-permute-start.13 = (bf16[24,64,128]{2,1,0:T(8,128)(2,1)}, bf16[24,64,128]{2,1,0:T(8,128)(2,1)S(1)}, u32[]{:S(2)}, u32[]{:S(2)}) collective-permute-start(bf16[24,64,128]{2,1,0:T(8,128)(2,1)} %get-tuple-element.340), channel_id=1, source_target_pairs={{0,1},{4,5},{8,9},{12,13},{16,17},{20,21},{24,25},{28,29}} | collective-permute-start | bytes 1179656 | tf_op jit(solution)/shard_map/ppermute | solution.py:208
  206.2 23.5 %collective-permute-start.36 = (bf16[4,2,2,1,48,384]{5,4,3,2,1,0:T(8,128)(2,1)S(1)}, bf16[4,2,2,1,48,384]{5,4,3,2,1,0:T(8,128)(2,1)S(1)}, u32[]{:S(2)}, u32[]{:S(2)}) collective-permute-start(bf16[4,2,2,1,48,384]{5,4,3,2,1,0:T(8,128)(2,1)S(1)} %pad_maximum_fusion.46), channel_id=1, source_target_pairs={{0,1},{1,0},{2,3},{3,2},{4,5},{5,4},{6,7},{7,6},{8,9},{9,8},{10,11... | collective-permute-start | bytes 1769480 | tf_op jit(solution)/shard_map/ppermute | solution.py:70
  210.1 21.1 %collective-permute-start.39 = (bf16[4,2,2,1,48,384]{5,4,3,2,1,0:T(8,128)(2,1)S(1)}, bf16[4,2,2,1,48,384]{5,4,3,2,1,0:T(8,128)(2,1)S(1)}, u32[]{:S(2)}, u32[]{:S(2)}) collective-permute-start(bf16[4,2,2,1,48,384]{5,4,3,2,1,0:T(8,128)(2,1)S(1)} %pad_maximum_fusion.47), channel_id=1, source_target_pairs={{0,1},{1,0},{2,3},{3,2},{4,5},{5,4},{6,7},{7,6},{8,9},{9,8},{10,11... | collective-permute-start | bytes 1769480 | tf_op jit(solution)/shard_map/ppermute | solution.py:70
  216.9 20.0 %collective-permute-start.14 = (bf16[24,64,128]{2,1,0:T(8,128)(2,1)S(1)}, bf16[24,64,128]{2,1,0:T(8,128)(2,1)S(1)}, u32[]{:S(2)}, u32[]{:S(2)}) collective-permute-start(bf16[24,64,128]{2,1,0:T(8,128)(2,1)S(1)} %fusion.49), channel_id=1, source_target_pairs={{1,2},{5,6},{9,10},{13,14},{17,18},{21,22},{25,26},{29,30}} | collective-permute-start | bytes 1179656 | tf_op jit(solution)/shard_map/ppermute | solution.py:208
  225.5 40.6 %collective-permute-start.51 = (bf16[4,2,2,1,24,896]{5,4,3,2,1,0:T(8,128)(2,1)}, bf16[4,2,2,1,24,896]{5,4,3,2,1,0:T(8,128)(2,1)}, u32[]{:S(2)}, u32[]{:S(2)}) collective-permute-start(bf16[4,2,2,1,24,896]{5,4,3,2,1,0:T(8,128)(2,1)} %pad_maximum_fusion.43), channel_id=1, source_target_pairs={{0,1},{1,0},{2,3},{3,2},{4,5},{5,4},{6,7},{7,6},{8,9},{9,8},{10,11... | collective-permute-start | bytes 2064392 | tf_op jit(solution)/shard_map/ppermute | solution.py:70
  231.2 38.0 %collective-permute-start.48 = (bf16[4,2,2,1,24,1024]{5,4,3,2,1,0:T(8,128)(2,1)}, bf16[4,2,2,1,24,1024]{5,4,3,2,1,0:T(8,128)(2,1)}, u32[]{:S(2)}, u32[]{:S(2)}) collective-permute-start(bf16[4,2,2,1,24,1024]{5,4,3,2,1,0:T(8,128)(2,1)} %pad_maximum_fusion.41), channel_id=1, source_target_pairs={{0,1},{1,0},{2,3},{3,2},{4,5},{5,4},{6,7},{7,6},{8,9},{9,8},{10,11... | collective-permute-start | bytes 2359304 | tf_op jit(solution)/shard_map/ppermute | solution.py:70
  237.0 15.2 %collective-permute-start.15 = (bf16[24,64,128]{2,1,0:T(8,128)(2,1)S(1)}, bf16[24,64,128]{2,1,0:T(8,128)(2,1)S(1)}, u32[]{:S(2)}, u32[]{:S(2)}) collective-permute-start(bf16[24,64,128]{2,1,0:T(8,128)(2,1)S(1)} %add_convert_fusion.16), channel_id=1, source_target_pairs={{2,3},{6,7},{10,11},{14,15},{18,19},{22,23},{26,27},{30,31}} | collective-permute-start | bytes 1179656 | tf_op jit(solution)/shard_map/ppermute | solution.py:208
  249.6 59.9 %collective-permute-start.64 = (bf16[4,2,2,1,24,768]{5,4,3,2,1,0:T(8,128)(2,1)}, bf16[4,2,2,1,24,768]{5,4,3,2,1,0:T(8,128)(2,1)}, u32[]{:S(2)}, u32[]{:S(2)}) collective-permute-start(bf16[4,2,2,1,24,768]{5,4,3,2,1,0:T(8,128)(2,1)} %pad_maximum_fusion.48), channel_id=1, source_target_pairs={{0,1},{1,0},{2,3},{3,2},{4,5},{5,4},{6,7},{7,6},{8,9},{9,8},{10,11... | collective-permute-start | bytes 1769480 | tf_op jit(solution)/shard_map/ppermute | solution.py:70
  250.5 60.1 %collective-permute-start.67 = (bf16[4,2,2,1,24,768]{5,4,3,2,1,0:T(8,128)(2,1)}, bf16[4,2,2,1,24,768]{5,4,3,2,1,0:T(8,128)(2,1)}, u32[]{:S(2)}, u32[]{:S(2)}) collective-permute-start(bf16[4,2,2,1,24,768]{5,4,3,2,1,0:T(8,128)(2,1)} %pad_maximum_fusion.49), channel_id=1, source_target_pairs={{0,1},{1,0},{2,3},{3,2},{4,5},{5,4},{6,7},{7,6},{8,9},{9,8},{10,11... | collective-permute-start | bytes 1769480 | tf_op jit(solution)/shard_map/ppermute | solution.py:70
  252.3 54.0 %collective-permute-start.75 = (bf16[4,1,2,1,48,384]{5,4,3,2,1,0:T(8,128)(2,1)}, bf16[4,1,2,1,48,384]{5,4,3,2,1,0:T(8,128)(2,1)}, u32[]{:S(2)}, u32[]{:S(2)}) collective-permute-start(bf16[4,1,2,1,48,384]{5,4,3,2,1,0:T(8,128)(2,1)} %pad_maximum_fusion.63), channel_id=1, source_target_pairs={{0,4},{1,5},{2,6},{3,7},{4,0},{5,1},{6,2},{7,3},{8,12},{9,13},{10,... | collective-permute-start | bytes 884744 | tf_op jit(solution)/shard_map/ppermute | solution.py:70
  266.1 41.6 %collective-permute-start.78 = (bf16[4,2,1,1,48,384]{5,4,3,2,1,0:T(8,128)(2,1)}, bf16[4,2,1,1,48,384]{5,4,3,2,1,0:T(8,128)(2,1)}, u32[]{:S(2)}, u32[]{:S(2)}) collective-permute-start(bf16[4,2,1,1,48,384]{5,4,3,2,1,0:T(8,128)(2,1)} %pad_maximum_fusion.64), channel_id=1, source_target_pairs={{0,2},{1,3},{2,0},{3,1},{4,6},{5,7},{6,4},{7,5},{8,10},{9,11},{10,... | collective-permute-start | bytes 884744 | tf_op jit(solution)/shard_map/ppermute | solution.py:70
  296.2 17.9 %collective-permute-start.53 = (bf16[24,64,128]{2,1,0:T(8,128)(2,1)}, bf16[24,64,128]{2,1,0:T(8,128)(2,1)S(1)}, u32[]{:S(2)}, u32[]{:S(2)}) collective-permute-start(bf16[24,64,128]{2,1,0:T(8,128)(2,1)} %get-tuple-element.345), channel_id=1, source_target_pairs={{0,1},{4,5},{8,9},{12,13},{16,17},{20,21},{24,25},{28,29}} | collective-permute-start | bytes 1179656 | tf_op jit(solution)/shard_map/ppermute | solution.py:208
  355.1 25.3 %collective-permute-start.80 = (bf16[24,64,128]{2,1,0:T(8,128)(2,1)}, bf16[24,64,128]{2,1,0:T(8,128)(2,1)S(1)}, u32[]{:S(2)}, u32[]{:S(2)}) collective-permute-start(bf16[24,64,128]{2,1,0:T(8,128)(2,1)} %get-tuple-element.349), channel_id=1, source_target_pairs={{3,2},{7,6},{11,10},{15,14},{19,18},{23,22},{27,26},{31,30}} | collective-permute-start | bytes 1179656 | tf_op jit(solution)/shard_map/ppermute | solution.py:208
  367.8 13.7 %collective-permute-start.156 = (bf16[4,2,2,1,48,384]{5,4,3,2,1,0:T(8,128)(2,1)}, bf16[4,2,2,1,48,384]{5,4,3,2,1,0:T(8,128)(2,1)}, u32[]{:S(2)}, u32[]{:S(2)}) collective-permute-start(bf16[4,2,2,1,48,384]{5,4,3,2,1,0:T(8,128)(2,1)} %constant_dynamic-slice_fusion.4), channel_id=1, source_target_pairs={{0,1},{1,0},{2,3},{3,2},{4,5},{5,4},{6,7},{7,6},{8,9},{9,8},{10,11... | collective-permute-start | bytes 1769480 | tf_op jit(solution)/shard_map/ppermute | solution.py:70
  376.6 13.6 %collective-permute-start.127 = (bf16[4,2,2,1,24,768]{5,4,3,2,1,0:T(8,128)(2,1)S(1)}, bf16[4,2,2,1,24,768]{5,4,3,2,1,0:T(8,128)(2,1)S(1)}, u32[]{:S(2)}, u32[]{:S(2)}) collective-permute-start(bf16[4,2,2,1,24,768]{5,4,3,2,1,0:T(8,128)(2,1)S(1)} %constant_dynamic-slice_fusion.16), channel_id=1, source_target_pairs={{0,1},{1,0},{2,3},{3,2},{4,5},{5,4},{6,7},{7,6},{8,9},{9,8},{10,11... | collective-permute-start | bytes 1769480 | tf_op jit(solution)/shard_map/ppermute | solution.py:70
  377.0 14.8 %collective-permute-start.124 = (bf16[4,2,2,1,24,768]{5,4,3,2,1,0:T(8,128)(2,1)S(1)}, bf16[4,2,2,1,24,768]{5,4,3,2,1,0:T(8,128)(2,1)S(1)}, u32[]{:S(2)}, u32[]{:S(2)}) collective-permute-start(bf16[4,2,2,1,24,768]{5,4,3,2,1,0:T(8,128)(2,1)S(1)} %constant_dynamic-slice_fusion.19), channel_id=1, source_target_pairs={{0,1},{1,0},{2,3},{3,2},{4,5},{5,4},{6,7},{7,6},{8,9},{9,8},{10,11... | collective-permute-start | bytes 1769480 | tf_op jit(solution)/shard_map/ppermute | solution.py:70
  385.0 15.7 %collective-permute-start.154 = (bf16[4,2,1,1,48,384]{5,4,3,2,1,0:T(8,128)(2,1)S(1)}, bf16[4,2,1,1,48,384]{5,4,3,2,1,0:T(8,128)(2,1)S(1)}, u32[]{:S(2)}, u32[]{:S(2)}) collective-permute-start(bf16[4,2,1,1,48,384]{5,4,3,2,1,0:T(8,128)(2,1)S(1)} %constant_dynamic-slice_fusion.6), channel_id=1, source_target_pairs={{0,2},{1,3},{2,0},{3,1},{4,6},{5,7},{6,4},{7,5},{8,10},{9,11},{10,... | collective-permute-start | bytes 884744 | tf_op jit(solution)/shard_map/ppermute | solution.py:70
  392.0 15.0 %collective-permute-start.125 = (bf16[4,2,1,1,24,768]{5,4,3,2,1,0:T(8,128)(2,1)S(1)}, bf16[4,2,1,1,24,768]{5,4,3,2,1,0:T(8,128)(2,1)S(1)}, u32[]{:S(2)}, u32[]{:S(2)}) collective-permute-start(bf16[4,2,1,1,24,768]{5,4,3,2,1,0:T(8,128)(2,1)S(1)} %constant_dynamic-slice_fusion.18), channel_id=1, source_target_pairs={{0,2},{1,3},{2,0},{3,1},{4,6},{5,7},{6,4},{7,5},{8,10},{9,11},{10,... | collective-permute-start | bytes 884744 | tf_op jit(solution)/shard_map/ppermute | solution.py:70
  392.4 44.8 %collective-permute-start.82 = (bf16[24,64,128]{2,1,0:T(8,128)(2,1)S(1)}, bf16[24,64,128]{2,1,0:T(8,128)(2,1)S(1)}, u32[]{:S(2)}, u32[]{:S(2)}) collective-permute-start(bf16[24,64,128]{2,1,0:T(8,128)(2,1)S(1)} %multiply_convert_fusion.22), channel_id=1, source_target_pairs={{1,0},{5,4},{9,8},{13,12},{17,16},{21,20},{25,24},{29,28}} | collective-permute-start | bytes 1179656 | tf_op jit(solution)/shard_map/ppermute | solution.py:208
  393.8 16.1 %collective-permute-start.158 = (bf16[4,1,1,1,48,384]{5,4,3,2,1,0:T(8,128)(2,1)S(1)}, bf16[4,1,1,1,48,384]{5,4,3,2,1,0:T(8,128)(2,1)S(1)}, u32[]{:S(2)}, u32[]{:S(2)}) collective-permute-start(bf16[4,1,1,1,48,384]{5,4,3,2,1,0:T(8,128)(2,1)S(1)} %constant_dynamic-slice_fusion.2), channel_id=1, source_target_pairs={{0,2},{1,3},{2,0},{3,1},{4,6},{5,7},{6,4},{7,5},{8,10},{9,11},{10,... | collective-permute-start | bytes 442376 | tf_op jit(solution)/shard_map/ppermute | solution.py:70
  422.7 111.8 %collective-permute-start.161 = (bf16[1,1,1,1,48,768]{5,4,3,2,1,0:T(8,128)(2,1)}, bf16[1,1,1,1,48,768]{5,4,3,2,1,0:T(8,128)(2,1)}, u32[]{:S(2)}, u32[]{:S(2)}) collective-permute-start(bf16[1,1,1,1,48,768]{5,4,3,2,1,0:T(8,128)(2,1)} %get-tuple-element.262), channel_id=1, source_target_pairs={{0,8},{1,9},{2,10},{3,11},{4,12},{5,13},{6,14},{7,15},{8,16},{9,17... | collective-permute-start | bytes 221192 | tf_op jit(solution)/shard_map/ppermute | solution.py:79
  428.5 106.2 %collective-permute-start.164 = (bf16[1,1,1,1,48,768]{5,4,3,2,1,0:T(8,128)(2,1)}, bf16[1,1,1,1,48,768]{5,4,3,2,1,0:T(8,128)(2,1)}, u32[]{:S(2)}, u32[]{:S(2)}) collective-permute-start(bf16[1,1,1,1,48,768]{5,4,3,2,1,0:T(8,128)(2,1)} %get-tuple-element.263), channel_id=1, source_target_pairs={{8,0},{9,1},{10,2},{11,3},{12,4},{13,5},{14,6},{15,7},{16,8},{17,9... | collective-permute-start | bytes 221192 | tf_op jit(solution)/shard_map/ppermute | solution.py:79
  430.5 100.5 %collective-permute-start.132 = (bf16[1,1,1,1,24,1536]{5,4,3,2,1,0:T(8,128)(2,1)}, bf16[1,1,1,1,24,1536]{5,4,3,2,1,0:T(8,128)(2,1)}, u32[]{:S(2)}, u32[]{:S(2)}) collective-permute-start(bf16[1,1,1,1,24,1536]{5,4,3,2,1,0:T(8,128)(2,1)} %get-tuple-element.274), channel_id=1, source_target_pairs={{0,8},{1,9},{2,10},{3,11},{4,12},{5,13},{6,14},{7,15},{8,16},{9,17... | collective-permute-start | bytes 221192 | tf_op jit(solution)/shard_map/ppermute | solution.py:79
  435.7 96.5 %collective-permute-start.135 = (bf16[1,1,1,1,24,1536]{5,4,3,2,1,0:T(8,128)(2,1)}, bf16[1,1,1,1,24,1536]{5,4,3,2,1,0:T(8,128)(2,1)}, u32[]{:S(2)}, u32[]{:S(2)}) collective-permute-start(bf16[1,1,1,1,24,1536]{5,4,3,2,1,0:T(8,128)(2,1)} %get-tuple-element.275), channel_id=1, source_target_pairs={{8,0},{9,1},{10,2},{11,3},{12,4},{13,5},{14,6},{15,7},{16,8},{17,9... | collective-permute-start | bytes 221192 | tf_op jit(solution)/shard_map/ppermute | solution.py:79
  502.4 34.6 %collective-permute-start.144 = (bf16[4,2,2,1,48,384]{5,4,3,2,1,0:T(8,128)(2,1)}, bf16[4,2,2,1,48,384]{5,4,3,2,1,0:T(8,128)(2,1)}, u32[]{:S(2)}, u32[]{:S(2)}) collective-permute-start(bf16[4,2,2,1,48,384]{5,4,3,2,1,0:T(8,128)(2,1)} %constant_dynamic-slice_fusion.10), channel_id=1, source_target_pairs={{0,1},{1,0},{2,3},{3,2},{4,5},{5,4},{6,7},{7,6},{8,9},{9,8},{10,11... | collective-permute-start | bytes 1769480 | tf_op jit(solution)/shard_map/ppermute | solution.py:70
  541.3 15.0 %collective-permute-start.142 = (bf16[4,2,1,1,48,384]{5,4,3,2,1,0:T(8,128)(2,1)S(1)}, bf16[4,2,1,1,48,384]{5,4,3,2,1,0:T(8,128)(2,1)S(1)}, u32[]{:S(2)}, u32[]{:S(2)}) collective-permute-start(bf16[4,2,1,1,48,384]{5,4,3,2,1,0:T(8,128)(2,1)S(1)} %constant_dynamic-slice_fusion.12), channel_id=1, source_target_pairs={{0,2},{1,3},{2,0},{3,1},{4,6},{5,7},{6,4},{7,5},{8,10},{9,11},{10,... | collective-permute-start | bytes 884744 | tf_op jit(solution)/shard_map/ppermute | solution.py:70
  545.9 16.7 %collective-permute-start.113 = (bf16[4,2,1,1,24,768]{5,4,3,2,1,0:T(8,128)(2,1)S(1)}, bf16[4,2,1,1,24,768]{5,4,3,2,1,0:T(8,128)(2,1)S(1)}, u32[]{:S(2)}, u32[]{:S(2)}) collective-permute-start(bf16[4,2,1,1,24,768]{5,4,3,2,1,0:T(8,128)(2,1)S(1)} %constant_dynamic-slice_fusion.24), channel_id=1, source_target_pairs={{0,2},{1,3},{2,0},{3,1},{4,6},{5,7},{6,4},{7,5},{8,10},{9,11},{10,... | collective-permute-start | bytes 884744 | tf_op jit(solution)/shard_map/ppermute | solution.py:70
  546.6 30.6 %collective-permute-start.101 = (bf16[4,2,1,1,24,896]{5,4,3,2,1,0:T(8,128)(2,1)S(1)}, bf16[4,2,1,1,24,896]{5,4,3,2,1,0:T(8,128)(2,1)S(1)}, u32[]{:S(2)}, u32[]{:S(2)}) collective-permute-start(bf16[4,2,1,1,24,896]{5,4,3,2,1,0:T(8,128)(2,1)S(1)} %constant_dynamic-slice_fusion.30), channel_id=1, source_target_pairs={{0,2},{1,3},{2,0},{3,1},{4,6},{5,7},{6,4},{7,5},{8,10},{9,11},{10,... | collective-permute-start | bytes 1032200 | tf_op jit(solution)/shard_map/ppermute | solution.py:70
  549.7 41.8 %collective-permute-start.86 = (bf16[24,64,128]{2,1,0:T(8,128)(2,1)S(1)}, bf16[24,64,128]{2,1,0:T(8,128)(2,1)S(1)}, u32[]{:S(2)}, u32[]{:S(2)}) collective-permute-start(bf16[24,64,128]{2,1,0:T(8,128)(2,1)S(1)} %multiply_convert_fusion.20), channel_id=1, source_target_pairs={{1,0},{5,4},{9,8},{13,12},{17,16},{21,20},{25,24},{29,28}} | collective-permute-start | bytes 1179656 | tf_op jit(solution)/shard_map/ppermute | solution.py:208
  556.2 16.0 %collective-permute-start.146 = (bf16[4,1,1,1,48,384]{5,4,3,2,1,0:T(8,128)(2,1)S(1)}, bf16[4,1,1,1,48,384]{5,4,3,2,1,0:T(8,128)(2,1)S(1)}, u32[]{:S(2)}, u32[]{:S(2)}) collective-permute-start(bf16[4,1,1,1,48,384]{5,4,3,2,1,0:T(8,128)(2,1)S(1)} %constant_dynamic-slice_fusion.8), channel_id=1, source_target_pairs={{0,2},{1,3},{2,0},{3,1},{4,6},{5,7},{6,4},{7,5},{8,10},{9,11},{10,... | collective-permute-start | bytes 442376 | tf_op jit(solution)/shard_map/ppermute | solution.py:70
  556.4 17.4 %collective-permute-start.143 = (bf16[4,1,1,1,48,384]{5,4,3,2,1,0:T(8,128)(2,1)S(1)}, bf16[4,1,1,1,48,384]{5,4,3,2,1,0:T(8,128)(2,1)S(1)}, u32[]{:S(2)}, u32[]{:S(2)}) collective-permute-start(bf16[4,1,1,1,48,384]{5,4,3,2,1,0:T(8,128)(2,1)S(1)} %constant_dynamic-slice_fusion.11), channel_id=1, source_target_pairs={{0,4},{1,5},{2,6},{3,7},{4,0},{5,1},{6,2},{7,3},{8,12},{9,13},{10,... | collective-permute-start | bytes 442376 | tf_op jit(solution)/shard_map/ppermute | solution.py:70
  562.6 16.3 %collective-permute-start.117 = (bf16[4,1,1,1,24,768]{5,4,3,2,1,0:T(8,128)(2,1)S(1)}, bf16[4,1,1,1,24,768]{5,4,3,2,1,0:T(8,128)(2,1)S(1)}, u32[]{:S(2)}, u32[]{:S(2)}) collective-permute-start(bf16[4,1,1,1,24,768]{5,4,3,2,1,0:T(8,128)(2,1)S(1)} %constant_dynamic-slice_fusion.20), channel_id=1, source_target_pairs={{0,2},{1,3},{2,0},{3,1},{4,6},{5,7},{6,4},{7,5},{8,10},{9,11},{10,... | collective-permute-start | bytes 442376 | tf_op jit(solution)/shard_map/ppermute | solution.py:70
  578.9 108.0 %collective-permute-start.102 = (bf16[4,1,1,1,24,896]{5,4,3,2,1,0:T(8,128)(2,1)}, bf16[4,1,1,1,24,896]{5,4,3,2,1,0:T(8,128)(2,1)}, u32[]{:S(2)}, u32[]{:S(2)}) collective-permute-start(bf16[4,1,1,1,24,896]{5,4,3,2,1,0:T(8,128)(2,1)} %constant_dynamic-slice_fusion.29), channel_id=1, source_target_pairs={{0,4},{1,5},{2,6},{3,7},{4,0},{5,1},{6,2},{7,3},{8,12},{9,13},{10,... | collective-permute-start | bytes 516104 | tf_op jit(solution)/shard_map/ppermute | solution.py:70
  582.7 52.9 %collective-permute-start.148 = (bf16[1,1,1,1,48,768]{5,4,3,2,1,0:T(8,128)(2,1)}, bf16[1,1,1,1,48,768]{5,4,3,2,1,0:T(8,128)(2,1)}, u32[]{:S(2)}, u32[]{:S(2)}) collective-permute-start(bf16[1,1,1,1,48,768]{5,4,3,2,1,0:T(8,128)(2,1)} %get-tuple-element.258), channel_id=1, source_target_pairs={{0,8},{1,9},{2,10},{3,11},{4,12},{5,13},{6,14},{7,15},{8,16},{9,17... | collective-permute-start | bytes 221192 | tf_op jit(solution)/shard_map/ppermute | solution.py:79
  585.5 51.5 %collective-permute-start.151 = (bf16[1,1,1,1,48,768]{5,4,3,2,1,0:T(8,128)(2,1)}, bf16[1,1,1,1,48,768]{5,4,3,2,1,0:T(8,128)(2,1)}, u32[]{:S(2)}, u32[]{:S(2)}) collective-permute-start(bf16[1,1,1,1,48,768]{5,4,3,2,1,0:T(8,128)(2,1)} %get-tuple-element.259), channel_id=1, source_target_pairs={{16,8},{17,9},{18,10},{19,11},{20,12},{21,13},{22,14},{23,15},{24,... | collective-permute-start | bytes 221192 | tf_op jit(solution)/shard_map/ppermute | solution.py:79
  587.5 60.5 %collective-permute-start.119 = (bf16[1,1,1,1,24,1536]{5,4,3,2,1,0:T(8,128)(2,1)}, bf16[1,1,1,1,24,1536]{5,4,3,2,1,0:T(8,128)(2,1)}, u32[]{:S(2)}, u32[]{:S(2)}) collective-permute-start(bf16[1,1,1,1,24,1536]{5,4,3,2,1,0:T(8,128)(2,1)} %get-tuple-element.270), channel_id=1, source_target_pairs={{0,8},{1,9},{2,10},{3,11},{4,12},{5,13},{6,14},{7,15},{8,16},{9,17... | collective-permute-start | bytes 221192 | tf_op jit(solution)/shard_map/ppermute | solution.py:79
  634.9 15.8 %collective-permute-start.122 = (bf16[1,1,1,1,24,1536]{5,4,3,2,1,0:T(8,128)(2,1)S(1)}, bf16[1,1,1,1,24,1536]{5,4,3,2,1,0:T(8,128)(2,1)S(1)}, u32[]{:S(2)}, u32[]{:S(2)}) collective-permute-start(bf16[1,1,1,1,24,1536]{5,4,3,2,1,0:T(8,128)(2,1)S(1)} %copy-done.212), channel_id=1, source_target_pairs={{16,8},{17,9},{18,10},{19,11},{20,12},{21,13},{22,14},{23,15},{24,... | collective-permute-start | bytes 221192 | tf_op jit(solution)/shard_map/ppermute | solution.py:79
  635.6 26.8 %collective-permute-start.87 = (f32[3,1792]{1,0:T(4,128)S(1)}, f32[3,1792]{1,0:T(4,128)S(1)}, u32[]{:S(2)}, u32[]{:S(2)}) collective-permute-start(f32[3,1792]{1,0:T(4,128)S(1)} %copy-done.258), channel_id=1, source_target_pairs={{1,0},{2,1},{3,2},{5,4},{6,5},{7,6},{9,8},{10,9},{11,10},{13,12},{... | collective-permute-start | bytes 64520 | tf_op jit(solution)/shard_map/ppermute | solution.py:22
  648.0 50.4 %collective-permute-start.103 = (bf16[4,2,2,1,24,1024]{5,4,3,2,1,0:T(8,128)(2,1)}, bf16[4,2,2,1,24,1024]{5,4,3,2,1,0:T(8,128)(2,1)}, u32[]{:S(2)}, u32[]{:S(2)}) collective-permute-start(bf16[4,2,2,1,24,1024]{5,4,3,2,1,0:T(8,128)(2,1)} %constant_dynamic-slice_fusion.28), channel_id=1, source_target_pairs={{0,1},{1,0},{2,3},{3,2},{4,5},{5,4},{6,7},{7,6},{8,9},{9,8},{10,11... | collective-permute-start | bytes 2359304 | tf_op jit(solution)/shard_map/ppermute | solution.py:70
  648.0 46.2 %collective-permute-start.149 = (bf16[1,1,1,1,48,768]{5,4,3,2,1,0:T(8,128)(2,1)}, bf16[1,1,1,1,48,768]{5,4,3,2,1,0:T(8,128)(2,1)}, u32[]{:S(2)}, u32[]{:S(2)}) collective-permute-start(bf16[1,1,1,1,48,768]{5,4,3,2,1,0:T(8,128)(2,1)} %get-tuple-element.256), channel_id=1, source_target_pairs={{0,8},{1,9},{2,10},{3,11},{4,12},{5,13},{6,14},{7,15},{8,16},{9,17... | collective-permute-start | bytes 221192 | tf_op jit(solution)/shard_map/ppermute | solution.py:79
  659.4 34.8 %collective-permute-start.152 = (bf16[1,1,1,1,48,768]{5,4,3,2,1,0:T(8,128)(2,1)}, bf16[1,1,1,1,48,768]{5,4,3,2,1,0:T(8,128)(2,1)}, u32[]{:S(2)}, u32[]{:S(2)}) collective-permute-start(bf16[1,1,1,1,48,768]{5,4,3,2,1,0:T(8,128)(2,1)} %get-tuple-element.257), channel_id=1, source_target_pairs={{8,0},{9,1},{10,2},{11,3},{12,4},{13,5},{14,6},{15,7},{16,8},{17,9... | collective-permute-start | bytes 221192 | tf_op jit(solution)/shard_map/ppermute | solution.py:79
  662.4 26.9 %collective-permute-start.120 = (bf16[1,1,1,1,24,1536]{5,4,3,2,1,0:T(8,128)(2,1)}, bf16[1,1,1,1,24,1536]{5,4,3,2,1,0:T(8,128)(2,1)}, u32[]{:S(2)}, u32[]{:S(2)}) collective-permute-start(bf16[1,1,1,1,24,1536]{5,4,3,2,1,0:T(8,128)(2,1)} %get-tuple-element.268), channel_id=1, source_target_pairs={{0,8},{1,9},{2,10},{3,11},{4,12},{5,13},{6,14},{7,15},{8,16},{9,17... | collective-permute-start | bytes 221192 | tf_op jit(solution)/shard_map/ppermute | solution.py:79
  700.0 13.8 %collective-permute-start.104 = (bf16[4,1,2,1,24,1024]{5,4,3,2,1,0:T(8,128)(2,1)S(1)}, bf16[4,1,2,1,24,1024]{5,4,3,2,1,0:T(8,128)(2,1)S(1)}, u32[]{:S(2)}, u32[]{:S(2)}) collective-permute-start(bf16[4,1,2,1,24,1024]{5,4,3,2,1,0:T(8,128)(2,1)S(1)} %constant_dynamic-slice_fusion.27), channel_id=1, source_target_pairs={{0,4},{1,5},{2,6},{3,7},{4,0},{5,1},{6,2},{7,3},{8,12},{9,13},{10,... | collective-permute-start | bytes 1179656 | tf_op jit(solution)/shard_map/ppermute | solution.py:70
  702.4 19.8 %collective-permute-start.92 = (bf16[4,1,2,1,24,1024]{5,4,3,2,1,0:T(8,128)(2,1)S(1)}, bf16[4,1,2,1,24,1024]{5,4,3,2,1,0:T(8,128)(2,1)S(1)}, u32[]{:S(2)}, u32[]{:S(2)}) collective-permute-start(bf16[4,1,2,1,24,1024]{5,4,3,2,1,0:T(8,128)(2,1)S(1)} %constant_dynamic-slice_fusion.33), channel_id=1, source_target_pairs={{0,4},{1,5},{2,6},{3,7},{4,0},{5,1},{6,2},{7,3},{8,12},{9,13},{10,... | collective-permute-start | bytes 1179656 | tf_op jit(solution)/shard_map/ppermute | solution.py:70
  707.6 17.8 %collective-permute-start.90 = (bf16[4,1,1,1,24,896]{5,4,3,2,1,0:T(8,128)(2,1)S(1)}, bf16[4,1,1,1,24,896]{5,4,3,2,1,0:T(8,128)(2,1)S(1)}, u32[]{:S(2)}, u32[]{:S(2)}) collective-permute-start(bf16[4,1,1,1,24,896]{5,4,3,2,1,0:T(8,128)(2,1)S(1)} %constant_dynamic-slice_fusion.35), channel_id=1, source_target_pairs={{0,4},{1,5},{2,6},{3,7},{4,0},{5,1},{6,2},{7,3},{8,12},{9,13},{10,... | collective-permute-start | bytes 516104 | tf_op jit(solution)/shard_map/ppermute | solution.py:70
  742.0 13.1 %collective-permute-start.108 = (bf16[1,1,1,1,24,1920]{5,4,3,2,1,0:T(8,128)(2,1)S(1)}, bf16[1,1,1,1,24,1920]{5,4,3,2,1,0:T(8,128)(2,1)S(1)}, u32[]{:S(2)}, u32[]{:S(2)}) collective-permute-start(bf16[1,1,1,1,24,1920]{5,4,3,2,1,0:T(8,128)(2,1)S(1)} %get-tuple-element.248), channel_id=1, source_target_pairs={{0,8},{1,9},{2,10},{3,11},{4,12},{5,13},{6,14},{7,15},{8,16},{9,17... | collective-permute-start | bytes 276488 | tf_op jit(solution)/shard_map/ppermute | solution.py:79
  (407 other events, 2887.7 us)

commit v2 on v1

v2 whole, which is shorter than its diff:
```python
import jax
import jax.numpy as jnp
from jax import lax
from jax.experimental import pallas as pl
from jax.experimental.pallas import tpu as pltpu
from jax.sharding import PartitionSpec as P

INNER = 1536
HEADS = 24
HEAD_DIM = 64
STATE = 128
KCONV = 4
SPAN = 256
XBC = INNER + 2 * STATE


epsilon = 1e-05


def shifted(block, axis, distance):
    devices = range(lax.axis_size(axis))
    route = [(i - distance, i) for i in devices if i - distance in devices]
    return lax.ppermute(block, axis, route)


AXES = ("dp", "fsdp")


def radices(count):
    factors = []
    radix = 2
    while count > 1:
        while count % radix:
            radix += 1
        factors.append(radix)
        count //= radix
    return factors


class Grid:
    def __init__(self):
        self.count = lax.axis_size("dp") * lax.axis_size("fsdp")
        self.factors = radices(self.count)
        self.place = lax.axis_index("dp") * lax.axis_size("fsdp") + lax.axis_index("fsdp")
        self.strides = []
        stride = 1
        for radix in self.factors:
            self.strides.append(stride)
            stride *= radix
        self.depth = len(self.factors)

    def digit(self, k):
        return (self.place // self.strides[k]) % self.factors[k]

    def dims(self):
        return tuple(reversed(self.factors))

    def axis(self, k):
        return self.depth - 1 - k

    def swap(self, block, k):
        stride = self.strides[k]
        route = []
        for i in range(self.count):
            up = (i // stride) % 2 == 0
            route.append((i, i + stride if up else i - stride))
        return lax.ppermute(block, AXES, route)

    def hop(self, block, k, way, keep):
        stride, radix = self.strides[k], self.factors[k]
        route = []
        for i in range(self.count):
            digit = (i // stride) % radix
            if 0 <= digit + way < radix and keep(digit):
                route.append((i, i + way * stride))
        return lax.ppermute(block, AXES, route)

    def gather_step(self, block, k):
        axis, radix = self.axis(k), self.factors[k]
        digit = self.digit(k)
        if radix == 2:
            other = self.swap(block, k)
            first = jnp.where(digit == 0, block, other)
            second = jnp.where(digit == 0, other, block)
            return jnp.concatenate([first, second], axis=axis)
        before, after = [], []
        left = right = block
        for d in range(1, radix):
            left = self.hop(left, k, 1, lambda digit: digit >= d - 1)
            right = self.hop(right, k, -1, lambda digit: digit + d - 1 < radix)
            before.insert(0, left)
            after.append(right)
        line = jnp.concatenate(before + [block] + after, axis=axis)
        return lax.dynamic_slice_in_dim(line, radix - 1 - digit, radix, axis)

    def scatter_step(self, block, k, kind):
        axis, radix = self.axis(k), self.factors[k]
        digit = self.digit(k)

        def pick(index):
            index = jnp.clip(index, 0, radix - 1)
            return lax.dynamic_slice_in_dim(block, index, 1, axis)

        wide = jnp.float32
        if radix == 2:
            got = self.swap(pick(1 - digit), k)
            return (pick(digit).astype(wide) + got.astype(wide)).astype(kind)
        total = pick(digit).astype(wide)
        for way in (1, -1):
            run = None
            for d in range(radix - 1, 0, -1):
                part = pick(digit + way * d)
                if run is not None:
                    part = (part.astype(wide) + run.astype(wide)).astype(block.dtype)
                run = self.hop(part, k, way, lambda digit: 0 <= digit + way * d < radix)
            total = total + run.astype(wide)
        return total.astype(kind)

    def orders(self):
        far = list(range(self.depth - 1, 2, -1))
        return far, ([1, 2], [2, 1])

    def sum_all(self, value):
        for k in range(self.depth):
            value = value + self.swap(value, k)
        return value


def tied(value, *others):
    others = [o for o in others if o is not None]
    if not others:
        return value
    return lax.optimization_barrier((value, *others))[0]


def gather_pack(grid, pieces, after_far, after_near):
    far, orders = grid.orders()
    rows = pieces[0].shape[0]
    block = jnp.concatenate(pieces, axis=1)
    block = tied(block.reshape((1,) * grid.depth + block.shape), after_far)
    for k in far:
        block = grid.gather_step(block, k)
    near = tied(block, after_near)
    cut = pieces[0].shape[1]
    parts = [near[..., :cut], near[..., cut:]]
    for at in range(2):
        parts = [grid.gather_step(p, order[at]) for p, order in zip(parts, orders)]
    wholes = [grid.gather_step(p, 0).reshape(-1, p.shape[-1]) for p in parts]
    return wholes, block, parts[0]


def scatter_pack(grid, wholes):
    far, orders = grid.orders()
    rows = wholes[0].shape[0] // grid.count
    parts = []
    for whole, order in zip(wholes, orders):
        part = whole.reshape(grid.dims() + (rows, whole.shape[1]))
        for k in (0, *order):
            part = grid.scatter_step(part, k, BF16)
        parts.append(part)
    cut = wholes[0].shape[1]
    block = jnp.concatenate(parts, axis=-1)
    near = list(reversed(far))
    for k in near:
        block = grid.scatter_step(block, k, F32 if k == near[-1] else BF16)
    block = block.reshape(rows, -1)
    return block[:, :cut], block[:, cut:]


def state_chain(growth, keep, fresh, axis, way):
    devices = lax.axis_size(axis)
    carry = jnp.zeros_like(fresh)
    for s in range(1, devices):
        leaving = (growth * carry + fresh) * keep
        at = s - 1 if way == 1 else devices - s
        got = lax.ppermute(leaving.astype(jnp.bfloat16), axis, [(at, at + way)])
        carry = carry + got.astype(jnp.float32)
    return carry


LANES = 128
PAIRS = INNER // LANES
F32 = jnp.float32
BF16 = jnp.bfloat16
FAR = -1e30


def dot(a, b):
    return jnp.dot(a, b, preferred_element_type=F32)


def dot_nt(a, b):
    return lax.dot_general(a, b, (((1,), (1,)), ((), ())), preferred_element_type=F32)


def flip(a):
    return a.astype(F32).T


def split3(value):
    high = value.astype(BF16)
    rest = value - high.astype(F32)
    mid = rest.astype(BF16)
    low = (rest - mid.astype(F32)).astype(BF16)
    return jnp.concatenate([high, mid, low], axis=1)


def head_sum(value, spread):
    high = value.astype(BF16)
    low = (value - high.astype(F32)).astype(BF16)
    return dot_nt(high, spread) + dot_nt(low, spread)


def lanes_of(p):
    return pl.ds(pl.multiple_of(p * LANES, LANES), LANES)


def sigmoid(v):
    return 1.0 / (1.0 + jnp.exp(-v))


def iota(shape, axis):
    return lax.broadcasted_iota(jnp.int32, shape, axis)


def call(body, outs, *args, scratch=(), flops=2e9):
    vm = pl.BlockSpec(memory_space=pltpu.VMEM)
    size = sum(a.size * a.dtype.itemsize for a in args)
    return pl.pallas_call(
        body,
        out_shape=[jax.ShapeDtypeStruct(s, d) for s, d in outs],
        in_specs=[vm] * len(args),
        out_specs=[vm] * len(outs),
        scratch_shapes=list(scratch),
        compiler_params=pltpu.CompilerParams(vmem_limit_bytes=52 * 2**20),
        cost_estimate=pl.CostEstimate(flops=int(flops), bytes_accessed=int(size), transcendentals=0),
    )(*args)


def project_body(hidden, gain, wa, wb, normed, conv_in, dt):
    h = hidden[...]
    scale = lax.rsqrt(jnp.mean(h * h, axis=-1, keepdims=True) + epsilon)
    low = (h * scale * gain[...]).astype(BF16)
    normed[...] = low
    cut = wa.shape[1]
    rest = XBC - cut
    conv_in[:, :cut] = dot(low, wa[...]).astype(BF16)
    second = dot(low, wb[...])
    conv_in[:, cut:] = second[:, :rest].astype(BF16)
    dt[...] = jnp.where(iota((SPAN, LANES), 1) < HEADS, second[:, rest : rest + LANES], 0.0)


def conv_pre(ext, weight, bias, lanes):
    total = bias[:, lanes] + weight[KCONV - 1 : KCONV, lanes] * ext[8 : 8 + SPAN, lanes]
    for s in range(1, KCONV):
        tap = weight[KCONV - 1 - s : KCONV - s, lanes]
        total = total + tap * ext[8 - s : 8 - s + SPAN, lanes]
    return total


def triangle(upper):
    i, j = iota((SPAN, SPAN), 0), iota((SPAN, SPAN), 1)
    return jnp.where((i <= j) if upper else (i >= j), 1.0, 0.0).astype(F32)


def running(mask, value):
    return jnp.dot(mask, value, precision=lax.Precision.HIGHEST, preferred_element_type=F32)


def states_body(
    conv_in, rim, weight, bias, dt, dt_bias, a_log, valid, spread,
    x, keys, queries, step, cum, fresh, growth, ext, wide,
):
    ext[:8] = rim[...].astype(F32)
    ext[8:] = conv_in[...].astype(F32)

    def act(lanes):
        pre = conv_pre(ext, weight, bias, lanes)
        return (pre * sigmoid(pre)).astype(BF16)

    keys[...] = act(pl.ds(INNER, LANES))
    queries[...] = act(pl.ds(INNER + LANES, LANES))
    raw = dt[...] + dt_bias[...]
    size = jnp.maximum(raw, 0.0) + jnp.log1p(jnp.exp(-jnp.abs(raw)))
    size = jnp.where(iota((SPAN, LANES), 1) < HEADS, size * valid[...], 0.0)
    step[...] = size
    total = running(triangle(False), -jnp.exp(a_log[...]) * size)
    cum[...] = total
    last = total[SPAN - 1 :]
    tail = jnp.exp(last - total) * size
    wide[...] = split3(tail)
    grow = split3(jnp.broadcast_to(jnp.exp(last), (8, LANES)))
    turned = flip(keys[...]).astype(BF16)

    def pair(p, carry):
        lanes = lanes_of(p)
        low = act(lanes)
        x[:, lanes] = low
        weighted = (low.astype(F32) * dot(wide[...], spread[:, lanes])).astype(BF16)
        fresh[:, lanes] = dot(turned, weighted)
        growth[:, lanes] = dot(grow, spread[:, lanes])
        return carry

    lax.fori_loop(0, PAIRS, pair, 0)


def diag_body(x, keys, queries, step, cum, skip, spread, y, scores, cum_t, step_t, wide):
    scores[...] = dot_nt(queries[...], keys[...])
    cum_t[...] = cum[...].T
    step_t[...] = step[...].T
    wide[...] = split3(cum[...])
    half = SPAN // 2

    def pair(p, carry):
        lanes = lanes_of(p)
        xp = x[:, lanes]
        col = dot(wide[...], spread[:, lanes])
        turned = pltpu.roll(col, HEAD_DIM, 1)
        first = iota((SPAN, LANES), 1) < HEAD_DIM
        both = []
        for k in range(2):
            c = jnp.where(first, col, turned) if k == 0 else jnp.where(first, turned, col)
            row = cum_t[pl.ds(2 * p + k, 1), :]
            steps = step_t[pl.ds(2 * p + k, 1), :]
            tri = iota((SPAN, half), 0) >= iota((SPAN, half), 1)
            f0 = jnp.exp(jnp.where(tri, c - row[:, :half], FAR))
            m0 = (scores[:, :half] * f0 * steps[:, :half]).astype(BF16)
            f1 = jnp.exp(jnp.where(tri[:half], c[half:] - row[:, half:], FAR))
            m1 = (scores[half:, half:] * f1 * steps[:, half:]).astype(BF16)
            d0 = dot(m0, xp[:half])
            d1 = dot(m1, xp[half:])
            both.append(jnp.concatenate([d0[:half], d0[half:] + d1], axis=0))
        y[:, lanes] = jnp.where(first, both[0], both[1]) + skip[:, lanes] * xp.astype(F32)
        return carry

    lax.fori_loop(0, PAIRS, pair, 0)


def finish_body(y, gate, queries, carried, cum, gain, w_out, hidden, spread, mixed, normed_out, result, wide, total, gated):
    wide[...] = split3(jnp.exp(cum[...]))
    total[...] = jnp.zeros_like(total)

    def mix(p, carry):
        lanes = lanes_of(p)
        rise = dot(wide[...], spread[:, lanes])
        m = y[:, lanes] + rise * dot(queries[...], carried[:, lanes])
        mixed[:, lanes] = m
        g = gate[:, lanes]
        v = m * (g * sigmoid(g))
        gated[:, lanes] = v
        total[...] += v * v
        return carry

    lax.fori_loop(0, PAIRS, mix, 0)
    mean = jnp.sum(total[...], axis=1, keepdims=True) * (1.0 / INNER)
    scale = lax.rsqrt(mean + epsilon)

    def norm(p, carry):
        lanes = lanes_of(p)
        normed_out[:, lanes] = (gated[:, lanes] * scale * gain[:, lanes]).astype(BF16)
        return carry

    lax.fori_loop(0, PAIRS, norm, 0)
    result[...] = hidden[...] + dot(normed_out[...], w_out[...])


def open_body(
    grad, w_out, mixed, gate, gain, queries, carried, cum, x, spread,
    gain_grad, gate_low, diag_low, entering_grad, query_grad, cum_grad, skip_grad, wide, square, cross, back,
):
    out_low = grad[...].astype(BF16)
    square[...] = jnp.zeros_like(square)
    cross[...] = jnp.zeros_like(cross)
    query_grad[...] = jnp.zeros_like(query_grad)
    cum_grad[...] = jnp.zeros_like(cum_grad)
    wide[...] = split3(jnp.exp(cum[...]))

    def first(p, carry):
        lanes = lanes_of(p)
        g = dot_nt(out_low, w_out[lanes, :])
        back[:, lanes] = g
        a = gate[:, lanes]
        v = mixed[:, lanes] * (a * sigmoid(a))
        square[...] += v * v
        cross[...] += v * (g * gain[:, lanes])
        return carry

    lax.fori_loop(0, PAIRS, first, 0)
    scale = lax.rsqrt(jnp.sum(square[...], axis=1, keepdims=True) * (1.0 / INNER) + epsilon)
    share = jnp.sum(cross[...], axis=1, keepdims=True) * (1.0 / INNER) * scale * scale * scale
    turned = flip(queries[...]).astype(BF16)

    def second(p, carry):
        lanes = lanes_of(p)
        g = back[:, lanes]
        a = gate[:, lanes]
        s = sigmoid(a)
        act = a * s
        m = mixed[:, lanes]
        v = m * act
        gain_grad[:, lanes] = jnp.sum(g * v * scale, axis=0, keepdims=True)
        dv = scale * (g * gain[:, lanes]) - v * share
        gate_low[:, lanes] = (dv * m * (s + act * (1.0 - s))).astype(BF16)
        gm = dv * act
        diag_low[:, lanes] = gm.astype(BF16)
        skip_grad[:, lanes] = jnp.sum(gm * x[:, lanes].astype(F32), axis=0, keepdims=True)
        risen = dot(wide[...], spread[:, lanes]) * gm
        low = risen.astype(BF16)
        kept = carried[:, lanes]
        heads = spread[:LANES, lanes]
        cum_grad[...] += head_sum(risen * dot(queries[...], kept), heads)
        entering_grad[:, lanes] = dot(turned, low)
        query_grad[...] += dot_nt(low, kept)
        return carry

    lax.fori_loop(0, PAIRS, second, 0)


def pairs_body(
    diag_low, x, keys, queries, step, cum, skip, spread, query_in,
    x_grad, key_grad, query_grad, step_grad, row_grad, scores, score_grad, cum_t, wide, wide_step,
):
    scores[...] = dot_nt(keys[...], queries[...])
    score_grad[...] = jnp.zeros_like(score_grad)
    step_grad[...] = jnp.zeros_like(step_grad)
    row_grad[...] = jnp.zeros_like(row_grad)
    cum_t[...] = cum[...].T
    wide[...] = split3(cum[...])
    wide_step[...] = split3(step[...])
    half = SPAN // 2

    def pair(p, carry):
        lanes = lanes_of(p)
        xp = x[:, lanes]
        dp = diag_low[:, lanes]
        first = iota((SPAN, LANES), 1) < HEAD_DIM
        col = dot(wide[...], spread[:, lanes])
        col_turned = pltpu.roll(col, HEAD_DIM, 1)
        stp = dot(wide_step[...], spread[:, lanes])
        stp_turned = pltpu.roll(stp, HEAD_DIM, 1)
        both = []
        for k in range(2):
            mine = first if k == 0 else jnp.logical_not(first)
            c = jnp.where(mine, col, col_turned)
            st = jnp.where(mine, stp, stp_turned)
            row = cum_t[pl.ds(2 * p + k, 1), :]
            tri = iota((SPAN, half), 0) <= iota((SPAN, half), 1) + half
            xk = jnp.where(mine, xp.astype(F32), 0.0).astype(BF16)
            g1 = dot_nt(xk, dp[half:])
            g0 = dot_nt(xk[:half], dp[:half])
            f1 = jnp.exp(jnp.where(tri, row[:, half:] - c, FAR))
            f0 = jnp.exp(jnp.where(tri[half:], row[:, :half] - c[:half], FAR))
            w1, w0 = g1 * f1, g0 * f0
            s1, s0 = scores[:, half:], scores[:half, :half]
            st0 = st[:half]
            score_grad[:, half:] += w1 * st
            score_grad[:half, :half] += w0 * st0
            q1, q0 = w1 * s1, w0 * s0
            each = jnp.sum(q1, axis=1, keepdims=True)
            each = jnp.concatenate(
                [each[:half] + jnp.sum(q0, axis=1, keepdims=True), each[half:]], axis=0
            )
            step_grad[...] += jnp.where(iota((SPAN, LANES), 1) == 2 * p + k, each, 0.0)
            across = jnp.concatenate(
                [
                    jnp.sum(q0 * st0, axis=0, keepdims=True),
                    jnp.sum(q1 * st, axis=0, keepdims=True),
                ],
                axis=1,
            )
            row_grad[pl.ds(2 * p + k, 1), :] = across
            m1 = (s1 * f1 * st).astype(BF16)
            m0 = (s0 * f0 * st0).astype(BF16)
            top = dot(m1, dp[half:])
            low = dot(m0, dp[:half])
            both.append(jnp.concatenate([top[:half] + low, top[half:]], axis=0))
        x_grad[:, lanes] = jnp.where(first, both[0], both[1]) + skip[:, lanes] * dp.astype(F32)
        return carry

    lax.fori_loop(0, PAIRS, pair, 0)
    low = score_grad[...].astype(BF16)
    key_grad[...] = dot(low, queries[...])
    query_grad[...] = query_in[...] + dot(score_grad[...].T.astype(BF16), keys[...])


def close_body(
    pending, carried, keys, x, step, cum, x_grad, key_in, query_grad, step_in, row_grad, cum_in,
    conv_in, rim, weight, bias, dt, dt_bias, a_log, valid, spread,
    act_grad, dt_low, dt_bias_grad, a_log_grad, bias_grad, weight_grad,
    ext, wide, tail_grad, grow_grad, key_grad,
):
    ext[:8] = rim[...].astype(F32)
    ext[8:] = conv_in[...].astype(F32)
    total = cum[...]
    size = step[...]
    last = total[SPAN - 1 :]
    fade = jnp.exp(last - total)
    tail = fade * size
    wide[...] = split3(tail)
    tail_grad[...] = jnp.zeros_like(tail_grad)
    grow_grad[...] = jnp.zeros_like(grow_grad)
    key_grad[...] = key_in[...]

    def through(lanes, grad):
        pre = conv_pre(ext, weight, bias, lanes)
        s = sigmoid(pre)
        ga = grad * (s * (1.0 + pre * (1.0 - s)))
        act_grad[:, lanes] = ga
        bias_grad[:, lanes] = jnp.sum(ga, axis=0, keepdims=True)
        for k in range(KCONV):
            at = 8 - (KCONV - 1 - k)
            weight_grad[k : k + 1, lanes] = jnp.sum(
                ga * ext[at : at + SPAN, lanes], axis=0, keepdims=True
            )

    def pair(p, carry):
        lanes = lanes_of(p)
        late = pending[:, lanes]
        low = late.astype(BF16)
        xp = x[:, lanes].astype(F32)
        heads = spread[:LANES, lanes]
        over = dot(wide[...], spread[:, lanes])
        gw = dot(keys[...], low)
        tail_grad[...] += head_sum(gw * xp, heads)
        key_grad[...] += dot_nt((xp * over).astype(BF16), low)
        column = jnp.sum(late * carried[:, lanes].astype(F32), axis=0, keepdims=True)
        grow_grad[...] += head_sum(jnp.broadcast_to(column, (8, LANES)), heads)
        through(lanes, x_grad[:, lanes] + gw * over)
        return carry

    lax.fori_loop(0, PAIRS, pair, 0)
    through(pl.ds(INNER, LANES), key_grad[...])
    through(pl.ds(INNER + LANES, LANES), query_grad[...])
    tg = tail_grad[...]
    run = tg * tail
    cg = cum_in[...] + row_grad[...].T - size * step_in[...] - run
    end = jnp.sum(run, axis=0, keepdims=True) + grow_grad[:1] * jnp.exp(last)
    cg = cg + jnp.where(iota((SPAN, LANES), 0) == SPAN - 1, end, 0.0)
    rate = jnp.exp(a_log[...])
    decay_grad = running(triangle(True), cg)
    sg = tg * fade + step_in[...] - rate * decay_grad
    a_log_grad[...] = jnp.sum(decay_grad * (-rate * size), axis=0, keepdims=True)
    pre_grad = sg * valid[...] * sigmoid(dt[...] + dt_bias[...])
    pre_grad = jnp.where(iota((SPAN, LANES), 1) < HEADS, pre_grad, 0.0)
    dt_bias_grad[...] = jnp.sum(pre_grad, axis=0, keepdims=True)
    dt_low[...] = pre_grad.astype(BF16)


def inward_body(act_grad, rim_grad, weight, dt_low, gate_part, wa, wb, hidden, gain, grad, first, grad_out, gain_grad, ext):
    ext[:SPAN] = act_grad[...]
    ext[SPAN:] = rim_grad[...]

    def conv(c, carry):
        lanes = lanes_of(c)
        total = weight[KCONV - 1 : KCONV, lanes] * ext[:SPAN, lanes]
        for s in range(1, KCONV):
            total = total + weight[KCONV - 1 - s : KCONV - s, lanes] * ext[s : s + SPAN, lanes]
        first[:, lanes] = total.astype(BF16)
        return carry

    lax.fori_loop(0, XBC // LANES, conv, 0)
    first[:, XBC:] = dt_low[...]
    cut = wa.shape[1]
    back = gate_part[...] + dot_nt(first[:, :cut], wa[...]) + dot_nt(first[:, cut:], wb[...])
    h = hidden[...]
    scale = lax.rsqrt(jnp.mean(h * h, axis=-1, keepdims=True) + epsilon)
    gain_grad[...] = jnp.sum(back * h * scale, axis=0, keepdims=True)
    back = back * gain[...]
    share = jnp.mean(back * h, axis=-1, keepdims=True) * scale * scale * scale
    grad_out[...] = grad[...] + back * scale - h * share


def padded(row):
    return jnp.pad(row.astype(F32), (0, LANES - row.shape[0]))[None]


def layer_forward(hidden, weights, heads, keep, valid, spread):
    norm_gain, wa, wb, w_gate, conv_weight, conv_bias, gate_gain, w_out = weights
    dt_bias, a_log, skip = heads
    count = hidden.shape[0]
    normed, conv_in, dt = call(
        project_body,
        [((count, hidden.shape[1]), BF16), ((count, XBC), BF16), ((count, LANES), F32)],
        hidden, norm_gain, wa, wb,
    )
    rim = (shifted(conv_in[count - 8 :], "fsdp", 1).astype(F32) * keep).astype(BF16)
    x, keys, queries, step, cum, fresh, growth = call(
        states_body,
        [
            ((count, INNER), BF16), ((count, STATE), BF16), ((count, STATE), BF16), ((count, LANES), F32),
            ((count, LANES), F32), ((STATE, INNER), F32), ((8, INNER), F32),
        ],
        conv_in, rim, conv_weight, conv_bias, dt, dt_bias, a_log, valid, spread,
        scratch=[pltpu.VMEM((count + 8, XBC), F32), pltpu.VMEM((count, 3 * LANES), BF16)],
        flops=5e8,
    )
    growth = growth[:1]
    carried = (keep * state_chain(keep * growth, 1.0, fresh, "fsdp", 1)).astype(BF16)
    (y,) = call(
        diag_body, [((count, INNER), F32)], x, keys, queries, step, cum, skip, spread,
        scratch=[
            pltpu.VMEM((SPAN, SPAN), F32), pltpu.VMEM((LANES, count), F32), pltpu.VMEM((LANES, count), F32),
            pltpu.VMEM((count, 3 * LANES), BF16),
        ],
        flops=4e9,
    )
    gate = dot(normed, w_gate)
    mixed, normed_out, result = call(
        finish_body,
        [((count, INNER), F32), ((count, INNER), BF16), (hidden.shape, F32)],
        y, gate, queries, carried, cum, gate_gain, w_out, hidden, spread,
        scratch=[
            pltpu.VMEM((count, 3 * LANES), BF16), pltpu.VMEM((count, LANES), F32), pltpu.VMEM((count, INNER), F32),
        ],
    )
    saved = (hidden, normed, conv_in, dt, rim, x, keys, queries, step, cum, growth, carried, gate, mixed, normed_out)
    return result, saved


def layer_backward(grad, saved, weights, heads, keep, valid, spread):
    norm_gain, wa, wb, w_gate, conv_weight, conv_bias, gate_gain, w_out = weights
    dt_bias, a_log, skip = heads
    hidden, normed, conv_in, dt, rim, x, keys, queries, step, cum, growth, carried, gate, mixed, normed_out = saved
    count = hidden.shape[0]
    row = (1, INNER)
    gain_grad, gate_low, diag_low, entering_grad, query_part, cum_part, skip_grad = call(
        open_body,
        [
            (row, F32), ((count, INNER), BF16), ((count, INNER), BF16), ((STATE, INNER), F32), ((count, STATE), F32),
            ((count, LANES), F32), (row, F32),
        ],
        grad, w_out, mixed, gate, gate_gain, queries, carried, cum, x, spread,
        scratch=[
            pltpu.VMEM((count, 3 * LANES), BF16), pltpu.VMEM((count, LANES), F32), pltpu.VMEM((count, LANES), F32),
            pltpu.VMEM((count, INNER), F32),
        ],
    )
    grad_w_out = dot(normed_out.T, grad.astype(BF16)).astype(BF16)
    pending = state_chain(growth, keep, entering_grad, "fsdp", -1)
    x_grad, key_grad, query_grad, step_grad, row_grad = call(
        pairs_body,
        [
            ((count, INNER), F32), ((count, STATE), F32), ((count, STATE), F32), ((count, LANES), F32),
            ((LANES, count), F32),
        ],
        diag_low, x, keys, queries, step, cum, skip, spread, query_part,
        scratch=[
            pltpu.VMEM((SPAN, SPAN), F32), pltpu.VMEM((SPAN, SPAN), F32), pltpu.VMEM((LANES, count), F32),
            pltpu.VMEM((count, 3 * LANES), BF16), pltpu.VMEM((count, 3 * LANES), BF16),
        ],
        flops=8e9,
    )
    grad_w_gate = dot(normed.T, gate_low).astype(BF16)
    gate_part = dot(gate_low, w_gate.T)
    act_grad, dt_low, dt_bias_grad, a_log_grad, bias_grad, weight_grad = call(
        close_body,
        [
            ((count, XBC), F32), ((count, LANES), BF16), ((1, LANES), F32), ((1, LANES), F32), ((1, XBC), F32),
            ((KCONV, XBC), F32),
        ],
        pending, carried, keys, x, step, cum, x_grad, key_grad, query_grad, step_grad, row_grad, cum_part,
        conv_in, rim, conv_weight, conv_bias, dt, dt_bias, a_log, valid, spread,
        scratch=[
            pltpu.VMEM((count + 8, XBC), F32), pltpu.VMEM((count, 3 * LANES), BF16), pltpu.VMEM((count, LANES), F32),
            pltpu.VMEM((8, LANES), F32), pltpu.VMEM((count, STATE), F32),
        ],
    )
    rim_grad = shifted(act_grad[:8] * keep, "fsdp", -1)
    first, grad_out, norm_grad = call(
        inward_body,
        [((count, XBC + LANES), BF16), (hidden.shape, F32), ((1, hidden.shape[1]), F32)],
        act_grad, rim_grad, conv_weight, dt_low, gate_part, wa, wb, hidden, norm_gain, grad,
        scratch=[pltpu.VMEM((count + 8, XBC), F32)],
    )
    grad_first = dot(normed.T, first).astype(BF16)
    skip_sum = jnp.sum(skip_grad.reshape(HEADS, HEAD_DIM), axis=1)
    rows = (norm_grad[0], weight_grad, bias_grad[0], gain_grad[0])
    head_grads = jnp.stack([dt_bias_grad[0, :HEADS], a_log_grad[0, :HEADS], skip_sum])
    return grad_out, (grad_w_out, grad_w_gate, grad_first), rows, head_grads


def shards(
    tokens,
    starts,
    valid,
    norm_gain,
    w_gate,
    w_xbc,
    w_dt,
    conv_weight,
    conv_bias,
    dt_bias,
    a_log,
    skip_weight,
    gate_gain,
    w_out,
    cotangent,
):
    layers = norm_gain.shape[0]
    grid = Grid()
    count = grid.count
    rows, outer = w_gate.shape[1], w_out.shape[1]
    taps, chans = conv_weight.shape[1:]
    small = rows + (taps + 1) * chans + outer
    small_cols = -(-small // rows)
    spare = rows * small_cols - small
    pad = LANES - HEADS - small_cols
    cut = XBC // 2 // LANES * LANES
    at_small = XBC + HEADS
    firsts, seconds = [], []
    last_far = last_near = None
    for l in range(layers):
        extra = jnp.concatenate([norm_gain[l], conv_weight[l].reshape(-1), conv_bias[l], gate_gain[l]])
        extra = jnp.pad(extra, (0, spare)).reshape(rows, small_cols)
        tail = jnp.concatenate([w_xbc[l][:, cut:], w_dt[l], extra, jnp.zeros((rows, pad), BF16)], 1)
        pair, last_far, last_near = gather_pack(grid, [w_xbc[l][:, :cut], tail], last_far, last_near)
        firsts.append(pair)
        outs = w_out[l].reshape(rows, -1)
        pair, last_far, last_near = gather_pack(grid, [w_gate[l], outs], last_far, last_near)
        seconds.append(pair)
    wholes, heads = [], []
    split = rows + taps * chans
    for l in range(layers):
        wa, wb = firsts[l]
        extra = wb[:, at_small - cut : at_small - cut + small_cols].reshape(count, -1).astype(F32)
        kernel = jnp.moveaxis(extra[:, rows:split].reshape(count, taps, chans), 1, 0)
        wholes.append(
            (
                extra[:, :rows].reshape(1, -1),
                wa,
                wb,
                seconds[l][0],
                kernel.reshape(taps, -1),
                extra[:, split : split + chans].reshape(1, -1),
                extra[:, split + chans : small].reshape(1, -1),
                seconds[l][1].reshape(INNER, -1),
            )
        )
        heads.append((padded(dt_bias[l]), padded(a_log[l]), jnp.repeat(skip_weight[l], HEAD_DIM)[None]))
    spread = (iota((3 * LANES, INNER), 0) % LANES == iota((3 * LANES, INNER), 1) // HEAD_DIM).astype(BF16)
    keep = 1.0 - starts[0].astype(F32)
    valid = valid.astype(F32)[:, None]
    hidden = tokens.astype(F32)
    saves = []
    for l in range(layers):
        hidden, saved = layer_forward(hidden, wholes[l], heads[l], keep, valid, spread)
        saves.append(saved)
    grad = cotangent.astype(F32)
    owned, summed = [None] * layers, [None] * layers
    for l in reversed(range(layers)):
        grad, mats, row_grads, summed[l] = layer_backward(
            grad, saves[l], wholes[l], heads[l], keep, valid, spread
        )
        grad_w_out, grad_w_gate, grad_first = mats
        grad_norm, grad_kernel, grad_bias, grad_gain = row_grads
        gate_sum, out_sum = scatter_pack(grid, [grad_w_gate, grad_w_out.reshape(count * rows, -1)])
        extra = jnp.concatenate(
            [
                grad_norm.reshape(count, rows),
                jnp.moveaxis(grad_kernel.reshape(taps, count, chans), 0, 1).reshape(count, -1),
                grad_bias.reshape(count, chans),
                grad_gain.reshape(count, outer),
                jnp.zeros((count, spare), F32),
            ],
            axis=1,
        ).reshape(count * rows, small_cols)
        grad_first = lax.dynamic_update_slice(grad_first, extra.astype(BF16), (0, at_small))
        left, right = scatter_pack(grid, [grad_first[:, :cut], grad_first[:, cut:]])
        extra = right[:, at_small - cut : at_small - cut + small_cols].reshape(-1)
        owned[l] = (
            extra[:rows],
            gate_sum,
            jnp.concatenate([left, right[:, : XBC - cut]], axis=1),
            right[:, XBC - cut : at_small - cut],
            extra[rows:split].reshape(taps, chans),
            extra[split : split + chans],
            extra[split + chans : small],
            out_sum.reshape(outer, -1),
        )
    sums = grid.sum_all(jnp.stack(summed))

    def stacked(position):
        return jnp.stack([member[position] for member in owned])

    return (
        hidden,
        grad,
        stacked(0),
        stacked(1),
        stacked(2),
        stacked(3),
        stacked(4),
        stacked(5),
        sums[:, 0],
        sums[:, 1],
        sums[:, 2],
        stacked(6),
        stacked(7),
    )


def solution(mesh):
    return jax.shard_map(
        shards,
        mesh=mesh,
        in_specs=(
            P(("dp", "fsdp"), None),
            P(("dp", "fsdp")),
            P(("dp", "fsdp")),
            P(None, ("dp", "fsdp")),
            P(None, ("dp", "fsdp"), None),
            P(None, ("dp", "fsdp"), None),
            P(None, ("dp", "fsdp"), None),
            P(None, None, ("dp", "fsdp")),
            P(None, ("dp", "fsdp")),
            P(),
            P(),
            P(),
            P(None, ("dp", "fsdp")),
            P(None, ("dp", "fsdp"), None),
            P(("dp", "fsdp"), None),
        ),
        out_specs=(
            P(("dp", "fsdp"), None),
            P(("dp", "fsdp"), None),
            P(None, ("dp", "fsdp")),
            P(None, ("dp", "fsdp"), None),
            P(None, ("dp", "fsdp"), None),
            P(None, ("dp", "fsdp"), None),
            P(None, None, ("dp", "fsdp")),
            P(None, ("dp", "fsdp")),
            P(),
            P(),
            P(),
            P(None, ("dp", "fsdp")),
            P(None, ("dp", "fsdp"), None),
        ),
        check_vma=False,
    )
```

time: 778 us -> 523 us (0.67)
  starting transfers between devices: 249 us -> 103 us
  Pallas kernels: 0 us -> 137 us
  matrix products: 101 us -> 23.7 us
  local copies, waits for them, and re-layouts: 141 us -> 71.1 us
  other arithmetic: 133 us -> 76.2 us
  waiting for transfers between devices: 133 us -> 97.4 us
    ppermute x74 -> x0, starting transfers between devices: 147 us -> none  [the longest x72 135 us: hop(): return lax.ppermute(block, AXES, route)]
    pallas_call x0 -> x16, Pallas kernels: none -> 137 us  [call(): pl.pallas_call(body, out_shape=[jax.ShapeDtypeStruct(s, d) for s, d in ou...]
    dot_general x48 -> x10, matrix products: 101 us -> 23.7 us  [dot(): return jnp.dot(a, b, preferred_element_type=F32)]
    ppermute x74 -> x0, waiting for transfers between devices: 69.5 us -> none  [the longest x72 65 us: hop(): return lax.ppermute(block, AXES, route)]
    ppermute x75 -> x69, waiting for transfers between devices: 63.1 us -> 96.6 us  [swap(): return lax.ppermute(block, AXES, route)]
    reduce_sum x14 -> x2, other arithmetic: 24.3 us -> 0.23 us  [layer_backward(): skip_sum = jnp.sum(skip_grad.reshape(HEADS, HEAD_DIM), axis=1)]
    another operation x34 -> x19, other arithmetic: 25.2 us -> 5.92 us  [the longest x8 5.14 us: stacked(): return jnp.stack([member[position] for member in owned])]
    mul x25 -> x0, local copies, waits for them, and re-layouts: 17.7 us -> none  [the longest x6 5.96 us: layer_forward(): state_out = rise[..., None] * from_state]
  transfers between devices with their start and end apart: 165 -> 85, of which waited for: 43 -> 30; matrix products, arithmetic and copies ran while one was open for 41% -> 29% of each run, Pallas kernels for 0% -> 23%
where the time goes in v2:
time: 523 us; the launch traced here: 513 us
  Pallas kernels  137 us (26%)
  starting transfers between devices  103 us (20%)
  waiting for transfers between devices  97.4 us (19%)
  other arithmetic  76.2 us (15%)
  local copies, waits for them, and re-layouts  71.1 us (14%)
  matrix products  23.7 us (5%)
    pallas_call x16, Pallas kernels, call(): pl.pallas_call(body, out_shape=[jax.ShapeDtypeStruct(s, d) for s, d in ou...  137 us
    ppermute x69, waiting for transfers between devices, swap(): return lax.ppermute(block, AXES, route)  96.6 us
    ppermute x69, starting transfers between devices, swap(): return lax.ppermute(block, AXES, route)  79.9 us
    dot_general x10, matrix products, dot(): return jnp.dot(a, b, preferred_element_type=F32)  23.7 us
    ppermute x12, starting transfers between devices, state_chain(): got = lax.ppermute(leaving.astype(jnp.bfloat16), axis, [(at, at + way)])  17.5 us
    concatenate x33, other arithmetic, gather_step(): return jnp.concatenate([first, second], axis=axis)  17.3 us
    dynamic_slice x28, local copies, waits for them, and re-layouts, pick(): return lax.dynamic_slice_in_dim(block, index, 1, axis)  17.2 us
    convert_element_type x28, other arithmetic, scatter_step(): return (pick(digit).astype(wide) + got.astype(wide)).astype(kind)  17.2 us
  transfers between devices with their start and end apart: 85, of which 30 were waited for; matrix products, arithmetic and copies ran while one was open for 29% of the time, Pallas kernels for 23%

profile of v2, /device:TPU:0, one launch (start us, length us, event | category | flops | bytes accessed | tf_op | source)
XLA Modules:
  0.0 513.2 jit_solution(17050084597893785559)
XLA Ops:
  2.8 4.1 collective-permute-start.9
  12.7 5.2 %collective-permute-done = bf16[1,1,1,1,1,24,1920]{6,5,4,3,2,1,0:T(8,128)(2,1)S(1)} collective-permute-done((bf16[1,1,1,1,1,24,1920]{6,5,4,3,2,1,0:T(8,128)(2,1)S(1)}, bf16[1,1,1,1,1,24,1920]{6,5,4,3,2,1,0:T(8,128)(2,1)S(1)}, u32[]{:S(2)}, u32[]{:S(2)}) %collective-permute-start) | collective-permute-done | bytes 92192 | tf_op jit(solution)/shard_map/ppermute | solution.py:67
  20.2 5.4 %collective-permute-done.1 = bf16[2,1,1,1,1,24,1920]{6,5,4,3,2,1,0:T(8,128)(2,1)S(1)} collective-permute-done((bf16[2,1,1,1,1,24,1920]{6,5,4,3,2,1,0:T(8,128)(2,1)S(1)}, bf16[2,1,1,1,1,24,1920]{6,5,4,3,2,1,0:T(8,128)(2,1)S(1)}, u32[]{:S(2)}, u32[]{:S(2)}) %collective-permute-start.1) | collective-permute-done | bytes 184352 | tf_op jit(solution)/shard_map/ppermute | solution.py:67
  30.3 3.2 collective-permute-start.20
  35.1 2.6 collective-permute-done.20
  40.2 3.2 collective-permute-done.21
  43.5 2.9 collective-permute-start.29
  49.8 2.7 collective-permute-done.29
  53.5 2.6 collective-permute-done.11
  65.9 3.9 shard_map.246
  78.5 7.6 %shard_map.247 = (bf16[256,1536]{1,0:T(8,128)(2,1)S(1)}, bf16[256,128]{1,0:T(8,128)(2,1)S(1)}, bf16[256,128]{1,0:T(8,128)(2,1)S(1)}, f32[256,128]{1,0:T(8,128)S(...) custom-call(bf16[256,1792]{1,0:T(8,128)(2,1)} %get-tuple-element.87.conv_in, ...), custom_call_target="tpu_custom_call" | custom-call | flops 500000000 | bytes 2294784 | tf_op jit(solution)/shard_map/pallas_call | solution.py:229
  87.6 2.4 collective-permute-start.14
  90.1 8.2 %shard_map.248.y = f32[256,1536]{1,0:T(8,128)} custom-call(bf16[256,1536]{1,0:T(8,128)(2,1)S(1)} %get-tuple-element.89.x, bf16[256,128]{1,0:T(8,128)(2,1)S(1)} %get-tuple-element.90.keys, bf16[256,128]{1,0:T(8,128)(2,1)S(1)} %get-tuple-element.91.queries, f32[256,128]{1,0:T(8,128)S(1)} %get-tuple-element.92.step, f32[256,128]{1,0:T(8,128)S(1)} %get-tuple-element.93.cum, ...), custom_call_target="tpu_custom_call" | custom-call | flops 4000000000 | bytes 2365440 | tf_op jit(solution)/shard_map/pallas_call | solution.py:229
  101.4 7.0 %collective-permute-done.26 = bf16[2,2,1,2,1,24,896]{6,5,4,3,2,1,0:T(8,128)(2,1)S(1)} collective-permute-done((bf16[2,2,1,2,1,24,896]{6,5,4,3,2,1,0:T(8,128)(2,1)S(1)}, bf16[2,2,1,2,1,24,896]{6,5,4,3,2,1,0:T(8,128)(2,1)S(1)}, u32[]{:S(2)}, u32[]{:S(2)}) %collective-permute-start.26) | collective-permute-done | bytes 344096 | tf_op jit(solution)/shard_map/ppermute | solution.py:67
  115.2 4.5 collective-permute-done.31
  119.7 2.7 collective-permute-done.37
  132.5 4.8 reshape_reshape.12.w_out
  137.3 3.7 fusion.51.gate
  142.1 8.2 %shard_map.249 = (f32[256,1536]{1,0:T(8,128)}, bf16[256,1536]{1,0:T(8,128)(2,1)S(1)}, f32[256,768]{1,0:T(8,128)}) custom-call(f32[256,1536]{1,0:T(8,128)} %shard_map.248.y, f32[256,1536]{1,0:T(8,128)} %fusion.51.gate, bf16[256,128]{1,0:T(8,128)(2,1)S(1)} %get-tuple-element.91.queries, bf16[128,1536]{1,0:T(8,128)(2,1)S(1)} %multiply_convert_fusion.5.carried, ...), custom_call_target="tpu_custom_call" | custom-call | flops 2000000000 | bytes 8067072 | tf_op jit(solution)/shard_map/pallas_call | solution.py:229
  156.4 3.9 shard_map.250
  165.5 7.6 %shard_map.251 = (bf16[256,1536]{1,0:T(8,128)(2,1)S(1)}, bf16[256,128]{1,0:T(8,128)(2,1)S(1)}, bf16[256,128]{1,0:T(8,128)(2,1)S(1)}, f32[256,128]{1,0:T(8,128)S(...) custom-call(bf16[256,1792]{1,0:T(8,128)(2,1)} %get-tuple-element.102.conv_in, ...), custom_call_target="tpu_custom_call" | custom-call | flops 500000000 | bytes 2294784 | tf_op jit(solution)/shard_map/pallas_call | solution.py:229
  174.6 2.3 collective-permute-start.34
  180.1 8.2 %shard_map.252.y = f32[256,1536]{1,0:T(8,128)} custom-call(bf16[256,1536]{1,0:T(8,128)(2,1)S(1)} %get-tuple-element.104.x, bf16[256,128]{1,0:T(8,128)(2,1)S(1)} %get-tuple-element.105.keys, bf16[256,128]{1,0:T(8,128)(2,1)S(1)} %get-tuple-element.106.queries, f32[256,128]{1,0:T(8,128)S(1)} %get-tuple-element.107.step, f32[256,128]{1,0:T(8,128)S(1)} %get-tuple-element.108.cum, ...), custom_call_target="tpu_custom_call" | custom-call | flops 4000000000 | bytes 2365440 | tf_op jit(solution)/shard_map/pallas_call | solution.py:229
  194.3 4.7 reshape_reshape.13.w_out
  199.0 3.7 fusion.52.gate
  203.9 8.1 %shard_map.253 = (f32[256,1536]{1,0:T(8,128)}, bf16[256,1536]{1,0:T(8,128)(2,1)S(1)}, f32[256,768]{1,0:T(8,128)}) custom-call(f32[256,1536]{1,0:T(8,128)} %shard_map.252.y, f32[256,1536]{1,0:T(8,128)} %fusion.52.gate, bf16[256,128]{1,0:T(8,128)(2,1)S(1)} %get-tuple-element.106.queries, bf16[128,1536]{1,0:T(8,128)(2,1)S(1)} %multiply_convert_fusion.4.carried, ...), custom_call_target="tpu_custom_call" | custom-call | flops 2000000000 | bytes 8067072 | tf_op jit(solution)/shard_map/pallas_call | solution.py:229
  212.0 13.2 %shard_map.254 = (f32[1,1536]{1,0:T(1,128)S(1)}, bf16[256,1536]{1,0:T(8,128)(2,1)S(1)}, bf16[256,1536]{1,0:T(8,128)(2,1)}, f32[128,1536]{1,0:T(8,128)}, f32[256,...) custom-call(f32[256,768]{1,0:T(8,128)} %convert_element_type.480.grad, ...), custom_call_target="tpu_custom_call" | custom-call | flops 2000000000 | bytes 8853504 | tf_op jit(solution)/shard_map/pallas_call | solution.py:229
  228.8 2.2 convolution_convert_fusion
  231.1 4.7 reshape_reshape.15
  235.8 2.4 constant_dynamic-slice_fusion.3
  241.8 11.1 %shard_map.255 = (f32[256,1536]{1,0:T(8,128)}, f32[256,128]{1,0:T(8,128)S(1)}, f32[256,128]{1,0:T(8,128)S(1)}, f32[256,128]{1,0:T(8,128)S(1)}, f32[128,256]{1,0:T(8,128)S(1)}) custom-call(bf16[256,1536]{1,0:T(8,128)(2,1)S(1)} %copy-done.24, bf16[256,1536]{1,0:T(8,128)(2,1)} %copy-done.5, bf16[256,128]{1,0:T(8,128)(2,1)S(1)} %get-tuple-element.105.keys, ...), custom_call_target="tpu_custom_call" | custom-call | flops 8000000000 | bytes 3282944 | tf_op jit(solution)/shard_map/pallas_call | solution.py:229
  259.2 3.5 fusion.53.gate_part
  272.0 3.2 collective-permute-start.73
  277.4 10.8 %shard_map.256 = (f32[256,1792]{1,0:T(8,128)}, bf16[256,128]{1,0:T(8,128)(2,1)S(1)}, f32[1,128]{1,0:T(1,128)S(1)}, f32[1,128]{1,0:T(1,128)S(1)}, f32[1,1792]{1,0:T(1,128)S(1)}, /*index=5*/f32[4,1792]{1,0:T(4,128)S(1)}) custom-call(f32[128,1536]{1,0:T(8,128)} %convert_add_fusion.5.pending, bf16[128,1536]{1,0:T(8,128)(2,1)S(1)} %multiply_convert_fusion.4.carried, ...), custom_call_target="tpu_custom_call" | custom-call | flops 2000000000 | bytes 6816768 | tf_op jit(solution)/shard_map/pallas_call | solution.py:229
  293.4 5.4 %shard_map.257 = (bf16[256,1920]{1,0:T(8,128)(2,1)}, f32[256,768]{1,0:T(8,128)S(1)}, f32[1,768]{1,0:T(1,128)S(1)}) custom-call(f32[256,1792]{1,0:T(8,128)} %get-tuple-element.125.act_grad, f32[8,1792]{1,0:T(8,128)S(1)} %collective-permute-done.43.rim_grad, f32[4,1792]{1,0:T(4,128)S(1)} %reshape.180.weight, bf16[256,128]{1,0:T(8,128)(2,1)S(1)} %get-tuple-element.126.dt_low, ...), custom_call_target="tpu_custom_call" | custom-call | flops 2000000000 | bytes 7298048 | tf_op jit(solution)/shard_map/pallas_call | solution.py:229
  299.3 3.8 convolution_convert_fusion.4
  303.1 3.1 dynamic_update_slice.7
  306.2 2.5 slice.331
  308.8 2.7 slice.332
  311.5 2.2 convolution_convert_fusion.2
  313.7 4.7 reshape_reshape.14
  318.5 2.4 constant_dynamic-slice_fusion.10
  320.9 2.9 collective-permute-start.67
  323.7 13.2 %shard_map.258 = (f32[1,1536]{1,0:T(1,128)S(1)}, bf16[256,1536]{1,0:T(8,128)(2,1)S(1)}, bf16[256,1536]{1,0:T(8,128)(2,1)}, f32[128,1536]{1,0:T(8,128)}, f32[256,...) custom-call(f32[256,768]{1,0:T(8,128)} %copy-done.2, bf16[1536,768]{1,0:T(8,128)(2,1)} %reshape_reshape.12.w_out, ...), custom_call_target="tpu_custom_call" | custom-call | flops 2000000000 | bytes 8853504 | tf_op jit(solution)/shard_map/pallas_call | solution.py:229
  344.8 11.2 %shard_map.259 = (f32[256,1536]{1,0:T(8,128)}, f32[256,128]{1,0:T(8,128)S(1)}, f32[256,128]{1,0:T(8,128)S(1)}, f32[256,128]{1,0:T(8,128)S(1)}, f32[128,256]{1,0:T(8,128)S(1)}) custom-call(bf16[256,1536]{1,0:T(8,128)(2,1)S(1)} %copy-done.23, bf16[256,1536]{1,0:T(8,128)(2,1)} %copy-done.3, bf16[256,128]{1,0:T(8,128)(2,1)S(1)} %copy-done.28, ...), custom_call_target="tpu_custom_call" | custom-call | flops 8000000000 | bytes 3282944 | tf_op jit(solution)/shard_map/pallas_call | solution.py:229
  362.8 3.5 collective-permute-start.77
  367.6 5.6 %collective-permute-start.57 = (bf16[2,2,2,1,1,24,896]{6,5,4,3,2,1,0:T(8,128)(2,1)S(1)}, bf16[2,2,2,1,1,24,896]{6,5,4,3,2,1,0:T(8,128)(2,1)S(1)}, u32[]{:S(2)}, u32[]{:S(2)}) collective-permute-start(bf16[2,2,2,1,1,24,896]{6,5,4,3,2,1,0:T(8,128)(2,1)S(1)} %constant_dynamic-slice_fusion.19), channel_id=1, source_target_pairs={{0,2},{1,3},{2,0},{3,1},{4,6},{5,7},{6,4},{7,5},{8,10},{9,11},{10,... | collective-permute-start | bytes 1032200 | tf_op jit(solution)/shard_map/ppermute | solution.py:67
  374.4 3.1 collective-permute-done.77
  380.0 4.2 collective-permute-done.57
  386.9 5.8 %collective-permute-done.78 = bf16[2,1,1,1,1,24,3072]{6,5,4,3,2,1,0:T(8,128)(2,1)S(1)} collective-permute-done((bf16[2,1,1,1,1,24,3072]{6,5,4,3,2,1,0:T(8,128)(2,1)S(1)}, bf16[2,1,1,1,1,24,3072]{6,5,4,3,2,1,0:T(8,128)(2,1)S(1)}, u32[]{:S(2)}, u32[]{:S(2)}) %collective-permute-start.78) | collective-permute-done | bytes 294944 | tf_op jit(solution)/shard_map/ppermute | solution.py:67
  394.2 2.8 collective-permute-start.79
  402.1 11.0 %shard_map.260 = (f32[256,1792]{1,0:T(8,128)}, bf16[256,128]{1,0:T(8,128)(2,1)S(1)}, f32[1,128]{1,0:T(1,128)S(1)}, f32[1,128]{1,0:T(1,128)S(1)}, f32[1,1792]{1,0:T(1,128)S(1)}, /*index=5*/f32[4,1792]{1,0:T(4,128)S(1)}) custom-call(f32[128,1536]{1,0:T(8,128)} %convert_add_fusion.4.pending, bf16[128,1536]{1,0:T(8,128)(2,1)S(1)} %multiply_convert_fusion.5.carried, ...), custom_call_target="tpu_custom_call" | custom-call | flops 2000000000 | bytes 6816768 | tf_op jit(solution)/shard_map/pallas_call | solution.py:229
  416.6 2.7 collective-permute-done.81
  428.0 3.2 collective-permute-done.84
  433.1 2.6 collective-permute-start.61
  437.5 5.7 %shard_map.261 = (bf16[256,1920]{1,0:T(8,128)(2,1)}, f32[256,768]{1,0:T(8,128)}, f32[1,768]{1,0:T(1,128)S(1)}) custom-call(f32[256,1792]{1,0:T(8,128)} %get-tuple-element.139.act_grad, f32[8,1792]{1,0:T(8,128)S(1)} %collective-permute-done.47.rim_grad, f32[4,1792]{1,0:T(4,128)S(1)} %reshape.169.weight, bf16[256,128]{1,0:T(8,128)(2,1)S(1)} %get-tuple-element.140.dt_low, ...), custom_call_target="tpu_custom_call" | custom-call | flops 2000000000 | bytes 7298048 | tf_op jit(solution)/shard_map/pallas_call | solution.py:229
  445.8 2.4 dynamic_update_slice.6
  455.9 4.1 collective-permute-done.62
  462.5 4.7 collective-permute-done.63
  476.3 2.7 collective-permute-done.69
  484.0 5.4 %collective-permute-done.70 = bf16[2,1,1,1,1,24,3072]{6,5,4,3,2,1,0:T(8,128)(2,1)S(1)} collective-permute-done((bf16[2,1,1,1,1,24,3072]{6,5,4,3,2,1,0:T(8,128)(2,1)S(1)}, bf16[2,1,1,1,1,24,3072]{6,5,4,3,2,1,0:T(8,128)(2,1)S(1)}, u32[]{:S(2)}, u32[]{:S(2)}) %collective-permute-start.70) | collective-permute-done | bytes 294944 | tf_op jit(solution)/shard_map/ppermute | solution.py:67
  491.2 5.0 collective-permute-done.71
  497.2 4.8 collective-permute-done.54
  504.9 3.6 collective-permute-done.55
  (694 shorter events, 196.8 us)
Async XLA Ops:
  2.8 15.9 %collective-permute-start.9 = (bf16[1,1,1,1,1,24,3072]{6,5,4,3,2,1,0:T(8,128)(2,1)S(1)}, bf16[1,1,1,1,1,24,3072]{6,5,4,3,2,1,0:T(8,128)(2,1)S(1)}, u32[]{:S(2)}, u32[]{:S(2)}) collective-permute-start(bf16[1,1,1,1,1,24,3072]{6,5,4,3,2,1,0:T(8,128)(2,1)S(1)} %get-tuple-element.95), channel_id=1, source_target_pairs={{0,16},{1,17},{2,18},{3,19},{4,20},{5,21},{6,22},{7,23},{8,24},{9,... | collective-permute-start | bytes 442376 | tf_op jit(solution)/shard_map/ppermute | solution.py:67
  7.5 10.4 %collective-permute-start = (bf16[1,1,1,1,1,24,1920]{6,5,4,3,2,1,0:T(8,128)(2,1)S(1)}, bf16[1,1,1,1,1,24,1920]{6,5,4,3,2,1,0:T(8,128)(2,1)S(1)}, u32[]{:S(2)}, u32[]{:S(2)}) collective-permute-start(bf16[1,1,1,1,1,24,1920]{6,5,4,3,2,1,0:T(8,128)(2,1)S(1)} %bitcast.176), channel_id=1, source_target_pairs={{0,16},{1,17},{2,18},{3,19},{4,20},{5,21},{6,22},{7,23},{8,24},{9,... | collective-permute-start | bytes 276488 | tf_op jit(solution)/shard_map/ppermute | solution.py:67
  17.9 7.6 %collective-permute-start.1 = (bf16[2,1,1,1,1,24,1920]{6,5,4,3,2,1,0:T(8,128)(2,1)S(1)}, bf16[2,1,1,1,1,24,1920]{6,5,4,3,2,1,0:T(8,128)(2,1)S(1)}, u32[]{:S(2)}, u32[]{:S(2)}) collective-permute-start(bf16[2,1,1,1,1,24,1920]{6,5,4,3,2,1,0:T(8,128)(2,1)S(1)} %pad_maximum_fusion.33), channel_id=1, source_target_pairs={{0,8},{1,9},{2,10},{3,11},{4,12},{5,13},{6,14},{7,15},{8,0},{9,1},... | collective-permute-start | bytes 552968 | tf_op jit(solution)/shard_map/ppermute | solution.py:67
  18.8 11.4 %collective-permute-start.10 = (bf16[2,1,1,1,1,24,3072]{6,5,4,3,2,1,0:T(8,128)(2,1)S(1)}, bf16[2,1,1,1,1,24,3072]{6,5,4,3,2,1,0:T(8,128)(2,1)S(1)}, u32[]{:S(2)}, u32[]{:S(2)}) collective-permute-start(bf16[2,1,1,1,1,24,3072]{6,5,4,3,2,1,0:T(8,128)(2,1)S(1)} %pad_maximum_fusion.29), channel_id=1, source_target_pairs={{0,8},{1,9},{2,10},{3,11},{4,12},{5,13},{6,14},{7,15},{8,0},{9,1},... | collective-permute-start | bytes 884744 | tf_op jit(solution)/shard_map/ppermute | solution.py:67
  25.7 7.8 %collective-permute-start.5 = (bf16[2,2,1,1,1,24,896]{6,5,4,3,2,1,0:T(8,128)(2,1)S(1)}, bf16[2,2,1,1,1,24,896]{6,5,4,3,2,1,0:T(8,128)(2,1)S(1)}, u32[]{:S(2)}, u32[]{:S(2)}) collective-permute-start(bf16[2,2,1,1,1,24,896]{6,5,4,3,2,1,0:T(8,128)(2,1)S(1)} %fusion.21), channel_id=1, source_target_pairs={{0,2},{1,3},{2,0},{3,1},{4,6},{5,7},{6,4},{7,5},{8,10},{9,11},{10,... | collective-permute-start | bytes 516104 | tf_op jit(solution)/shard_map/ppermute | solution.py:67
  27.3 11.2 %collective-permute-start.2 = (bf16[2,2,1,1,1,24,1024]{6,5,4,3,2,1,0:T(8,128)(2,1)S(1)}, bf16[2,2,1,1,1,24,1024]{6,5,4,3,2,1,0:T(8,128)(2,1)S(1)}, u32[]{:S(2)}, u32[]{:S(2)}) collective-permute-start(bf16[2,2,1,1,1,24,1024]{6,5,4,3,2,1,0:T(8,128)(2,1)S(1)} %fusion.16), channel_id=1, source_target_pairs={{0,4},{1,5},{2,6},{3,7},{4,0},{5,1},{6,2},{7,3},{8,12},{9,13},{10,... | collective-permute-start | bytes 589832 | tf_op jit(solution)/shard_map/ppermute | solution.py:67
  33.5 12.9 %collective-permute-start.6 = (bf16[2,2,1,2,1,24,896]{6,5,4,3,2,1,0:T(8,128)(2,1)S(1)}, bf16[2,2,1,2,1,24,896]{6,5,4,3,2,1,0:T(8,128)(2,1)S(1)}, u32[]{:S(2)}, u32[]{:S(2)}) collective-permute-start(bf16[2,2,1,2,1,24,896]{6,5,4,3,2,1,0:T(8,128)(2,1)S(1)} %pad_maximum_fusion.26), channel_id=1, source_target_pairs={{0,4},{1,5},{2,6},{3,7},{4,0},{5,1},{6,2},{7,3},{8,12},{9,13},{10,... | collective-permute-start | bytes 1032200 | tf_op jit(solution)/shard_map/ppermute | solution.py:67
  38.6 14.7 %collective-permute-start.3 = (bf16[2,2,2,1,1,24,1024]{6,5,4,3,2,1,0:T(8,128)(2,1)S(1)}, bf16[2,2,2,1,1,24,1024]{6,5,4,3,2,1,0:T(8,128)(2,1)S(1)}, u32[]{:S(2)}, u32[]{:S(2)}) collective-permute-start(bf16[2,2,2,1,1,24,1024]{6,5,4,3,2,1,0:T(8,128)(2,1)S(1)} %pad_maximum_fusion.23), channel_id=1, source_target_pairs={{0,2},{1,3},{2,0},{3,1},{4,6},{5,7},{6,4},{7,5},{8,10},{9,11},{10,... | collective-permute-start | bytes 1179656 | tf_op jit(solution)/shard_map/ppermute | solution.py:67
  43.5 9.0 %collective-permute-start.29 = (bf16[1,1,1,1,1,24,3072]{6,5,4,3,2,1,0:T(8,128)(2,1)S(1)}, bf16[1,1,1,1,1,24,3072]{6,5,4,3,2,1,0:T(8,128)(2,1)S(1)}, u32[]{:S(2)}, u32[]{:S(2)}) collective-permute-start(bf16[1,1,1,1,1,24,3072]{6,5,4,3,2,1,0:T(8,128)(2,1)S(1)} %get-tuple-element.110), channel_id=1, source_target_pairs={{0,16},{1,17},{2,18},{3,19},{4,20},{5,21},{6,22},{7,23},{8,24},{9,... | collective-permute-start | bytes 442376 | tf_op jit(solution)/shard_map/ppermute | solution.py:67
  46.6 15.8 %collective-permute-start.7 = (bf16[2,2,2,2,1,24,896]{6,5,4,3,2,1,0:T(8,128)(2,1)S(1)}, bf16[2,2,2,2,1,24,896]{6,5,4,3,2,1,0:T(8,128)(2,1)S(1)}, u32[]{:S(2)}, u32[]{:S(2)}) collective-permute-start(bf16[2,2,2,2,1,24,896]{6,5,4,3,2,1,0:T(8,128)(2,1)S(1)} %pad_maximum_fusion.14), channel_id=1, source_target_pairs={{0,1},{1,0},{2,3},{3,2},{4,5},{5,4},{6,7},{7,6},{8,9},{9,8},{10,11... | collective-permute-start | bytes 2064392 | tf_op jit(solution)/shard_map/ppermute | solution.py:67
  46.7 9.5 %collective-permute-start.11 = (bf16[2,2,1,1,1,24,1536]{6,5,4,3,2,1,0:T(8,128)(2,1)S(1)}, bf16[2,2,1,1,1,24,1536]{6,5,4,3,2,1,0:T(8,128)(2,1)S(1)}, u32[]{:S(2)}, u32[]{:S(2)}) collective-permute-start(bf16[2,2,1,1,1,24,1536]{6,5,4,3,2,1,0:T(8,128)(2,1)S(1)} %get-tuple-element.214), channel_id=1, source_target_pairs={{0,2},{1,3},{2,0},{3,1},{4,6},{5,7},{6,4},{7,5},{8,10},{9,11},{10,... | collective-permute-start | bytes 884744 | tf_op jit(solution)/shard_map/ppermute | solution.py:67
  48.3 9.1 %collective-permute-start.17 = (bf16[2,2,1,1,1,24,1536]{6,5,4,3,2,1,0:T(8,128)(2,1)S(1)}, bf16[2,2,1,1,1,24,1536]{6,5,4,3,2,1,0:T(8,128)(2,1)S(1)}, u32[]{:S(2)}, u32[]{:S(2)}) collective-permute-start(bf16[2,2,1,1,1,24,1536]{6,5,4,3,2,1,0:T(8,128)(2,1)S(1)} %get-tuple-element.213), channel_id=1, source_target_pairs={{0,4},{1,5},{2,6},{3,7},{4,0},{5,1},{6,2},{7,3},{8,12},{9,13},{10,... | collective-permute-start | bytes 884744 | tf_op jit(solution)/shard_map/ppermute | solution.py:67
  52.5 8.9 %collective-permute-start.30 = (bf16[2,1,1,1,1,24,3072]{6,5,4,3,2,1,0:T(8,128)(2,1)S(1)}, bf16[2,1,1,1,1,24,3072]{6,5,4,3,2,1,0:T(8,128)(2,1)S(1)}, u32[]{:S(2)}, u32[]{:S(2)}) collective-permute-start(bf16[2,1,1,1,1,24,3072]{6,5,4,3,2,1,0:T(8,128)(2,1)S(1)} %pad_maximum_fusion.30), channel_id=1, source_target_pairs={{0,8},{1,9},{2,10},{3,11},{4,12},{5,13},{6,14},{7,15},{8,0},{9,1},... | collective-permute-start | bytes 884744 | tf_op jit(solution)/shard_map/ppermute | solution.py:67
  53.4 10.4 %collective-permute-start.4 = (bf16[2,2,2,2,1,24,1024]{6,5,4,3,2,1,0:T(8,128)(2,1)S(1)}, bf16[2,2,2,2,1,24,1024]{6,5,4,3,2,1,0:T(8,128)(2,1)S(1)}, u32[]{:S(2)}, u32[]{:S(2)}) collective-permute-start(bf16[2,2,2,2,1,24,1024]{6,5,4,3,2,1,0:T(8,128)(2,1)S(1)} %pad_maximum_fusion.12), channel_id=1, source_target_pairs={{0,1},{1,0},{2,3},{3,2},{4,5},{5,4},{6,7},{7,6},{8,9},{9,8},{10,11... | collective-permute-start | bytes 2359304 | tf_op jit(solution)/shard_map/ppermute | solution.py:67
  58.5 14.9 %collective-permute-start.12 = (bf16[2,2,1,2,1,24,1536]{6,5,4,3,2,1,0:T(8,128)(2,1)}, bf16[2,2,1,2,1,24,1536]{6,5,4,3,2,1,0:T(8,128)(2,1)}, u32[]{:S(2)}, u32[]{:S(2)}) collective-permute-start(bf16[2,2,1,2,1,24,1536]{6,5,4,3,2,1,0:T(8,128)(2,1)} %pad_maximum_fusion.17), channel_id=1, source_target_pairs={{0,4},{1,5},{2,6},{3,7},{4,0},{5,1},{6,2},{7,3},{8,12},{9,13},{10,... | collective-permute-start | bytes 1769480 | tf_op jit(solution)/shard_map/ppermute | solution.py:67
  60.9 16.2 %collective-permute-start.18 = (bf16[2,2,2,1,1,24,1536]{6,5,4,3,2,1,0:T(8,128)(2,1)}, bf16[2,2,2,1,1,24,1536]{6,5,4,3,2,1,0:T(8,128)(2,1)}, u32[]{:S(2)}, u32[]{:S(2)}) collective-permute-start(bf16[2,2,2,1,1,24,1536]{6,5,4,3,2,1,0:T(8,128)(2,1)} %pad_maximum_fusion.18), channel_id=1, source_target_pairs={{0,2},{1,3},{2,0},{3,1},{4,6},{5,7},{6,4},{7,5},{8,10},{9,11},{10,... | collective-permute-start | bytes 1769480 | tf_op jit(solution)/shard_map/ppermute | solution.py:67
  70.6 7.8 %collective-permute-start.8 = (bf16[8,1792]{1,0:T(8,128)(2,1)S(1)}, bf16[8,1792]{1,0:T(8,128)(2,1)S(1)}, u32[]{:S(2)}, u32[]{:S(2)}) collective-permute-start(bf16[8,1792]{1,0:T(8,128)(2,1)S(1)} %slice.251), channel_id=1, source_target_pairs={{0,1},{1,2},{2,3},{4,5},{5,6},{6,7},{8,9},{9,10},{10,11},{12,13},{... | collective-permute-start | bytes 86024 | tf_op jit(solution)/shard_map/ppermute | solution.py:23
  74.8 55.1 %collective-permute-start.13 = (bf16[2,2,2,2,1,24,1536]{6,5,4,3,2,1,0:T(8,128)(2,1)S(1)}, bf16[2,2,2,2,1,24,1536]{6,5,4,3,2,1,0:T(8,128)(2,1)S(1)}, u32[]{:S(2)}, u32[]{:S(2)}) collective-permute-start(bf16[2,2,2,2,1,24,1536]{6,5,4,3,2,1,0:T(8,128)(2,1)S(1)} %pad_maximum_fusion.8), channel_id=1, source_target_pairs={{0,1},{1,0},{2,3},{3,2},{4,5},{5,4},{6,7},{7,6},{8,9},{9,8},{10,11... | collective-permute-start | bytes 3538952 | tf_op jit(solution)/shard_map/ppermute | solution.py:67
  76.0 22.9 %collective-permute-start.25 = (bf16[2,2,1,1,1,24,896]{6,5,4,3,2,1,0:T(8,128)(2,1)S(1)}, bf16[2,2,1,1,1,24,896]{6,5,4,3,2,1,0:T(8,128)(2,1)S(1)}, u32[]{:S(2)}, u32[]{:S(2)}) collective-permute-start(bf16[2,2,1,1,1,24,896]{6,5,4,3,2,1,0:T(8,128)(2,1)S(1)} %slice.272), channel_id=1, source_target_pairs={{0,2},{1,3},{2,0},{3,1},{4,6},{5,7},{6,4},{7,5},{8,10},{9,11},{10,... | collective-permute-start | bytes 516104 | tf_op jit(solution)/shard_map/ppermute | solution.py:67
  76.0 24.0 %collective-permute-start.22 = (bf16[2,2,1,1,1,24,1024]{6,5,4,3,2,1,0:T(8,128)(2,1)S(1)}, bf16[2,2,1,1,1,24,1024]{6,5,4,3,2,1,0:T(8,128)(2,1)S(1)}, u32[]{:S(2)}, u32[]{:S(2)}) collective-permute-start(bf16[2,2,1,1,1,24,1024]{6,5,4,3,2,1,0:T(8,128)(2,1)S(1)} %slice.269), channel_id=1, source_target_pairs={{0,4},{1,5},{2,6},{3,7},{4,0},{5,1},{6,2},{7,3},{8,12},{9,13},{10,... | collective-permute-start | bytes 589832 | tf_op jit(solution)/shard_map/ppermute | solution.py:67
  78.4 48.0 %collective-permute-start.19 = (bf16[2,2,2,2,1,24,1536]{6,5,4,3,2,1,0:T(8,128)(2,1)S(1)}, bf16[2,2,2,2,1,24,1536]{6,5,4,3,2,1,0:T(8,128)(2,1)S(1)}, u32[]{:S(2)}, u32[]{:S(2)}) collective-permute-start(bf16[2,2,2,2,1,24,1536]{6,5,4,3,2,1,0:T(8,128)(2,1)S(1)} %pad_maximum_fusion.9), channel_id=1, source_target_pairs={{0,1},{1,0},{2,3},{3,2},{4,5},{5,4},{6,7},{7,6},{8,9},{9,8},{10,11... | collective-permute-start | bytes 3538952 | tf_op jit(solution)/shard_map/ppermute | solution.py:67
  87.6 12.8 %collective-permute-start.14 = (bf16[128,1536]{1,0:T(8,128)(2,1)S(1)}, bf16[128,1536]{1,0:T(8,128)(2,1)S(1)}, u32[]{:S(2)}, u32[]{:S(2)}) collective-permute-start(bf16[128,1536]{1,0:T(8,128)(2,1)S(1)} %add_convert_fusion.17), channel_id=1, source_target_pairs={{0,1},{4,5},{8,9},{12,13},{16,17},{20,21},{24,25},{28,29}} | collective-permute-start | bytes 1179656 | tf_op jit(solution)/shard_map/ppermute | solution.py:176
  99.0 9.4 %collective-permute-start.26 = (bf16[2,2,1,2,1,24,896]{6,5,4,3,2,1,0:T(8,128)(2,1)S(1)}, bf16[2,2,1,2,1,24,896]{6,5,4,3,2,1,0:T(8,128)(2,1)S(1)}, u32[]{:S(2)}, u32[]{:S(2)}) collective-permute-start(bf16[2,2,1,2,1,24,896]{6,5,4,3,2,1,0:T(8,128)(2,1)S(1)} %pad_maximum_fusion.27), channel_id=1, source_target_pairs={{0,4},{1,5},{2,6},{3,7},{4,0},{5,1},{6,2},{7,3},{8,12},{9,13},{10,... | collective-permute-start | bytes 1032200 | tf_op jit(solution)/shard_map/ppermute | solution.py:67
  100.1 10.2 %collective-permute-start.23 = (bf16[2,2,2,1,1,24,1024]{6,5,4,3,2,1,0:T(8,128)(2,1)S(1)}, bf16[2,2,2,1,1,24,1024]{6,5,4,3,2,1,0:T(8,128)(2,1)S(1)}, u32[]{:S(2)}, u32[]{:S(2)}) collective-permute-start(bf16[2,2,2,1,1,24,1024]{6,5,4,3,2,1,0:T(8,128)(2,1)S(1)} %pad_maximum_fusion.24), channel_id=1, source_target_pairs={{0,2},{1,3},{2,0},{3,1},{4,6},{5,7},{6,4},{7,5},{8,10},{9,11},{10,... | collective-permute-start | bytes 1179656 | tf_op jit(solution)/shard_map/ppermute | solution.py:67
  100.6 13.0 %collective-permute-start.15 = (bf16[128,1536]{1,0:T(8,128)(2,1)S(1)}, bf16[128,1536]{1,0:T(8,128)(2,1)S(1)}, u32[]{:S(2)}, u32[]{:S(2)}) collective-permute-start(bf16[128,1536]{1,0:T(8,128)(2,1)S(1)} %fusion.2), channel_id=1, source_target_pairs={{1,2},{5,6},{9,10},{13,14},{17,18},{21,22},{25,26},{29,30}} | collective-permute-start | bytes 1179656 | tf_op jit(solution)/shard_map/ppermute | solution.py:176
  109.5 40.8 %collective-permute-start.27 = (bf16[2,2,2,2,1,24,896]{6,5,4,3,2,1,0:T(8,128)(2,1)}, bf16[2,2,2,2,1,24,896]{6,5,4,3,2,1,0:T(8,128)(2,1)}, u32[]{:S(2)}, u32[]{:S(2)}) collective-permute-start(bf16[2,2,2,2,1,24,896]{6,5,4,3,2,1,0:T(8,128)(2,1)} %pad_maximum_fusion.15), channel_id=1, source_target_pairs={{0,1},{1,0},{2,3},{3,2},{4,5},{5,4},{6,7},{7,6},{8,9},{9,8},{10,11... | collective-permute-start | bytes 2064392 | tf_op jit(solution)/shard_map/ppermute | solution.py:67
  110.2 9.5 %collective-permute-start.31 = (bf16[2,2,1,1,1,24,1536]{6,5,4,3,2,1,0:T(8,128)(2,1)S(1)}, bf16[2,2,1,1,1,24,1536]{6,5,4,3,2,1,0:T(8,128)(2,1)S(1)}, u32[]{:S(2)}, u32[]{:S(2)}) collective-permute-start(bf16[2,2,1,1,1,24,1536]{6,5,4,3,2,1,0:T(8,128)(2,1)S(1)} %get-tuple-element.208), channel_id=1, source_target_pairs={{0,2},{1,3},{2,0},{3,1},{4,6},{5,7},{6,4},{7,5},{8,10},{9,11},{10,... | collective-permute-start | bytes 884744 | tf_op jit(solution)/shard_map/ppermute | solution.py:67
  113.5 8.9 %collective-permute-start.37 = (bf16[2,2,1,1,1,24,1536]{6,5,4,3,2,1,0:T(8,128)(2,1)S(1)}, bf16[2,2,1,1,1,24,1536]{6,5,4,3,2,1,0:T(8,128)(2,1)S(1)}, u32[]{:S(2)}, u32[]{:S(2)}) collective-permute-start(bf16[2,2,1,1,1,24,1536]{6,5,4,3,2,1,0:T(8,128)(2,1)S(1)} %get-tuple-element.207), channel_id=1, source_target_pairs={{0,4},{1,5},{2,6},{3,7},{4,0},{5,1},{6,2},{7,3},{8,12},{9,13},{10,... | collective-permute-start | bytes 884744 | tf_op jit(solution)/shard_map/ppermute | solution.py:67
  119.7 33.4 %collective-permute-start.24 = (bf16[2,2,2,2,1,24,1024]{6,5,4,3,2,1,0:T(8,128)(2,1)}, bf16[2,2,2,2,1,24,1024]{6,5,4,3,2,1,0:T(8,128)(2,1)}, u32[]{:S(2)}, u32[]{:S(2)}) collective-permute-start(bf16[2,2,2,2,1,24,1024]{6,5,4,3,2,1,0:T(8,128)(2,1)} %pad_maximum_fusion.13), channel_id=1, source_target_pairs={{0,1},{1,0},{2,3},{3,2},{4,5},{5,4},{6,7},{7,6},{8,9},{9,8},{10,11... | collective-permute-start | bytes 2359304 | tf_op jit(solution)/shard_map/ppermute | solution.py:67
  122.4 18.5 %collective-permute-start.16 = (bf16[128,1536]{1,0:T(8,128)(2,1)}, bf16[128,1536]{1,0:T(8,128)(2,1)}, u32[]{:S(2)}, u32[]{:S(2)}) collective-permute-start(bf16[128,1536]{1,0:T(8,128)(2,1)} %add_convert_fusion.16), channel_id=1, source_target_pairs={{2,3},{6,7},{10,11},{14,15},{18,19},{22,23},{26,27},{30,31}} | collective-permute-start | bytes 1179656 | tf_op jit(solution)/shard_map/ppermute | solution.py:176
  126.4 36.4 %collective-permute-start.38 = (bf16[2,2,2,1,1,24,1536]{6,5,4,3,2,1,0:T(8,128)(2,1)}, bf16[2,2,2,1,1,24,1536]{6,5,4,3,2,1,0:T(8,128)(2,1)}, u32[]{:S(2)}, u32[]{:S(2)}) collective-permute-start(bf16[2,2,2,1,1,24,1536]{6,5,4,3,2,1,0:T(8,128)(2,1)} %pad_maximum_fusion.21), channel_id=1, source_target_pairs={{0,2},{1,3},{2,0},{3,1},{4,6},{5,7},{6,4},{7,5},{8,10},{9,11},{10,... | collective-permute-start | bytes 1769480 | tf_op jit(solution)/shard_map/ppermute | solution.py:67
  129.9 47.1 %collective-permute-start.32 = (bf16[2,2,1,2,1,24,1536]{6,5,4,3,2,1,0:T(8,128)(2,1)}, bf16[2,2,1,2,1,24,1536]{6,5,4,3,2,1,0:T(8,128)(2,1)}, u32[]{:S(2)}, u32[]{:S(2)}) collective-permute-start(bf16[2,2,1,2,1,24,1536]{6,5,4,3,2,1,0:T(8,128)(2,1)} %pad_maximum_fusion.20), channel_id=1, source_target_pairs={{0,4},{1,5},{2,6},{3,7},{4,0},{5,1},{6,2},{7,3},{8,12},{9,13},{10,... | collective-permute-start | bytes 1769480 | tf_op jit(solution)/shard_map/ppermute | solution.py:67
  164.1 26.5 %collective-permute-start.39 = (bf16[2,2,2,2,1,24,1536]{6,5,4,3,2,1,0:T(8,128)(2,1)S(1)}, bf16[2,2,2,2,1,24,1536]{6,5,4,3,2,1,0:T(8,128)(2,1)S(1)}, u32[]{:S(2)}, u32[]{:S(2)}) collective-permute-start(bf16[2,2,2,2,1,24,1536]{6,5,4,3,2,1,0:T(8,128)(2,1)S(1)} %pad_maximum_fusion.11), channel_id=1, source_target_pairs={{0,1},{1,0},{2,3},{3,2},{4,5},{5,4},{6,7},{7,6},{8,9},{9,8},{10,11... | collective-permute-start | bytes 3538952 | tf_op jit(solution)/shard_map/ppermute | solution.py:67
  178.2 14.2 %collective-permute-start.33 = (bf16[2,2,2,2,1,24,1536]{6,5,4,3,2,1,0:T(8,128)(2,1)S(1)}, bf16[2,2,2,2,1,24,1536]{6,5,4,3,2,1,0:T(8,128)(2,1)S(1)}, u32[]{:S(2)}, u32[]{:S(2)}) collective-permute-start(bf16[2,2,2,2,1,24,1536]{6,5,4,3,2,1,0:T(8,128)(2,1)S(1)} %pad_maximum_fusion.10), channel_id=1, source_target_pairs={{0,1},{1,0},{2,3},{3,2},{4,5},{5,4},{6,7},{7,6},{8,9},{9,8},{10,11... | collective-permute-start | bytes 3538952 | tf_op jit(solution)/shard_map/ppermute | solution.py:67
  179.3 8.9 %collective-permute-start.35 = (bf16[128,1536]{1,0:T(8,128)(2,1)S(1)}, bf16[128,1536]{1,0:T(8,128)(2,1)S(1)}, u32[]{:S(2)}, u32[]{:S(2)}) collective-permute-start(bf16[128,1536]{1,0:T(8,128)(2,1)S(1)} %fusion.4), channel_id=1, source_target_pairs={{1,2},{5,6},{9,10},{13,14},{17,18},{21,22},{25,26},{29,30}} | collective-permute-start | bytes 1179656 | tf_op jit(solution)/shard_map/ppermute | solution.py:176
  189.2 13.5 %collective-permute-start.36 = (bf16[128,1536]{1,0:T(8,128)(2,1)}, bf16[128,1536]{1,0:T(8,128)(2,1)}, u32[]{:S(2)}, u32[]{:S(2)}) collective-permute-start(bf16[128,1536]{1,0:T(8,128)(2,1)} %add_convert_fusion.14), channel_id=1, source_target_pairs={{2,3},{6,7},{10,11},{14,15},{18,19},{22,23},{26,27},{30,31}} | collective-permute-start | bytes 1179656 | tf_op jit(solution)/shard_map/ppermute | solution.py:176
  227.2 28.4 %collective-permute-start.40 = (bf16[128,1536]{1,0:T(8,128)(2,1)}, bf16[128,1536]{1,0:T(8,128)(2,1)}, u32[]{:S(2)}, u32[]{:S(2)}) collective-permute-start(bf16[128,1536]{1,0:T(8,128)(2,1)} %multiply_convert_fusion.3), channel_id=1, source_target_pairs={{3,2},{7,6},{11,10},{15,14},{19,18},{23,22},{27,26},{31,30}} | collective-permute-start | bytes 1179656 | tf_op jit(solution)/shard_map/ppermute | solution.py:176
  238.2 27.1 %collective-permute-start.75 = (bf16[2,2,2,2,1,24,1536]{6,5,4,3,2,1,0:T(8,128)(2,1)}, bf16[2,2,2,2,1,24,1536]{6,5,4,3,2,1,0:T(8,128)(2,1)}, u32[]{:S(2)}, u32[]{:S(2)}) collective-permute-start(bf16[2,2,2,2,1,24,1536]{6,5,4,3,2,1,0:T(8,128)(2,1)} %constant_dynamic-slice_fusion.3), channel_id=1, source_target_pairs={{0,1},{1,0},{2,3},{3,2},{4,5},{5,4},{6,7},{7,6},{8,9},{9,8},{10,11... | collective-permute-start | bytes 3538952 | tf_op jit(solution)/shard_map/ppermute | solution.py:67
  241.2 28.2 %collective-permute-start.72 = (bf16[2,2,2,2,1,24,1536]{6,5,4,3,2,1,0:T(8,128)(2,1)}, bf16[2,2,2,2,1,24,1536]{6,5,4,3,2,1,0:T(8,128)(2,1)}, u32[]{:S(2)}, u32[]{:S(2)}) collective-permute-start(bf16[2,2,2,2,1,24,1536]{6,5,4,3,2,1,0:T(8,128)(2,1)} %constant_dynamic-slice_fusion.6), channel_id=1, source_target_pairs={{0,1},{1,0},{2,3},{3,2},{4,5},{5,4},{6,7},{7,6},{8,9},{9,8},{10,11... | collective-permute-start | bytes 3538952 | tf_op jit(solution)/shard_map/ppermute | solution.py:67
  264.0 11.2 %collective-permute-start.42 = (bf16[128,1536]{1,0:T(8,128)(2,1)S(1)}, bf16[128,1536]{1,0:T(8,128)(2,1)S(1)}, u32[]{:S(2)}, u32[]{:S(2)}) collective-permute-start(bf16[128,1536]{1,0:T(8,128)(2,1)S(1)} %multiply_convert_fusion.2), channel_id=1, source_target_pairs={{1,0},{5,4},{9,8},{13,12},{17,16},{21,20},{25,24},{29,28}} | collective-permute-start | bytes 1179656 | tf_op jit(solution)/shard_map/ppermute | solution.py:176
  268.1 91.4 %collective-permute-start.76 = (bf16[2,2,1,2,1,24,1536]{6,5,4,3,2,1,0:T(8,128)(2,1)}, bf16[2,2,1,2,1,24,1536]{6,5,4,3,2,1,0:T(8,128)(2,1)}, u32[]{:S(2)}, u32[]{:S(2)}) collective-permute-start(bf16[2,2,1,2,1,24,1536]{6,5,4,3,2,1,0:T(8,128)(2,1)} %constant_dynamic-slice_fusion.2), channel_id=1, source_target_pairs={{0,4},{1,5},{2,6},{3,7},{4,0},{5,1},{6,2},{7,3},{8,12},{9,13},{10,... | collective-permute-start | bytes 1769480 | tf_op jit(solution)/shard_map/ppermute | solution.py:67
  272.0 88.8 %collective-permute-start.73 = (bf16[2,2,2,1,1,24,1536]{6,5,4,3,2,1,0:T(8,128)(2,1)}, bf16[2,2,2,1,1,24,1536]{6,5,4,3,2,1,0:T(8,128)(2,1)}, u32[]{:S(2)}, u32[]{:S(2)}) collective-permute-start(bf16[2,2,2,1,1,24,1536]{6,5,4,3,2,1,0:T(8,128)(2,1)} %constant_dynamic-slice_fusion.5), channel_id=1, source_target_pairs={{0,2},{1,3},{2,0},{3,1},{4,6},{5,7},{6,4},{7,5},{8,10},{9,11},{10,... | collective-permute-start | bytes 1769480 | tf_op jit(solution)/shard_map/ppermute | solution.py:67
  320.9 73.3 %collective-permute-start.67 = (bf16[2,2,2,2,1,24,1536]{6,5,4,3,2,1,0:T(8,128)(2,1)}, bf16[2,2,2,2,1,24,1536]{6,5,4,3,2,1,0:T(8,128)(2,1)}, u32[]{:S(2)}, u32[]{:S(2)}) collective-permute-start(bf16[2,2,2,2,1,24,1536]{6,5,4,3,2,1,0:T(8,128)(2,1)} %constant_dynamic-slice_fusion.10), channel_id=1, source_target_pairs={{0,1},{1,0},{2,3},{3,2},{4,5},{5,4},{6,7},{7,6},{8,9},{9,8},{10,11... | collective-permute-start | bytes 3538952 | tf_op jit(solution)/shard_map/ppermute | solution.py:67
  338.9 74.2 %collective-permute-start.64 = (bf16[2,2,2,2,1,24,1536]{6,5,4,3,2,1,0:T(8,128)(2,1)}, bf16[2,2,2,2,1,24,1536]{6,5,4,3,2,1,0:T(8,128)(2,1)}, u32[]{:S(2)}, u32[]{:S(2)}) collective-permute-start(bf16[2,2,2,2,1,24,1536]{6,5,4,3,2,1,0:T(8,128)(2,1)} %constant_dynamic-slice_fusion.13), channel_id=1, source_target_pairs={{0,1},{1,0},{2,3},{3,2},{4,5},{5,4},{6,7},{7,6},{8,9},{9,8},{10,11... | collective-permute-start | bytes 3538952 | tf_op jit(solution)/shard_map/ppermute | solution.py:67
  340.3 17.1 %collective-permute-start.44 = (bf16[128,1536]{1,0:T(8,128)(2,1)}, bf16[128,1536]{1,0:T(8,128)(2,1)}, u32[]{:S(2)}, u32[]{:S(2)}) collective-permute-start(bf16[128,1536]{1,0:T(8,128)(2,1)} %multiply_convert_fusion.1), channel_id=1, source_target_pairs={{3,2},{7,6},{11,10},{15,14},{19,18},{23,22},{27,26},{31,30}} | collective-permute-start | bytes 1179656 | tf_op jit(solution)/shard_map/ppermute | solution.py:176
  362.8 14.7 %collective-permute-start.77 = (bf16[2,2,1,1,1,24,1536]{6,5,4,3,2,1,0:T(8,128)(2,1)S(1)}, bf16[2,2,1,1,1,24,1536]{6,5,4,3,2,1,0:T(8,128)(2,1)S(1)}, u32[]{:S(2)}, u32[]{:S(2)}) collective-permute-start(bf16[2,2,1,1,1,24,1536]{6,5,4,3,2,1,0:T(8,128)(2,1)S(1)} %constant_dynamic-slice_fusion.1), channel_id=1, source_target_pairs={{0,2},{1,3},{2,0},{3,1},{4,6},{5,7},{6,4},{7,5},{8,10},{9,11},{10,... | collective-permute-start | bytes 884744 | tf_op jit(solution)/shard_map/ppermute | solution.py:67
  366.5 11.8 %collective-permute-start.74 = (bf16[2,2,1,1,1,24,1536]{6,5,4,3,2,1,0:T(8,128)(2,1)S(1)}, bf16[2,2,1,1,1,24,1536]{6,5,4,3,2,1,0:T(8,128)(2,1)S(1)}, u32[]{:S(2)}, u32[]{:S(2)}) collective-permute-start(bf16[2,2,1,1,1,24,1536]{6,5,4,3,2,1,0:T(8,128)(2,1)S(1)} %constant_dynamic-slice_fusion.4), channel_id=1, source_target_pairs={{0,4},{1,5},{2,6},{3,7},{4,0},{5,1},{6,2},{7,3},{8,12},{9,13},{10,... | collective-permute-start | bytes 884744 | tf_op jit(solution)/shard_map/ppermute | solution.py:67
  367.6 16.6 %collective-permute-start.57 = (bf16[2,2,2,1,1,24,896]{6,5,4,3,2,1,0:T(8,128)(2,1)S(1)}, bf16[2,2,2,1,1,24,896]{6,5,4,3,2,1,0:T(8,128)(2,1)S(1)}, u32[]{:S(2)}, u32[]{:S(2)}) collective-permute-start(bf16[2,2,2,1,1,24,896]{6,5,4,3,2,1,0:T(8,128)(2,1)S(1)} %constant_dynamic-slice_fusion.19), channel_id=1, source_target_pairs={{0,2},{1,3},{2,0},{3,1},{4,6},{5,7},{6,4},{7,5},{8,10},{9,11},{10,... | collective-permute-start | bytes 1032200 | tf_op jit(solution)/shard_map/ppermute | solution.py:67
  377.5 41.9 %collective-permute-start.60 = (bf16[2,2,1,2,1,24,1024]{6,5,4,3,2,1,0:T(8,128)(2,1)S(1)}, bf16[2,2,1,2,1,24,1024]{6,5,4,3,2,1,0:T(8,128)(2,1)S(1)}, u32[]{:S(2)}, u32[]{:S(2)}) collective-permute-start(bf16[2,2,1,2,1,24,1024]{6,5,4,3,2,1,0:T(8,128)(2,1)S(1)} %constant_dynamic-slice_fusion.16), channel_id=1, source_target_pairs={{0,4},{1,5},{2,6},{3,7},{4,0},{5,1},{6,2},{7,3},{8,12},{9,13},{10,... | collective-permute-start | bytes 1179656 | tf_op jit(solution)/shard_map/ppermute | solution.py:67
  378.3 21.2 %collective-permute-start.46 = (bf16[128,1536]{1,0:T(8,128)(2,1)S(1)}, bf16[128,1536]{1,0:T(8,128)(2,1)S(1)}, u32[]{:S(2)}, u32[]{:S(2)}) collective-permute-start(bf16[128,1536]{1,0:T(8,128)(2,1)S(1)} %multiply_convert_fusion), channel_id=1, source_target_pairs={{1,0},{5,4},{9,8},{13,12},{17,16},{21,20},{25,24},{29,28}} | collective-permute-start | bytes 1179656 | tf_op jit(solution)/shard_map/ppermute | solution.py:176
  384.2 8.4 %collective-permute-start.78 = (bf16[2,1,1,1,1,24,3072]{6,5,4,3,2,1,0:T(8,128)(2,1)S(1)}, bf16[2,1,1,1,1,24,3072]{6,5,4,3,2,1,0:T(8,128)(2,1)S(1)}, u32[]{:S(2)}, u32[]{:S(2)}) collective-permute-start(bf16[2,1,1,1,1,24,3072]{6,5,4,3,2,1,0:T(8,128)(2,1)S(1)} %fusion.12), channel_id=1, source_target_pairs={{0,8},{1,9},{2,10},{3,11},{4,12},{5,13},{6,14},{7,15},{8,0},{9,1},... | collective-permute-start | bytes 884744 | tf_op jit(solution)/shard_map/ppermute | solution.py:67
  392.6 40.4 %collective-permute-start.58 = (bf16[2,2,1,1,1,24,896]{6,5,4,3,2,1,0:T(8,128)(2,1)}, bf16[2,2,1,1,1,24,896]{6,5,4,3,2,1,0:T(8,128)(2,1)}, u32[]{:S(2)}, u32[]{:S(2)}) collective-permute-start(bf16[2,2,1,1,1,24,896]{6,5,4,3,2,1,0:T(8,128)(2,1)} %constant_dynamic-slice_fusion.18), channel_id=1, source_target_pairs={{0,4},{1,5},{2,6},{3,7},{4,0},{5,1},{6,2},{7,3},{8,12},{9,13},{10,... | collective-permute-start | bytes 516104 | tf_op jit(solution)/shard_map/ppermute | solution.py:67
  394.2 59.0 %collective-permute-start.79 = (bf16[1,1,1,1,1,24,3072]{6,5,4,3,2,1,0:T(8,128)(2,1)}, bf16[1,1,1,1,1,24,3072]{6,5,4,3,2,1,0:T(8,128)(2,1)}, u32[]{:S(2)}, u32[]{:S(2)}) collective-permute-start(bf16[1,1,1,1,1,24,3072]{6,5,4,3,2,1,0:T(8,128)(2,1)} %constant_dynamic-slice_fusion), channel_id=1, source_target_pairs={{0,16},{1,17},{2,18},{3,19},{4,20},{5,21},{6,22},{7,23},{8,24},{9,... | collective-permute-start | bytes 442376 | tf_op jit(solution)/shard_map/ppermute | solution.py:67
  399.5 68.2 %collective-permute-start.68 = (bf16[2,2,1,2,1,24,1536]{6,5,4,3,2,1,0:T(8,128)(2,1)}, bf16[2,2,1,2,1,24,1536]{6,5,4,3,2,1,0:T(8,128)(2,1)}, u32[]{:S(2)}, u32[]{:S(2)}) collective-permute-start(bf16[2,2,1,2,1,24,1536]{6,5,4,3,2,1,0:T(8,128)(2,1)} %constant_dynamic-slice_fusion.9), channel_id=1, source_target_pairs={{0,4},{1,5},{2,6},{3,7},{4,0},{5,1},{6,2},{7,3},{8,12},{9,13},{10,... | collective-permute-start | bytes 1769480 | tf_op jit(solution)/shard_map/ppermute | solution.py:67
  419.4 50.3 %collective-permute-start.65 = (bf16[2,2,2,1,1,24,1536]{6,5,4,3,2,1,0:T(8,128)(2,1)}, bf16[2,2,2,1,1,24,1536]{6,5,4,3,2,1,0:T(8,128)(2,1)}, u32[]{:S(2)}, u32[]{:S(2)}) collective-permute-start(bf16[2,2,2,1,1,24,1536]{6,5,4,3,2,1,0:T(8,128)(2,1)} %constant_dynamic-slice_fusion.12), channel_id=1, source_target_pairs={{0,2},{1,3},{2,0},{3,1},{4,6},{5,7},{6,4},{7,5},{8,10},{9,11},{10,... | collective-permute-start | bytes 1769480 | tf_op jit(solution)/shard_map/ppermute | solution.py:67
  433.1 18.8 %collective-permute-start.61 = (bf16[2,2,1,1,1,24,1024]{6,5,4,3,2,1,0:T(8,128)(2,1)}, bf16[2,2,1,1,1,24,1024]{6,5,4,3,2,1,0:T(8,128)(2,1)}, u32[]{:S(2)}, u32[]{:S(2)}) collective-permute-start(bf16[2,2,1,1,1,24,1024]{6,5,4,3,2,1,0:T(8,128)(2,1)} %constant_dynamic-slice_fusion.15), channel_id=1, source_target_pairs={{0,2},{1,3},{2,0},{3,1},{4,6},{5,7},{6,4},{7,5},{8,10},{9,11},{10,... | collective-permute-start | bytes 589832 | tf_op jit(solution)/shard_map/ppermute | solution.py:67
  450.6 21.9 %collective-permute-start.48 = (bf16[2,2,2,2,1,24,896]{6,5,4,3,2,1,0:T(8,128)(2,1)}, bf16[2,2,2,2,1,24,896]{6,5,4,3,2,1,0:T(8,128)(2,1)}, u32[]{:S(2)}, u32[]{:S(2)}) collective-permute-start(bf16[2,2,2,2,1,24,896]{6,5,4,3,2,1,0:T(8,128)(2,1)} %constant_dynamic-slice_fusion.27), channel_id=1, source_target_pairs={{0,1},{1,0},{2,3},{3,2},{4,5},{5,4},{6,7},{7,6},{8,9},{9,8},{10,11... | collective-permute-start | bytes 2064392 | tf_op jit(solution)/shard_map/ppermute | solution.py:67
  451.9 23.5 %collective-permute-start.51 = (bf16[2,2,2,2,1,24,1024]{6,5,4,3,2,1,0:T(8,128)(2,1)}, bf16[2,2,2,2,1,24,1024]{6,5,4,3,2,1,0:T(8,128)(2,1)S(1)}, u32[]{:S(2)}, u32[]{:S(2)}) collective-permute-start(bf16[2,2,2,2,1,24,1024]{6,5,4,3,2,1,0:T(8,128)(2,1)} %constant_dynamic-slice_fusion.24), channel_id=1, source_target_pairs={{0,1},{1,0},{2,3},{3,2},{4,5},{5,4},{6,7},{7,6},{8,9},{9,8},{10,11... | collective-permute-start | bytes 2359304 | tf_op jit(solution)/shard_map/ppermute | solution.py:67
  469.0 9.9 %collective-permute-start.69 = (bf16[2,2,1,1,1,24,1536]{6,5,4,3,2,1,0:T(8,128)(2,1)S(1)}, bf16[2,2,1,1,1,24,1536]{6,5,4,3,2,1,0:T(8,128)(2,1)S(1)}, u32[]{:S(2)}, u32[]{:S(2)}) collective-permute-start(bf16[2,2,1,1,1,24,1536]{6,5,4,3,2,1,0:T(8,128)(2,1)S(1)} %constant_dynamic-slice_fusion.8), channel_id=1, source_target_pairs={{0,2},{1,3},{2,0},{3,1},{4,6},{5,7},{6,4},{7,5},{8,10},{9,11},{10,... | collective-permute-start | bytes 884744 | tf_op jit(solution)/shard_map/ppermute | solution.py:67
  470.9 9.9 %collective-permute-start.66 = (bf16[2,2,1,1,1,24,1536]{6,5,4,3,2,1,0:T(8,128)(2,1)S(1)}, bf16[2,2,1,1,1,24,1536]{6,5,4,3,2,1,0:T(8,128)(2,1)S(1)}, u32[]{:S(2)}, u32[]{:S(2)}) collective-permute-start(bf16[2,2,1,1,1,24,1536]{6,5,4,3,2,1,0:T(8,128)(2,1)S(1)} %constant_dynamic-slice_fusion.11), channel_id=1, source_target_pairs={{0,4},{1,5},{2,6},{3,7},{4,0},{5,1},{6,2},{7,3},{8,12},{9,13},{10,... | collective-permute-start | bytes 884744 | tf_op jit(solution)/shard_map/ppermute | solution.py:67
  473.8 9.3 %collective-permute-start.49 = (bf16[2,2,2,1,1,24,896]{6,5,4,3,2,1,0:T(8,128)(2,1)S(1)}, bf16[2,2,2,1,1,24,896]{6,5,4,3,2,1,0:T(8,128)(2,1)S(1)}, u32[]{:S(2)}, u32[]{:S(2)}) collective-permute-start(bf16[2,2,2,1,1,24,896]{6,5,4,3,2,1,0:T(8,128)(2,1)S(1)} %constant_dynamic-slice_fusion.26), channel_id=1, source_target_pairs={{0,2},{1,3},{2,0},{3,1},{4,6},{5,7},{6,4},{7,5},{8,10},{9,11},{10,... | collective-permute-start | bytes 1032200 | tf_op jit(solution)/shard_map/ppermute | solution.py:67
  475.8 13.8 %collective-permute-start.52 = (bf16[2,2,1,2,1,24,1024]{6,5,4,3,2,1,0:T(8,128)(2,1)S(1)}, bf16[2,2,1,2,1,24,1024]{6,5,4,3,2,1,0:T(8,128)(2,1)S(1)}, u32[]{:S(2)}, u32[]{:S(2)}) collective-permute-start(bf16[2,2,1,2,1,24,1024]{6,5,4,3,2,1,0:T(8,128)(2,1)S(1)} %constant_dynamic-slice_fusion.23), channel_id=1, source_target_pairs={{0,4},{1,5},{2,6},{3,7},{4,0},{5,1},{6,2},{7,3},{8,12},{9,13},{10,... | collective-permute-start | bytes 1179656 | tf_op jit(solution)/shard_map/ppermute | solution.py:67
  481.0 8.4 %collective-permute-start.70 = (bf16[2,1,1,1,1,24,3072]{6,5,4,3,2,1,0:T(8,128)(2,1)S(1)}, bf16[2,1,1,1,1,24,3072]{6,5,4,3,2,1,0:T(8,128)(2,1)S(1)}, u32[]{:S(2)}, u32[]{:S(2)}) collective-permute-start(bf16[2,1,1,1,1,24,3072]{6,5,4,3,2,1,0:T(8,128)(2,1)S(1)} %fusion.14), channel_id=1, source_target_pairs={{0,8},{1,9},{2,10},{3,11},{4,12},{5,13},{6,14},{7,15},{8,0},{9,1},... | collective-permute-start | bytes 884744 | tf_op jit(solution)/shard_map/ppermute | solution.py:67
  483.3 7.8 %collective-permute-start.50 = (bf16[2,2,1,1,1,24,896]{6,5,4,3,2,1,0:T(8,128)(2,1)S(1)}, bf16[2,2,1,1,1,24,896]{6,5,4,3,2,1,0:T(8,128)(2,1)S(1)}, u32[]{:S(2)}, u32[]{:S(2)}) collective-permute-start(bf16[2,2,1,1,1,24,896]{6,5,4,3,2,1,0:T(8,128)(2,1)S(1)} %constant_dynamic-slice_fusion.25), channel_id=1, source_target_pairs={{0,4},{1,5},{2,6},{3,7},{4,0},{5,1},{6,2},{7,3},{8,12},{9,13},{10,... | collective-permute-start | bytes 516104 | tf_op jit(solution)/shard_map/ppermute | solution.py:67
  (152 other events, 1040.2 us)
